TPU v7x, 128 devices: a whole 4x4x4 slice. The times are simulated.
128 devices in a mesh: blk: 64 (over z, y_hi, x, core), space: 2 (over y_lo).
Axes of the slice: x: 4, y: 4 (y_hi: 2, y_lo: 2; y = y_hi * 2 + y_lo), z: 4, core: 2. Of those that a mesh axis runs over, the one named last changes fastest.
Arguments:
- distribution: bfloat16 [2, 1792, 32, 2048], P(None, 'blk', 'space'), may hold values from -6 to 6
- face_signs: int32 [1792, 32], P('blk', 'space'), may hold values from 0 to 1
- stream_speed: float32 [2048], replicated, may hold values from 0.5 to 2
- factors: bfloat16 [3, 2048, 2048], P(None, 'blk'), may hold values from -0.125 to 0.125
- pair_list: int32 [3, 2], replicated, may hold values from 0 to 1
- frequency: float32 [3], replicated, may hold values from 0.5 to 2
Outputs:
- advanced: bfloat16 [2, 1792, 32, 2048], P(None, 'blk', 'space')
- collision: bfloat16 [3, 1792, 32, 2048], P(None, 'blk', 'space')
Inputs may be any that keep to these rules, and one draw needn't show every extreme that they name: Pair p gives the collision term of species pair_list[p, 0] against species pair_list[p, 1]. `face_signs`: 1 where the flow at a cell's face toward higher x goes toward higher x, 0 where it goes toward lower x; the face after the grid's last cell is a wall and its entry is not read.
All inputs are finite; a program needn't handle non-finite values.
Results may differ from a plain program's by a relative error of at most 0.0064.
Values may be sent and summed in bfloat16 or wider, within the bound.
No kernel may reach another device: no remote copies, remote signals or barrier semaphores. Data moves between devices by JAX's collectives and lax.ppermute only.
A program may use at most 192 MiB of HBM per device.

v0:
```python
import functools
import jax
import jax.numpy as jnp
from jax import lax
from jax.experimental import pallas as pl
from jax.experimental.pallas import tpu as pltpu
from jax.sharding import PartitionSpec as P

courant = 0.3
AXES = ("blk", "space")
SIZES = (4, 4, 4, 2)


def flat_index(z, y, x, core):
    return (((z * 2 + y // 2) * 4 + x) * 2 + core) * 2 + y % 2


def pairs_of(move):
    pairs = []
    for z in range(4):
        for y in range(4):
            for x in range(4):
                for core in range(2):
                    target = [v % n for v, n in zip(move(z, y, x, core), SIZES)]
                    pairs.append((flat_index(z, y, x, core), flat_index(*target)))
    return pairs


def along(step, first):
    return pairs_of(
        lambda z, y, x, core: (z, y, x + step, core)
        if (core == 0) == first
        else (z + step, y, x, core)
    )


PARTNER = pairs_of(lambda z, y, x, core: (z, y, x, 1 - core))
CROSS = pairs_of(lambda z, y, x, core: (z, 3 - y, x, core))
SIDE = pairs_of(lambda z, y, x, core: (z, y ^ 1, x, core))
UP1, DOWN1, FAR1 = along(1, True), along(-1, True), along(2, True)
UP2, DOWN2 = along(1, False), along(-1, False)


SMEM = pl.BlockSpec(memory_space=pltpu.SMEM)
HBM = pl.BlockSpec(memory_space=pltpu.HBM)
VMEM = pl.BlockSpec(memory_space=pltpu.VMEM)
DMA = pltpu.SemaphoreType.DMA


def cost(flops, moved):
    return pl.CostEstimate(flops=flops, bytes_accessed=moved, transcendentals=0)


def stay(array):
    return pltpu.with_memory_space_constraint(array, pltpu.HBM)


def packet_kernel(where_ref, signs_hbm, cells_ref, out_ref, rows, signs_ref, sem, sign_sem):
    first_part = where_ref[0] == 0
    species, lines, cells, coeffs = cells_ref.shape
    start = pl.multiple_of(jnp.where(first_part, cells - 8, 0), 8)
    copy = pltpu.make_async_copy(cells_ref.at[:, :, pl.ds(start, 8), :], rows, sem)
    copy.start()
    sign_copy = pltpu.make_async_copy(signs_hbm, signs_ref, sign_sem)
    sign_copy.start()
    out_ref[species * lines] = jnp.zeros((2, coeffs), jnp.bfloat16)
    sign_copy.wait()
    last = signs_ref[cells - 1 : cells, :].astype(jnp.float32)
    last = jnp.concatenate([last, last], axis=0).astype(jnp.bfloat16)
    out_ref[species * lines, :, 0:lines] = last
    copy.wait()

    def one(l, carry):
        for s in range(species):
            eight = rows[s, l].astype(jnp.float32)
            edge = jnp.where(first_part, eight[6:8], eight[0:2])
            out_ref[s * lines + l] = edge.astype(jnp.bfloat16)
        return carry

    lax.fori_loop(0, lines, one, 0)


def packet_of(cells, signs, where):
    species, lines, _, coeffs = cells.shape
    return pl.pallas_call(
        packet_kernel,
        in_specs=[SMEM, HBM, HBM],
        out_specs=VMEM,
        out_shape=jax.ShapeDtypeStruct((species * lines + 1, 2, coeffs), jnp.bfloat16),
        scratch_shapes=[
            pltpu.VMEM((species, lines, 8, coeffs), jnp.bfloat16),
            pltpu.VMEM(signs.shape, jnp.int32),
            DMA,
            DMA,
        ],
        cost_estimate=cost(cells.size, cells.size),
        compiler_params=pltpu.CompilerParams(vmem_limit_bytes=8 << 20),
        name="packet",
    )(where, stay(signs), stay(cells))


CHUNKS = 4


def transport_kernel(where_ref, speed_ref, signs_ref, packet_ref, cells_hbm, out_ref, out_hbm, cells_ref, in_sem, out_sem):
    first_part = where_ref[0] == 0
    species, lines, cells, coeffs = cells_ref.shape
    chunk = lines // CHUNKS

    def arriving(c):
        at = pl.ds(c * chunk, chunk)
        return pltpu.make_async_copy(cells_hbm.at[:, at], cells_ref.at[:, at], in_sem.at[c])

    def leaving(c):
        at = pl.ds(c * chunk, chunk)
        return pltpu.make_async_copy(out_ref.at[:, at], out_hbm.at[:, at], out_sem.at[c])

    for c in range(CHUNKS):
        arriving(c).start()
    width = 512
    row = lax.broadcasted_iota(jnp.int32, (cells, width), 0)
    row1 = lax.broadcasted_iota(jnp.int32, (cells, lines), 0)
    lane = lax.broadcasted_iota(jnp.int32, (cells, lines), 1)
    signs = (2 * signs_ref[...] - 1).astype(jnp.float32)
    signs = jnp.where(jnp.logical_and(row1 == cells - 1, jnp.logical_not(first_part)), 0.0, signs)
    got = 2.0 * packet_ref[species * lines, 0:1, 0:lines].astype(jnp.float32) - 1.0
    got = jnp.where(first_part, 0.0, got)

    def one(l, carry):
        d_right = jnp.sum(jnp.where(lane == l, signs, 0.0), axis=1, keepdims=True)
        d_first = jnp.sum(jnp.where(lane[0:1] == l, got, 0.0), axis=1, keepdims=True)
        d_right = jnp.broadcast_to(d_right, (cells, width))
        d_first = jnp.broadcast_to(d_first, (1, width))
        for c in range(coeffs // width):
            at = slice(c * width, (c + 1) * width)
            speed = speed_ref[:, at]
            for s in range(species):
                f = cells_ref[s, l, :, at].astype(jnp.float32)
                halo = packet_ref[s * lines + l, :, at].astype(jnp.float32)
                h0, h1 = halo[0:1], halo[1:2]
                zero = jnp.zeros_like(h0)
                left2, left1 = jnp.where(first_part, zero, h0), jnp.where(first_part, zero, h1)
                right1, right2 = jnp.where(first_part, h0, zero), jnp.where(first_part, h1, zero)
                before = jnp.where(row == 0, left1, pltpu.roll(f, 1, 0))
                after = jnp.where(row == cells - 1, right1, pltpu.roll(f, cells - 1, 0))
                upper = f + 0.5 * (f - before)
                lower = f - 0.5 * (after - f)
                lower_last = right1 - 0.5 * (right2 - right1)
                lower_next = jnp.where(row == cells - 1, lower_last, pltpu.roll(lower, cells - 1, 0))
                flux = d_right * speed * jnp.where(d_right > 0, upper, lower_next)
                upper_first = left1 + 0.5 * (left1 - left2)
                flux_first = d_first * speed * jnp.where(d_first > 0, upper_first, lower[0:1])
                flux_before = jnp.where(row == 0, flux_first, pltpu.roll(flux, 1, 0))
                out_ref[s, l, :, at] = (f - courant * (flux - flux_before)).astype(jnp.bfloat16)
        return carry

    for c in range(CHUNKS):
        arriving(c).wait()
        lax.fori_loop(c * chunk, (c + 1) * chunk, one, 0)
        leaving(c).start()
    for c in range(CHUNKS):
        leaving(c).wait()


def transport(cells, packet, signs, speed, where):
    return pl.pallas_call(
        transport_kernel,
        in_specs=[SMEM, VMEM, VMEM, VMEM, HBM],
        out_specs=[VMEM, HBM],
        out_shape=[
            pltpu.VMEM(cells.shape, jnp.bfloat16),
            jax.ShapeDtypeStruct(cells.shape, jnp.bfloat16),
        ],
        scratch_shapes=[pltpu.VMEM(cells.shape, jnp.bfloat16), DMA((CHUNKS,)), DMA((CHUNKS,))],
        cost_estimate=cost(30 * cells.size, 4 * cells.size),
        compiler_params=pltpu.CompilerParams(vmem_limit_bytes=16 << 20),
        name="transport",
    )(where, speed, signs, packet, stay(cells))


def join_kernel(*refs):
    out_ref = refs[-1]
    for i, ref in enumerate(refs[:-1]):
        out_ref[i] = ref[0]


def join(parts):
    shape = (len(parts),) + parts[0].shape[1:]
    return pl.pallas_call(
        join_kernel,
        in_specs=[VMEM] * len(parts),
        out_specs=VMEM,
        out_shape=pltpu.VMEM(shape, parts[0].dtype),
        cost_estimate=cost(parts[0].size, 16 * parts[0].size),
        compiler_params=pltpu.CompilerParams(vmem_limit_bytes=8 << 20),
        name="join",
    )(*parts)


def collide_kernel(count, first, last, freq_ref, pair_ref, adv_ref, *refs):
    groups, refs = refs[:count], refs[count:]
    acc_ref, refs = (None, refs) if first else (refs[0], refs[1:])
    out_ref = refs[0]
    species, rows, coeffs = adv_ref.shape
    pair_count = out_ref.shape[0]
    block = rows // 2
    nt = (((1,), (1,)), ((), ()))

    def leaving(i, p):
        staged, out_sem = refs[1:]
        at = pl.ds(pl.multiple_of(i * block, block), block)
        return pltpu.make_async_copy(staged.at[p, at, :], out_ref.at[p, at, :], out_sem.at[i, p])

    def part(g, which):
        return groups[g][:, which].reshape(-1, coeffs)

    for t in range(count // 2):
        mine, other = 2 * t, 2 * t + 1

        def step(i, carry, t=t, mine=mine, other=other):
            at = pl.ds(pl.multiple_of(i * block, block), block)
            a = adv_ref[:, at, :].reshape(species * block, coeffs)
            lefts, rights = [], []
            for g in (mine, other):
                w = jnp.concatenate([part(g, 0), part(g, 1)], axis=0)
                both = lax.dot_general(a, w, nt, preferred_element_type=jnp.float32)
                n = both.shape[1] // 2
                lefts.append(both[:, :n])
                rights.append(both[:, n:])
            left = jnp.concatenate(lefts, axis=1)
            right = jnp.concatenate(rights, axis=1)
            down = jnp.concatenate([part(mine, 2), part(other, 2)], axis=0)
            for p in range(pair_count):
                lp = jnp.where(pair_ref[0, p] == 1, left[block:], left[:block])
                rp = jnp.where(pair_ref[1, p] == 1, right[block:], right[:block])
                product = (freq_ref[p] * lp * rp).astype(jnp.bfloat16)
                term = jnp.dot(product, down, preferred_element_type=jnp.float32)
                if last:
                    refs[1][p, at, :] = (acc_ref[p, at, :] + term).astype(jnp.bfloat16)
                    leaving(i, p).start()
                    continue
                if t > 0:
                    term = out_ref[p, at, :] + term
                elif not first:
                    term = acc_ref[p, at, :] + term
                out_ref[p, at, :] = term
            return carry

        lax.fori_loop(0, 2, step, 0)
    if last:
        for i in range(2):
            for p in range(pair_count):
                leaving(i, p).wait()


def collide(adv, frequency, pairs, groups, acc, last=False):
    species, rows, coeffs = adv.shape
    pair_count = pairs.shape[1]
    ranks = sum(a.shape[0] * a.shape[2] for a in groups)
    assert not last or len(groups) == 2
    shape = (pair_count, rows, coeffs)
    operands = [frequency, pairs, adv] + groups + ([] if acc is None else [acc])
    scratch = []
    if last:
        scratch = [pltpu.VMEM(shape, jnp.bfloat16), DMA((2, pair_count))]
    return pl.pallas_call(
        functools.partial(collide_kernel, len(groups), acc is None, last),
        in_specs=[SMEM, SMEM] + [VMEM] * (len(operands) - 2),
        out_specs=HBM if last else VMEM,
        out_shape=jax.ShapeDtypeStruct(shape, jnp.bfloat16) if last else pltpu.VMEM(shape, jnp.float32),
        scratch_shapes=scratch,
        input_output_aliases={} if acc is None or last else {len(operands) - 1: 0},
        cost_estimate=cost(
            2 * ranks * coeffs * rows * (2 * species + pair_count),
            2 * (adv.size + 3 * ranks * coeffs),
        ),
        compiler_params=pltpu.CompilerParams(vmem_limit_bytes=20 << 20),
        name="collide",
    )(*operands)


def send(array, pairs):
    return lax.ppermute(array, AXES, pairs)


def phase(mine):
    return [mine, send(mine, UP1), send(mine, DOWN1), send(mine, FAR1)]


def after(array, *others):
    return lax.optimization_barrier((array,) + others)[0]


def local(distribution, face_signs, stream_speed, factors, pair_list, frequency):
    species, lines, cells, coeffs = distribution.shape
    here = lax.axis_index("space").astype(jnp.int32)[None]
    mine = factors[None]
    signs, pairs = face_signs.T, pair_list.T

    cross = send(mine, CROSS)
    parts_o = phase(mine)
    packet = packet_of(distribution, signs, here)
    got = send(packet, SIDE)
    parts_o[0] = after(mine, packet)
    group_o = join(parts_o)
    up_o, down_o = send(group_o, UP2), send(group_o, DOWN2)
    swap_o = send(group_o, PARTNER)

    parts_c = phase(after(cross, group_o))
    adv_near, advanced = transport(distribution, got, signs, stream_speed[None], here)
    parts_c[0] = after(parts_c[0], adv_near)
    group_c = join(parts_c)
    up_c, down_c = send(group_c, UP2), send(group_c, DOWN2)
    swap_c = send(group_c, PARTNER)

    adv = adv_near.reshape(species, lines * cells, coeffs)

    def step(groups, acc, last=False):
        return collide(adv, frequency, pairs, groups, acc, last)

    acc = step([after(group_o, group_c), swap_o], None)
    acc = step([group_c, swap_c], acc)
    up_o, down_o, _ = lax.optimization_barrier((up_o, down_o, acc))
    far_o = send(up_o, UP2)
    acc = step([up_o, send(up_o, PARTNER), down_o, send(down_o, PARTNER)], acc)
    down_c = after(down_c, acc)
    far_c = send(down_c, DOWN2)
    acc = step([down_c, send(down_c, PARTNER)], acc)
    far_o = after(far_o, acc)
    acc = step([far_o, send(far_o, PARTNER)], acc)
    up_c = after(up_c, acc)
    acc = step([up_c, send(up_c, PARTNER)], acc)
    out = step([far_c, send(far_c, PARTNER)], acc, last=True)
    collision = out.reshape(pair_list.shape[0], lines, cells, coeffs)
    return (advanced, collision)


def solution(mesh):
    return jax.shard_map(
        local,
        mesh=mesh,
        in_specs=(
            P(None, "blk", "space", None),
            P("blk", "space"),
            P(),
            P(None, "blk", None),
            P(),
            P(),
        ),
        out_specs=(P(None, "blk", "space", None), P(None, "blk", "space", None)),
        check_vma=False,
    )
```

profile of v0, /device:TPU:1, one launch (start us, length us, event | category | flops | bytes accessed | tf_op | source)
XLA Modules:
  0.0 136.1 jit_solution(3307436839587319305)
XLA Ops:
  0.6 2.5 %collective-permute-start.2 = (bf16[1,3,32,2048]{3,2,1,0:T(8,128)(2,1)}, bf16[1,3,32,2048]{3,2,1,0:T(8,128)(2,1)S(1)}, u32[]{:S(2)}, u32[]{:S(2)}) collective-permute-start(bf16[1,3,32,2048]{3,2,1,0:T(8,128)(2,1)} %bitcast.14), channel_id=1, source_target_pairs={{0,4},{2,34},{4,8},{6,38},{8,12},{10,42},{12,0},{14,46},{1,5},{3,3... | collective-permute-start | bytes 1179656 | tf_op jit(solution)/shard_map/ppermute | solution.py:283
  3.2 2.2 %collective-permute-start.3 = (bf16[1,3,32,2048]{3,2,1,0:T(8,128)(2,1)}, bf16[1,3,32,2048]{3,2,1,0:T(8,128)(2,1)S(1)}, u32[]{:S(2)}, u32[]{:S(2)}) collective-permute-start(bf16[1,3,32,2048]{3,2,1,0:T(8,128)(2,1)} %bitcast.15), channel_id=1, source_target_pairs={{0,12},{2,98},{4,0},{6,102},{8,4},{10,106},{12,8},{14,110},{1,13},... | collective-permute-start | bytes 1179656 | tf_op jit(solution)/shard_map/ppermute | solution.py:283
  5.4 1.2 collective-permute-start.4
  6.6 2.7 %collective-permute-start.1 = (bf16[1,3,32,2048]{3,2,1,0:T(8,128)(2,1)}, bf16[1,3,32,2048]{3,2,1,0:T(8,128)(2,1)S(1)}, u32[]{:S(2)}, u32[]{:S(2)}) collective-permute-start(bf16[1,3,32,2048]{3,2,1,0:T(8,128)(2,1)} %bitcast.17), channel_id=1, source_target_pairs={{0,17},{2,19},{4,21},{6,23},{8,25},{10,27},{12,29},{14,31},{1,16},... | collective-permute-start | bytes 1179656 | tf_op jit(solution)/shard_map/ppermute | solution.py:283
  9.3 2.3 %packet.1 = bf16[57,2,2048]{2,1,0:T(2,128)(2,1)S(1)} custom-call(s32[1]{0:T(128)} %bitcast.where_ref, s32[16,28]{1,0:T(8,128)} %bitcast.26, bf16[2,28,16,2048]{3,2,1,0:T(8,128)(2,1)} %cells_hbm.1), custom_call_target="tpu_custom_call" | custom-call | flops 1835008 | bytes 1835008 | tf_op jit(solution)/shard_map/packet/pallas_call | solution.py:85
  11.6 0.0 copy-start.2
  11.6 0.0 copy-start.4
  11.6 0.1 collective-permute-start
  11.7 2.9 %collective-permute-done.3.refs_2_ = bf16[1,3,32,2048]{3,2,1,0:T(8,128)(2,1)S(1)} collective-permute-done((bf16[1,3,32,2048]{3,2,1,0:T(8,128)(2,1)}, bf16[1,3,32,2048]{3,2,1,0:T(8,128)(2,1)S(1)}, u32[]{:S(2)}, u32[]{:S(2)}) %collective-permute-start.3) | collective-permute-done | bytes 393248 | tf_op jit(solution)/shard_map/ppermute | solution.py:283
  14.6 1.6 %collective-permute-done.4.refs_3_ = bf16[1,3,32,2048]{3,2,1,0:T(8,128)(2,1)S(1)} collective-permute-done((bf16[1,3,32,2048]{3,2,1,0:T(8,128)(2,1)}, bf16[1,3,32,2048]{3,2,1,0:T(8,128)(2,1)S(1)}, u32[]{:S(2)}, u32[]{:S(2)}) %collective-permute-start.4) | collective-permute-done | bytes 393248 | tf_op jit(solution)/shard_map/ppermute | solution.py:283
  16.2 0.1 join.2.refs_0_
  16.3 1.9 %collective-permute-done.1.refs_0_ = bf16[1,3,32,2048]{3,2,1,0:T(8,128)(2,1)S(1)} collective-permute-done((bf16[1,3,32,2048]{3,2,1,0:T(8,128)(2,1)}, bf16[1,3,32,2048]{3,2,1,0:T(8,128)(2,1)S(1)}, u32[]{:S(2)}, u32[]{:S(2)}) %collective-permute-start.1) | collective-permute-done | bytes 393248 | tf_op jit(solution)/shard_map/ppermute | solution.py:283
  18.2 0.0 collective-permute-start.5
  18.2 2.7 %collective-permute-start.6 = (bf16[1,3,32,2048]{3,2,1,0:T(8,128)(2,1)S(1)}, bf16[1,3,32,2048]{3,2,1,0:T(8,128)(2,1)S(1)}, u32[]{:S(2)}, u32[]{:S(2)}) collective-permute-start(bf16[1,3,32,2048]{3,2,1,0:T(8,128)(2,1)S(1)} %collective-permute-done.1.refs_0_), channel_id=1, source_target_pairs={{0,12},{2,98},{4,0},{6,102},{8,4},{10,106},{12,8},{14,110},{1,13},... | collective-permute-start | bytes 1179656 | tf_op jit(solution)/shard_map/ppermute | solution.py:283
  20.9 3.0 %collective-permute-start.12 = (bf16[4,3,32,2048]{3,2,1,0:T(8,128)(2,1)S(1)}, bf16[4,3,32,2048]{3,2,1,0:T(8,128)(2,1)S(1)}, u32[]{:S(2)}, u32[]{:S(2)}) collective-permute-start(bf16[4,3,32,2048]{3,2,1,0:T(8,128)(2,1)S(1)} %join.2.refs_0_), channel_id=1, source_target_pairs={{0,2},{2,0},{4,6},{6,4},{8,10},{10,8},{12,14},{14,12},{1,3},{3,1},... | collective-permute-start | bytes 4718600 | tf_op jit(solution)/shard_map/ppermute | solution.py:283
  23.9 9.5 %transport.1 = (bf16[2,28,16,2048]{3,2,1,0:T(8,128)(2,1)S(1)}, bf16[2,28,16,2048]{3,2,1,0:T(8,128)(2,1)}) custom-call(s32[1]{0:T(128)} %bitcast.where_ref, f32[1,2048]{1,0:T(1,128)S(1)} %bitcast.28, s32[16,28]{1,0:T(8,128)S(1)} %bitcast.27, bf16[57,2,2048]{2,1,0:T(2,128)(2,1)S(1)} %collective-permute-done.packet_ref, bf16[2,28,16,2048]{3,2,1,0:T(8,128)(2,1)} %cells_hbm.1), custom_call_target="tpu_custom_call" | custom-call | flops 55050240 | bytes 7340032 | tf_op jit(solution)/shard_map/transport/pallas_call | solution.py:166
  33.4 0.0 copy-start.1
  33.4 0.0 copy-start.3
  33.5 0.1 join.3.refs_0_
  33.6 1.0 collective-permute-start.11
  34.6 2.0 %collective-permute-start.10 = (bf16[4,3,32,2048]{3,2,1,0:T(8,128)(2,1)S(1)}, bf16[4,3,32,2048]{3,2,1,0:T(8,128)(2,1)S(1)}, u32[]{:S(2)}, u32[]{:S(2)}) collective-permute-start(bf16[4,3,32,2048]{3,2,1,0:T(8,128)(2,1)S(1)} %join.2.refs_0_), channel_id=1, source_target_pairs={{0,96},{2,14},{4,100},{6,2},{8,104},{10,6},{12,108},{14,10},{1,97}... | collective-permute-start | bytes 4718600 | tf_op jit(solution)/shard_map/ppermute | solution.py:283
  36.6 4.5 %collide.7.refs_2_ = f32[3,448,2048]{2,1,0:T(8,128)S(1)} custom-call(f32[3]{0:T(128)S(1)} %copy-done.3, s32[2,3]{1,0:T(2,128)S(1)} %bitcast.19, bf16[2,448,2048]{2,1,0:T(8,128)(2,1)S(1)} %bitcast.7, bf16[4,3,32,2048]{3,2,1,0:T(8,128)(2,1)S(1)} %join.2.refs_0_, bf16[4,3,32,2048]{3,2,1,0:T(8,128)(2,1)S(1)} %collective-permute-done.12.refs_1_), custom_call_target="tpu_custom_call" | custom-call | flops 3288334336 | bytes 6815744 | tf_op jit(solution)/shard_map/collide/pallas_call | solution.py:266
  41.2 5.5 %collide.8.refs_4_ = f32[3,448,2048]{2,1,0:T(8,128)S(1)} custom-call(f32[3]{0:T(128)S(1)} %copy-done.3, s32[2,3]{1,0:T(2,128)S(1)} %bitcast.20, bf16[2,448,2048]{2,1,0:T(8,128)(2,1)S(1)} %bitcast.8, bf16[4,3,32,2048]{3,2,1,0:T(8,128)(2,1)S(1)} %join.3.refs_0_, ...), custom_call_target="tpu_custom_call", output_to_operand_aliasing={{}: (5, {})} | custom-call | flops 3288334336 | bytes 6815744 | tf_op jit(solution)/shard_map/collide/pallas_call | solution.py:266
  46.8 7.4 %collective-permute-done.10.refs_2_ = bf16[4,3,32,2048]{3,2,1,0:T(8,128)(2,1)S(1)} collective-permute-done((bf16[4,3,32,2048]{3,2,1,0:T(8,128)(2,1)S(1)}, bf16[4,3,32,2048]{3,2,1,0:T(8,128)(2,1)S(1)}, u32[]{:S(2)}, u32[]{:S(2)}) %collective-permute-start.10) | collective-permute-done | bytes 1572896 | tf_op jit(solution)/shard_map/ppermute | solution.py:283
  54.1 3.0 %collective-permute-done.9.refs_0_ = bf16[4,3,32,2048]{3,2,1,0:T(8,128)(2,1)S(1)} collective-permute-done((bf16[4,3,32,2048]{3,2,1,0:T(8,128)(2,1)S(1)}, bf16[4,3,32,2048]{3,2,1,0:T(8,128)(2,1)S(1)}, u32[]{:S(2)}, u32[]{:S(2)}) %collective-permute-start.9) | collective-permute-done | bytes 1572896 | tf_op jit(solution)/shard_map/ppermute | solution.py:283
  57.1 0.4 collective-permute-start.13
  57.5 0.1 collective-permute-start.14
  57.6 2.0 %collective-permute-start.8 = (bf16[4,3,32,2048]{3,2,1,0:T(8,128)(2,1)S(1)}, bf16[4,3,32,2048]{3,2,1,0:T(8,128)(2,1)S(1)}, u32[]{:S(2)}, u32[]{:S(2)}) collective-permute-start(bf16[4,3,32,2048]{3,2,1,0:T(8,128)(2,1)S(1)} %join.3.refs_0_), channel_id=1, source_target_pairs={{0,96},{2,14},{4,100},{6,2},{8,104},{10,6},{12,108},{14,10},{1,97}... | collective-permute-start | bytes 4718600 | tf_op jit(solution)/shard_map/ppermute | solution.py:283
  59.7 0.9 collective-permute-done.13.refs_1_
  60.5 2.2 %collective-permute-done.14.refs_3_ = bf16[4,3,32,2048]{3,2,1,0:T(8,128)(2,1)S(1)} collective-permute-done((bf16[4,3,32,2048]{3,2,1,0:T(8,128)(2,1)S(1)}, bf16[4,3,32,2048]{3,2,1,0:T(8,128)(2,1)S(1)}, u32[]{:S(2)}, u32[]{:S(2)}) %collective-permute-start.14) | collective-permute-done | bytes 1572896 | tf_op jit(solution)/shard_map/ppermute | solution.py:283
  62.8 9.6 %collide.9.refs_2_ = f32[3,448,2048]{2,1,0:T(8,128)S(1)} custom-call(f32[3]{0:T(128)S(1)} %copy-done.3, s32[2,3]{1,0:T(2,128)S(1)} %bitcast.21, bf16[2,448,2048]{2,1,0:T(8,128)(2,1)S(1)} %bitcast.9, bf16[4,3,32,2048]{3,2,1,0:T(8,128)(2,1)S(1)} %collective-permute-done.9.refs_0_, ...), custom_call_target="tpu_custom_call", output_to_operand_aliasing={{}: (7, {})} | custom-call | flops 6576668672 | bytes 9961472 | tf_op jit(solution)/shard_map/collide/pallas_call | solution.py:266
  72.3 4.8 %collective-permute-done.8.refs_0_ = bf16[4,3,32,2048]{3,2,1,0:T(8,128)(2,1)S(1)} collective-permute-done((bf16[4,3,32,2048]{3,2,1,0:T(8,128)(2,1)S(1)}, bf16[4,3,32,2048]{3,2,1,0:T(8,128)(2,1)S(1)}, u32[]{:S(2)}, u32[]{:S(2)}) %collective-permute-start.8) | collective-permute-done | bytes 1572896 | tf_op jit(solution)/shard_map/ppermute | solution.py:283
  77.2 1.2 collective-permute-start.19
  78.4 0.9 collective-permute-start.18
  79.3 2.1 %collective-permute-done.19.refs_1_ = bf16[4,3,32,2048]{3,2,1,0:T(8,128)(2,1)S(1)} collective-permute-done((bf16[4,3,32,2048]{3,2,1,0:T(8,128)(2,1)S(1)}, bf16[4,3,32,2048]{3,2,1,0:T(8,128)(2,1)S(1)}, u32[]{:S(2)}, u32[]{:S(2)}) %collective-permute-start.19) | collective-permute-done | bytes 1572896 | tf_op jit(solution)/shard_map/ppermute | solution.py:283
  81.4 5.5 %collide.10.refs_2_ = f32[3,448,2048]{2,1,0:T(8,128)S(1)} custom-call(f32[3]{0:T(128)S(1)} %copy-done.3, s32[2,3]{1,0:T(2,128)S(1)} %bitcast.22, bf16[2,448,2048]{2,1,0:T(8,128)(2,1)S(1)} %bitcast.10, bf16[4,3,32,2048]{3,2,1,0:T(8,128)(2,1)S(1)} %collective-permute-done.8.refs_0_, ...), custom_call_target="tpu_custom_call", output_to_operand_aliasing={{}: (5, {})} | custom-call | flops 3288334336 | bytes 6815744 | tf_op jit(solution)/shard_map/collide/pallas_call | solution.py:266
  86.9 12.2 %collective-permute-done.18.refs_0_ = bf16[4,3,32,2048]{3,2,1,0:T(8,128)(2,1)S(1)} collective-permute-done((bf16[4,3,32,2048]{3,2,1,0:T(8,128)(2,1)S(1)}, bf16[4,3,32,2048]{3,2,1,0:T(8,128)(2,1)S(1)}, u32[]{:S(2)}, u32[]{:S(2)}) %collective-permute-start.18) | collective-permute-done | bytes 1572896 | tf_op jit(solution)/shard_map/ppermute | solution.py:283
  99.2 0.9 collective-permute-start.20
  100.0 0.9 collective-permute-start.17
  101.0 1.8 %collective-permute-start.15 = (bf16[4,3,32,2048]{3,2,1,0:T(8,128)(2,1)S(1)}, bf16[4,3,32,2048]{3,2,1,0:T(8,128)(2,1)S(1)}, u32[]{:S(2)}, u32[]{:S(2)}) collective-permute-start(bf16[4,3,32,2048]{3,2,1,0:T(8,128)(2,1)S(1)} %collective-permute-done.8.refs_0_), channel_id=1, source_target_pairs={{0,96},{2,14},{4,100},{6,2},{8,104},{10,6},{12,108},{14,10},{1,97}... | collective-permute-start | bytes 4718600 | tf_op jit(solution)/shard_map/ppermute | solution.py:283
  102.7 0.4 collective-permute-done.20.refs_1_
  103.1 5.5 %collide.11.refs_2_ = f32[3,448,2048]{2,1,0:T(8,128)S(1)} custom-call(f32[3]{0:T(128)S(1)} %copy-done.3, s32[2,3]{1,0:T(2,128)S(1)} %bitcast.23, bf16[2,448,2048]{2,1,0:T(8,128)(2,1)S(1)} %bitcast.11, bf16[4,3,32,2048]{3,2,1,0:T(8,128)(2,1)S(1)} %collective-permute-done.18.refs_0_, ...), custom_call_target="tpu_custom_call", output_to_operand_aliasing={{}: (5, {})} | custom-call | flops 3288334336 | bytes 6815744 | tf_op jit(solution)/shard_map/collide/pallas_call | solution.py:266
  108.6 12.2 %collective-permute-done.17.refs_0_ = bf16[4,3,32,2048]{3,2,1,0:T(8,128)(2,1)S(1)} collective-permute-done((bf16[4,3,32,2048]{3,2,1,0:T(8,128)(2,1)S(1)}, bf16[4,3,32,2048]{3,2,1,0:T(8,128)(2,1)S(1)}, u32[]{:S(2)}, u32[]{:S(2)}) %collective-permute-start.17) | collective-permute-done | bytes 1572896 | tf_op jit(solution)/shard_map/ppermute | solution.py:283
  120.8 0.9 collective-permute-start.21
  121.7 0.0 collective-permute-start.16
  121.7 3.0 %collective-permute-done.21.refs_1_ = bf16[4,3,32,2048]{3,2,1,0:T(8,128)(2,1)S(1)} collective-permute-done((bf16[4,3,32,2048]{3,2,1,0:T(8,128)(2,1)S(1)}, bf16[4,3,32,2048]{3,2,1,0:T(8,128)(2,1)S(1)}, u32[]{:S(2)}, u32[]{:S(2)}) %collective-permute-start.21) | collective-permute-done | bytes 1572896 | tf_op jit(solution)/shard_map/ppermute | solution.py:283
  124.7 5.5 %collide.12.refs_2_ = f32[3,448,2048]{2,1,0:T(8,128)S(1)} custom-call(f32[3]{0:T(128)S(1)} %copy-done.3, s32[2,3]{1,0:T(2,128)S(1)} %bitcast.24, bf16[2,448,2048]{2,1,0:T(8,128)(2,1)S(1)} %bitcast.12, bf16[4,3,32,2048]{3,2,1,0:T(8,128)(2,1)S(1)} %collective-permute-done.17.refs_0_, ...), custom_call_target="tpu_custom_call", output_to_operand_aliasing={{}: (5, {})} | custom-call | flops 3288334336 | bytes 6815744 | tf_op jit(solution)/shard_map/collide/pallas_call | solution.py:266
  130.3 5.7 %collide.13 = bf16[3,448,2048]{2,1,0:T(8,128)(2,1)} custom-call(f32[3]{0:T(128)S(1)} %copy-done.3, s32[2,3]{1,0:T(2,128)S(1)} %bitcast.25, bf16[2,448,2048]{2,1,0:T(8,128)(2,1)S(1)} %bitcast.13, bf16[4,3,32,2048]{3,2,1,0:T(8,128)(2,1)S(1)} %collective-permute-done.15.refs_0_, bf16[4,3,32,2048]{3,2,1,0:T(8,128)(2,1)S(1)} %collective-permute-done.16.refs_1_, ...), custom_call_target="tpu_custom_call" | custom-call | flops 3288334336 | bytes 6815744 | tf_op jit(solution)/shard_map/collide/pallas_call | solution.py:266
  (17 shorter events, 0.0 us)
Async XLA Ops:
  0.6 11.1 %collective-permute-start.2 = (bf16[1,3,32,2048]{3,2,1,0:T(8,128)(2,1)}, bf16[1,3,32,2048]{3,2,1,0:T(8,128)(2,1)S(1)}, u32[]{:S(2)}, u32[]{:S(2)}) collective-permute-start(bf16[1,3,32,2048]{3,2,1,0:T(8,128)(2,1)} %bitcast.14), channel_id=1, source_target_pairs={{0,4},{2,34},{4,8},{6,38},{8,12},{10,42},{12,0},{14,46},{1,5},{3,3... | collective-permute-start | bytes 1179656 | tf_op jit(solution)/shard_map/ppermute | solution.py:283
  3.2 11.5 %collective-permute-start.3 = (bf16[1,3,32,2048]{3,2,1,0:T(8,128)(2,1)}, bf16[1,3,32,2048]{3,2,1,0:T(8,128)(2,1)S(1)}, u32[]{:S(2)}, u32[]{:S(2)}) collective-permute-start(bf16[1,3,32,2048]{3,2,1,0:T(8,128)(2,1)} %bitcast.15), channel_id=1, source_target_pairs={{0,12},{2,98},{4,0},{6,102},{8,4},{10,106},{12,8},{14,110},{1,13},... | collective-permute-start | bytes 1179656 | tf_op jit(solution)/shard_map/ppermute | solution.py:283
  5.4 10.8 %collective-permute-start.4 = (bf16[1,3,32,2048]{3,2,1,0:T(8,128)(2,1)}, bf16[1,3,32,2048]{3,2,1,0:T(8,128)(2,1)S(1)}, u32[]{:S(2)}, u32[]{:S(2)}) collective-permute-start(bf16[1,3,32,2048]{3,2,1,0:T(8,128)(2,1)} %bitcast.16), channel_id=1, source_target_pairs={{0,8},{2,66},{4,12},{6,70},{8,0},{10,74},{12,4},{14,78},{1,9},{3,6... | collective-permute-start | bytes 1179656 | tf_op jit(solution)/shard_map/ppermute | solution.py:283
  6.6 11.6 %collective-permute-start.1 = (bf16[1,3,32,2048]{3,2,1,0:T(8,128)(2,1)}, bf16[1,3,32,2048]{3,2,1,0:T(8,128)(2,1)S(1)}, u32[]{:S(2)}, u32[]{:S(2)}) collective-permute-start(bf16[1,3,32,2048]{3,2,1,0:T(8,128)(2,1)} %bitcast.17), channel_id=1, source_target_pairs={{0,17},{2,19},{4,21},{6,23},{8,25},{10,27},{12,29},{14,31},{1,16},... | collective-permute-start | bytes 1179656 | tf_op jit(solution)/shard_map/ppermute | solution.py:283
  9.3 6.9 %copy-start = (bf16[3,32,2048]{2,1,0:T(8,128)(2,1)S(1)}, bf16[3,32,2048]{2,1,0:T(8,128)(2,1)}, u32[]{:S(2)}) copy-start(bf16[3,32,2048]{2,1,0:T(8,128)(2,1)} %param.9) | copy-start | bytes 1179652
  11.6 12.3 %copy-start.2 = (s32[28,16]{0,1:T(8,128)S(1)}, s32[28,16]{0,1:T(8,128)}, u32[]{:S(2)}) copy-start(s32[28,16]{0,1:T(8,128)} %param.7) | copy-start | bytes 5380
  11.6 12.3 %copy-start.4 = (f32[2048]{0:T(1024)S(1)}, f32[2048]{0:T(1024)}, u32[]{:S(2)}) copy-start(f32[2048]{0:T(1024)} %param.8) | copy-start | bytes 24580
  11.6 12.3 %collective-permute-start = (bf16[57,2,2048]{2,1,0:T(2,128)(2,1)S(1)}, bf16[57,2,2048]{2,1,0:T(2,128)(2,1)S(1)}, u32[]{:S(2)}, u32[]{:S(2)}) collective-permute-start(bf16[57,2,2048]{2,1,0:T(2,128)(2,1)S(1)} %packet.1), channel_id=1, source_target_pairs={{0,1},{2,3},{4,5},{6,7},{8,9},{10,11},{12,13},{14,15},{1,0},{3,2},... | collective-permute-start | bytes 1400840 | tf_op jit(solution)/shard_map/ppermute | solution.py:283
  18.2 15.2 %collective-permute-start.5 = (bf16[1,3,32,2048]{3,2,1,0:T(8,128)(2,1)S(1)}, bf16[1,3,32,2048]{3,2,1,0:T(8,128)(2,1)S(1)}, u32[]{:S(2)}, u32[]{:S(2)}) collective-permute-start(bf16[1,3,32,2048]{3,2,1,0:T(8,128)(2,1)S(1)} %collective-permute-done.1.refs_0_), channel_id=1, source_target_pairs={{0,4},{2,34},{4,8},{6,38},{8,12},{10,42},{12,0},{14,46},{1,5},{3,3... | collective-permute-start | bytes 1179656 | tf_op jit(solution)/shard_map/ppermute | solution.py:283
  18.2 15.2 %collective-permute-start.6 = (bf16[1,3,32,2048]{3,2,1,0:T(8,128)(2,1)S(1)}, bf16[1,3,32,2048]{3,2,1,0:T(8,128)(2,1)S(1)}, u32[]{:S(2)}, u32[]{:S(2)}) collective-permute-start(bf16[1,3,32,2048]{3,2,1,0:T(8,128)(2,1)S(1)} %collective-permute-done.1.refs_0_), channel_id=1, source_target_pairs={{0,12},{2,98},{4,0},{6,102},{8,4},{10,106},{12,8},{14,110},{1,13},... | collective-permute-start | bytes 1179656 | tf_op jit(solution)/shard_map/ppermute | solution.py:283
  20.9 12.6 %collective-permute-start.7 = (bf16[1,3,32,2048]{3,2,1,0:T(8,128)(2,1)S(1)}, bf16[1,3,32,2048]{3,2,1,0:T(8,128)(2,1)S(1)}, u32[]{:S(2)}, u32[]{:S(2)}) collective-permute-start(bf16[1,3,32,2048]{3,2,1,0:T(8,128)(2,1)S(1)} %collective-permute-done.1.refs_0_), channel_id=1, source_target_pairs={{0,8},{2,66},{4,12},{6,70},{8,0},{10,74},{12,4},{14,78},{1,9},{3,6... | collective-permute-start | bytes 1179656 | tf_op jit(solution)/shard_map/ppermute | solution.py:283
  20.9 15.8 %collective-permute-start.12 = (bf16[4,3,32,2048]{3,2,1,0:T(8,128)(2,1)S(1)}, bf16[4,3,32,2048]{3,2,1,0:T(8,128)(2,1)S(1)}, u32[]{:S(2)}, u32[]{:S(2)}) collective-permute-start(bf16[4,3,32,2048]{3,2,1,0:T(8,128)(2,1)S(1)} %join.2.refs_0_), channel_id=1, source_target_pairs={{0,2},{2,0},{4,6},{6,4},{8,10},{10,8},{12,14},{14,12},{1,3},{3,1},... | collective-permute-start | bytes 4718600 | tf_op jit(solution)/shard_map/ppermute | solution.py:283
  33.4 3.2 %copy-start.1 = (s32[3,2]{0,1:T(2,128)S(1)}, s32[3,2]{0,1:T(2,128)}, u32[]{:S(2)}) copy-start(s32[3,2]{0,1:T(2,128)} %param.10) | copy-start | bytes 76
  33.4 3.2 %copy-start.3 = (f32[3]{0:T(128)S(1)}, f32[3]{0:T(128)}, u32[]{:S(2)}) copy-start(f32[3]{0:T(128)} %freq_ref.13) | copy-start | bytes 40
  33.6 7.6 %collective-permute-start.11 = (bf16[4,3,32,2048]{3,2,1,0:T(8,128)(2,1)S(1)}, bf16[4,3,32,2048]{3,2,1,0:T(8,128)(2,1)S(1)}, u32[]{:S(2)}, u32[]{:S(2)}) collective-permute-start(bf16[4,3,32,2048]{3,2,1,0:T(8,128)(2,1)S(1)} %join.3.refs_0_), channel_id=1, source_target_pairs={{0,2},{2,0},{4,6},{6,4},{8,10},{10,8},{12,14},{14,12},{1,3},{3,1},... | collective-permute-start | bytes 4718600 | tf_op jit(solution)/shard_map/ppermute | solution.py:283
  34.6 19.6 %collective-permute-start.10 = (bf16[4,3,32,2048]{3,2,1,0:T(8,128)(2,1)S(1)}, bf16[4,3,32,2048]{3,2,1,0:T(8,128)(2,1)S(1)}, u32[]{:S(2)}, u32[]{:S(2)}) collective-permute-start(bf16[4,3,32,2048]{3,2,1,0:T(8,128)(2,1)S(1)} %join.2.refs_0_), channel_id=1, source_target_pairs={{0,96},{2,14},{4,100},{6,2},{8,104},{10,6},{12,108},{14,10},{1,97}... | collective-permute-start | bytes 4718600 | tf_op jit(solution)/shard_map/ppermute | solution.py:283
  36.6 20.5 %collective-permute-start.9 = (bf16[4,3,32,2048]{3,2,1,0:T(8,128)(2,1)S(1)}, bf16[4,3,32,2048]{3,2,1,0:T(8,128)(2,1)S(1)}, u32[]{:S(2)}, u32[]{:S(2)}) collective-permute-start(bf16[4,3,32,2048]{3,2,1,0:T(8,128)(2,1)S(1)} %join.2.refs_0_), channel_id=1, source_target_pairs={{0,32},{2,6},{4,36},{6,10},{8,40},{10,14},{12,44},{14,2},{1,33},{3... | collective-permute-start | bytes 4718600 | tf_op jit(solution)/shard_map/ppermute | solution.py:283
  57.1 3.4 %collective-permute-start.13 = (bf16[4,3,32,2048]{3,2,1,0:T(8,128)(2,1)S(1)}, bf16[4,3,32,2048]{3,2,1,0:T(8,128)(2,1)S(1)}, u32[]{:S(2)}, u32[]{:S(2)}) collective-permute-start(bf16[4,3,32,2048]{3,2,1,0:T(8,128)(2,1)S(1)} %collective-permute-done.9.refs_0_), channel_id=1, source_target_pairs={{0,2},{2,0},{4,6},{6,4},{8,10},{10,8},{12,14},{14,12},{1,3},{3,1},... | collective-permute-start | bytes 4718600 | tf_op jit(solution)/shard_map/ppermute | solution.py:283
  57.5 5.3 %collective-permute-start.14 = (bf16[4,3,32,2048]{3,2,1,0:T(8,128)(2,1)S(1)}, bf16[4,3,32,2048]{3,2,1,0:T(8,128)(2,1)S(1)}, u32[]{:S(2)}, u32[]{:S(2)}) collective-permute-start(bf16[4,3,32,2048]{3,2,1,0:T(8,128)(2,1)S(1)} %collective-permute-done.10.refs_2_), channel_id=1, source_target_pairs={{0,2},{2,0},{4,6},{6,4},{8,10},{10,8},{12,14},{14,12},{1,3},{3,1},... | collective-permute-start | bytes 4718600 | tf_op jit(solution)/shard_map/ppermute | solution.py:283
  57.6 19.6 %collective-permute-start.8 = (bf16[4,3,32,2048]{3,2,1,0:T(8,128)(2,1)S(1)}, bf16[4,3,32,2048]{3,2,1,0:T(8,128)(2,1)S(1)}, u32[]{:S(2)}, u32[]{:S(2)}) collective-permute-start(bf16[4,3,32,2048]{3,2,1,0:T(8,128)(2,1)S(1)} %join.3.refs_0_), channel_id=1, source_target_pairs={{0,96},{2,14},{4,100},{6,2},{8,104},{10,6},{12,108},{14,10},{1,97}... | collective-permute-start | bytes 4718600 | tf_op jit(solution)/shard_map/ppermute | solution.py:283
  77.2 4.3 %collective-permute-start.19 = (bf16[4,3,32,2048]{3,2,1,0:T(8,128)(2,1)S(1)}, bf16[4,3,32,2048]{3,2,1,0:T(8,128)(2,1)S(1)}, u32[]{:S(2)}, u32[]{:S(2)}) collective-permute-start(bf16[4,3,32,2048]{3,2,1,0:T(8,128)(2,1)S(1)} %collective-permute-done.8.refs_0_), channel_id=1, source_target_pairs={{0,2},{2,0},{4,6},{6,4},{8,10},{10,8},{12,14},{14,12},{1,3},{3,1},... | collective-permute-start | bytes 4718600 | tf_op jit(solution)/shard_map/ppermute | solution.py:283
  78.4 20.8 %collective-permute-start.18 = (bf16[4,3,32,2048]{3,2,1,0:T(8,128)(2,1)S(1)}, bf16[4,3,32,2048]{3,2,1,0:T(8,128)(2,1)S(1)}, u32[]{:S(2)}, u32[]{:S(2)}) collective-permute-start(bf16[4,3,32,2048]{3,2,1,0:T(8,128)(2,1)S(1)} %collective-permute-done.9.refs_0_), channel_id=1, source_target_pairs={{0,32},{2,6},{4,36},{6,10},{8,40},{10,14},{12,44},{14,2},{1,33},{3... | collective-permute-start | bytes 4718600 | tf_op jit(solution)/shard_map/ppermute | solution.py:283
  99.2 3.9 %collective-permute-start.20 = (bf16[4,3,32,2048]{3,2,1,0:T(8,128)(2,1)S(1)}, bf16[4,3,32,2048]{3,2,1,0:T(8,128)(2,1)S(1)}, u32[]{:S(2)}, u32[]{:S(2)}) collective-permute-start(bf16[4,3,32,2048]{3,2,1,0:T(8,128)(2,1)S(1)} %collective-permute-done.18.refs_0_), channel_id=1, source_target_pairs={{0,2},{2,0},{4,6},{6,4},{8,10},{10,8},{12,14},{14,12},{1,3},{3,1},... | collective-permute-start | bytes 4718600 | tf_op jit(solution)/shard_map/ppermute | solution.py:283
  100.0 20.8 %collective-permute-start.17 = (bf16[4,3,32,2048]{3,2,1,0:T(8,128)(2,1)S(1)}, bf16[4,3,32,2048]{3,2,1,0:T(8,128)(2,1)S(1)}, u32[]{:S(2)}, u32[]{:S(2)}) collective-permute-start(bf16[4,3,32,2048]{3,2,1,0:T(8,128)(2,1)S(1)} %join.3.refs_0_), channel_id=1, source_target_pairs={{0,32},{2,6},{4,36},{6,10},{8,40},{10,14},{12,44},{14,2},{1,33},{3... | collective-permute-start | bytes 4718600 | tf_op jit(solution)/shard_map/ppermute | solution.py:283
  101.0 20.7 %collective-permute-start.15 = (bf16[4,3,32,2048]{3,2,1,0:T(8,128)(2,1)S(1)}, bf16[4,3,32,2048]{3,2,1,0:T(8,128)(2,1)S(1)}, u32[]{:S(2)}, u32[]{:S(2)}) collective-permute-start(bf16[4,3,32,2048]{3,2,1,0:T(8,128)(2,1)S(1)} %collective-permute-done.8.refs_0_), channel_id=1, source_target_pairs={{0,96},{2,14},{4,100},{6,2},{8,104},{10,6},{12,108},{14,10},{1,97}... | collective-permute-start | bytes 4718600 | tf_op jit(solution)/shard_map/ppermute | solution.py:283
  120.8 3.9 %collective-permute-start.21 = (bf16[4,3,32,2048]{3,2,1,0:T(8,128)(2,1)S(1)}, bf16[4,3,32,2048]{3,2,1,0:T(8,128)(2,1)S(1)}, u32[]{:S(2)}, u32[]{:S(2)}) collective-permute-start(bf16[4,3,32,2048]{3,2,1,0:T(8,128)(2,1)S(1)} %collective-permute-done.17.refs_0_), channel_id=1, source_target_pairs={{0,2},{2,0},{4,6},{6,4},{8,10},{10,8},{12,14},{14,12},{1,3},{3,1},... | collective-permute-start | bytes 4718600 | tf_op jit(solution)/shard_map/ppermute | solution.py:283
  121.7 8.6 %collective-permute-start.16 = (bf16[4,3,32,2048]{3,2,1,0:T(8,128)(2,1)S(1)}, bf16[4,3,32,2048]{3,2,1,0:T(8,128)(2,1)S(1)}, u32[]{:S(2)}, u32[]{:S(2)}) collective-permute-start(bf16[4,3,32,2048]{3,2,1,0:T(8,128)(2,1)S(1)} %collective-permute-done.15.refs_0_), channel_id=1, source_target_pairs={{0,2},{2,0},{4,6},{6,4},{8,10},{10,8},{12,14},{14,12},{1,3},{3,1},... | collective-permute-start | bytes 4718600 | tf_op jit(solution)/shard_map/ppermute | solution.py:283
where the time goes:
time: 136 us
  waiting for transfers between devices  54.6 us (40%)
  Pallas kernels  53.9 us (40%)
  starting transfers between devices  26.6 us (20%)
    ppermute x22, waiting for transfers between devices, send(): return lax.ppermute(array, AXES, pairs)  54.6 us
    pallas_call x7, Pallas kernels, collide(): pl.pallas_call(functools.partial(collide_kernel, len(groups), acc is None...  41.9 us
    ppermute x22, starting transfers between devices, send(): return lax.ppermute(array, AXES, pairs)  26.6 us
    pallas_call x1, Pallas kernels, transport(): pl.pallas_call(transport_kernel, in_specs=[SMEM, VMEM, VMEM, VMEM, HBM],...  9.5 us
  transfers between devices with their start and end apart: 22, of which 13 were waited for; matrix products, arithmetic and copies ran while one was open for 0% of the time, Pallas kernels for 35%

commit v1 on v0

--- a/solution.py
+++ b/solution.py
@@ -55,7 +55,7 @@
     return pltpu.with_memory_space_constraint(array, pltpu.HBM)
 
 
-def packet_kernel(where_ref, signs_hbm, cells_ref, out_ref, rows, signs_ref, sem, sign_sem):
+def packet_kernel(where_ref, signs_hbm, cells_ref, out_ref, rows, edges, signs_ref, sem, sign_sem):
     first_part = where_ref[0] == 0
     species, lines, cells, coeffs = cells_ref.shape
     start = pl.multiple_of(jnp.where(first_part, cells - 8, 0), 8)
@@ -63,38 +63,41 @@
     copy.start()
     sign_copy = pltpu.make_async_copy(signs_hbm, signs_ref, sign_sem)
     sign_copy.start()
-    out_ref[species * lines] = jnp.zeros((2, coeffs), jnp.bfloat16)
+    total = species * lines
+    edges[:, total:, :] = jnp.zeros((2, 8, coeffs), jnp.float32)
     sign_copy.wait()
-    last = signs_ref[cells - 1 : cells, :].astype(jnp.float32)
-    last = jnp.concatenate([last, last], axis=0).astype(jnp.bfloat16)
-    out_ref[species * lines, :, 0:lines] = last
+    edges[0, total : total + 1, 0:lines] = signs_ref[cells - 1 : cells, :].astype(jnp.float32)
     copy.wait()
 
     def one(l, carry):
         for s in range(species):
             eight = rows[s, l].astype(jnp.float32)
-            edge = jnp.where(first_part, eight[6:8], eight[0:2])
-            out_ref[s * lines + l] = edge.astype(jnp.bfloat16)
+            at = pl.ds(s * lines + l, 1)
+            edges[0, at, :] = jnp.where(first_part, eight[6:7], eight[0:1])
+            edges[1, at, :] = jnp.where(first_part, eight[7:8], eight[1:2])
         return carry
 
     lax.fori_loop(0, lines, one, 0)
+    out_ref[...] = edges[...].astype(jnp.bfloat16)
 
 
 def packet_of(cells, signs, where):
     species, lines, _, coeffs = cells.shape
+    shape = (2, species * lines + 8, coeffs)
     return pl.pallas_call(
         packet_kernel,
         in_specs=[SMEM, HBM, HBM],
         out_specs=VMEM,
-        out_shape=jax.ShapeDtypeStruct((species * lines + 1, 2, coeffs), jnp.bfloat16),
+        out_shape=jax.ShapeDtypeStruct(shape, jnp.bfloat16),
         scratch_shapes=[
             pltpu.VMEM((species, lines, 8, coeffs), jnp.bfloat16),
+            pltpu.VMEM(shape, jnp.float32),
             pltpu.VMEM(signs.shape, jnp.int32),
             DMA,
             DMA,
         ],
         cost_estimate=cost(cells.size, cells.size),
-        compiler_params=pltpu.CompilerParams(vmem_limit_bytes=8 << 20),
+        compiler_params=pltpu.CompilerParams(vmem_limit_bytes=10 << 20),
         name="packet",
     )(where, stay(signs), stay(cells))
 
@@ -102,10 +105,13 @@
 CHUNKS = 4
 
 
-def transport_kernel(where_ref, speed_ref, signs_ref, packet_ref, cells_hbm, out_ref, out_hbm, cells_ref, in_sem, out_sem):
+def transport_kernel(
+    where_ref, speed_ref, signs_ref, packet_ref, cells_hbm, out_ref, out_hbm, cells_ref, sides, dirs, in_sem, out_sem
+):
     first_part = where_ref[0] == 0
     species, lines, cells, coeffs = cells_ref.shape
     chunk = lines // CHUNKS
+    total = species * lines
 
     def arriving(c):
         at = pl.ds(c * chunk, chunk)
@@ -117,41 +123,65 @@
 
     for c in range(CHUNKS):
         arriving(c).start()
-    width = 512
-    row = lax.broadcasted_iota(jnp.int32, (cells, width), 0)
-    row1 = lax.broadcasted_iota(jnp.int32, (cells, lines), 0)
-    lane = lax.broadcasted_iota(jnp.int32, (cells, lines), 1)
+
+    column = lax.broadcasted_iota(jnp.int32, (cells, lines), 0)
     signs = (2 * signs_ref[...] - 1).astype(jnp.float32)
-    signs = jnp.where(jnp.logical_and(row1 == cells - 1, jnp.logical_not(first_part)), 0.0, signs)
-    got = 2.0 * packet_ref[species * lines, 0:1, 0:lines].astype(jnp.float32) - 1.0
+    signs = jnp.where(jnp.logical_and(column == cells - 1, jnp.logical_not(first_part)), 0.0, signs)
+    got = 2.0 * packet_ref[0, total : total + 8, 0:lines].astype(jnp.float32) - 1.0
     got = jnp.where(first_part, 0.0, got)
+    for l in range(lines):
+        dirs[l, 0] = jnp.broadcast_to(signs[0:8, l : l + 1], (8, 128))
+        dirs[l, 1] = jnp.broadcast_to(signs[8:16, l : l + 1], (8, 128))
+        dirs[l, 2] = jnp.broadcast_to(got[0:1, l : l + 1], (8, 128))
+
+    def side(t, carry):
+        at = pl.ds(pl.multiple_of(t * 128, 128), 128)
+        h0 = packet_ref[0, :, at].astype(jnp.float32)[0:total]
+        h1 = packet_ref[1, :, at].astype(jnp.float32)[0:total]
+        zero = jnp.zeros_like(h0)
+        sides[0, t, 0:total] = jnp.where(first_part, zero, h1)
+        sides[1, t, 0:total] = jnp.where(first_part, h0, zero)
+        sides[2, t, 0:total] = jnp.where(first_part, h0 - 0.5 * (h1 - h0), h1 + 0.5 * (h1 - h0))
+        sides[3, t, 0:total] = jnp.where(first_part, h1 - h0, zero)
+        return carry
+
+    lax.fori_loop(0, coeffs // 128, side, 0)
+    row = lax.broadcasted_iota(jnp.int32, (8, 128), 0)
+    top, bottom = row == 0, row == 7
+
+    def down(low, high, edge):
+        low_r, high_r = pltpu.roll(low, 1, 0), pltpu.roll(high, 1, 0)
+        return jnp.where(top, edge, low_r), jnp.where(top, low_r, high_r)
+
+    def up(low, high, edge):
+        low_r, high_r = pltpu.roll(low, 7, 0), pltpu.roll(high, 7, 0)
+        return jnp.where(bottom, high_r, low_r), jnp.where(bottom, edge, high_r)
 
     def one(l, carry):
-        d_right = jnp.sum(jnp.where(lane == l, signs, 0.0), axis=1, keepdims=True)
-        d_first = jnp.sum(jnp.where(lane[0:1] == l, got, 0.0), axis=1, keepdims=True)
-        d_right = jnp.broadcast_to(d_right, (cells, width))
-        d_first = jnp.broadcast_to(d_first, (1, width))
-        for c in range(coeffs // width):
-            at = slice(c * width, (c + 1) * width)
-            speed = speed_ref[:, at]
+        d0, d1, df = dirs[l, 0], dirs[l, 1], dirs[l, 2]
+        p0, p1, pf = d0 > 0, d1 > 0, df > 0
+        for c in range(coeffs // 128):
+            at = slice(c * 128, (c + 1) * 128)
+            speed = jnp.broadcast_to(speed_ref[:, at], (8, 128))
+            v0, v1, vf = d0 * speed, d1 * speed, df * speed
             for s in range(species):
                 f = cells_ref[s, l, :, at].astype(jnp.float32)
-                halo = packet_ref[s * lines + l, :, at].astype(jnp.float32)
-                h0, h1 = halo[0:1], halo[1:2]
-                zero = jnp.zeros_like(h0)
-                left2, left1 = jnp.where(first_part, zero, h0), jnp.where(first_part, zero, h1)
-                right1, right2 = jnp.where(first_part, h0, zero), jnp.where(first_part, h1, zero)
-                before = jnp.where(row == 0, left1, pltpu.roll(f, 1, 0))
-                after = jnp.where(row == cells - 1, right1, pltpu.roll(f, cells - 1, 0))
-                upper = f + 0.5 * (f - before)
-                lower = f - 0.5 * (after - f)
-                lower_last = right1 - 0.5 * (right2 - right1)
-                lower_next = jnp.where(row == cells - 1, lower_last, pltpu.roll(lower, cells - 1, 0))
-                flux = d_right * speed * jnp.where(d_right > 0, upper, lower_next)
-                upper_first = left1 + 0.5 * (left1 - left2)
-                flux_first = d_first * speed * jnp.where(d_first > 0, upper_first, lower[0:1])
-                flux_before = jnp.where(row == 0, flux_first, pltpu.roll(flux, 1, 0))
-                out_ref[s, l, :, at] = (f - courant * (flux - flux_before)).astype(jnp.bfloat16)
+                f0, f1 = f[0:8], f[8:16]
+                left, right, ext, diff = (
+                    sides[k, c, pl.ds(s * lines + l, 8, stride=0), :] for k in range(4)
+                )
+                a0, a1 = up(f0, f1, right)
+                b0, b1 = down(f0, f1, left)
+                n0, n1 = a0 - f0, a1 - f1
+                m0, m1 = up(n0, n1, diff)
+                upper0, upper1 = f0 + 0.5 * (f0 - b0), f1 + 0.5 * (f1 - b1)
+                lower0, lower1 = a0 - 0.5 * m0, a1 - 0.5 * m1
+                flux0 = v0 * jnp.where(p0, upper0, lower0)
+                flux1 = v1 * jnp.where(p1, upper1, lower1)
+                first = vf * jnp.where(pf, ext, f0 - 0.5 * n0)
+                g0, g1 = down(flux0, flux1, first)
+                new = jnp.concatenate([f0 - courant * (flux0 - g0), f1 - courant * (flux1 - g1)], axis=0)
+                out_ref[s, l, :, at] = new.astype(jnp.bfloat16)
         return carry
 
     for c in range(CHUNKS):
@@ -163,6 +193,7 @@
 
 
 def transport(cells, packet, signs, speed, where):
+    species, lines, _, coeffs = cells.shape
     return pl.pallas_call(
         transport_kernel,
         in_specs=[SMEM, VMEM, VMEM, VMEM, HBM],
@@ -171,7 +202,13 @@
             pltpu.VMEM(cells.shape, jnp.bfloat16),
             jax.ShapeDtypeStruct(cells.shape, jnp.bfloat16),
         ],
-        scratch_shapes=[pltpu.VMEM(cells.shape, jnp.bfloat16), DMA((CHUNKS,)), DMA((CHUNKS,))],
+        scratch_shapes=[
+            pltpu.VMEM(cells.shape, jnp.bfloat16),
+            pltpu.VMEM((4, coeffs // 128, species * lines + 8, 128), jnp.float32),
+            pltpu.VMEM((cells.shape[1], 3, 8, 128), jnp.float32),
+            DMA((CHUNKS,)),
+            DMA((CHUNKS,)),
+        ],
         cost_estimate=cost(30 * cells.size, 4 * cells.size),
         compiler_params=pltpu.CompilerParams(vmem_limit_bytes=16 << 20),
         name="transport",
@@ -203,7 +240,8 @@
     out_ref = refs[0]
     species, rows, coeffs = adv_ref.shape
     pair_count = out_ref.shape[0]
-    block = rows // 2
+    blocks = 2 if last else 1
+    block = rows // blocks
     nt = (((1,), (1,)), ((), ()))
 
     def leaving(i, p):
@@ -246,9 +284,9 @@
                 out_ref[p, at, :] = term
             return carry
 
-        lax.fori_loop(0, 2, step, 0)
+        lax.fori_loop(0, blocks, step, 0)
     if last:
-        for i in range(2):
+        for i in range(blocks):
             for p in range(pair_count):
                 leaving(i, p).wait()
 
@@ -299,14 +337,13 @@
 
     cross = send(mine, CROSS)
     parts_o = phase(mine)
+    parts_c = phase(cross)
     packet = packet_of(distribution, signs, here)
     got = send(packet, SIDE)
     parts_o[0] = after(mine, packet)
     group_o = join(parts_o)
     up_o, down_o = send(group_o, UP2), send(group_o, DOWN2)
     swap_o = send(group_o, PARTNER)
-
-    parts_c = phase(after(cross, group_o))
     adv_near, advanced = transport(distribution, got, signs, stream_speed[None], here)
     parts_c[0] = after(parts_c[0], adv_near)
     group_c = join(parts_c)
@@ -322,15 +359,17 @@
     acc = step([group_c, swap_c], acc)
     up_o, down_o, _ = lax.optimization_barrier((up_o, down_o, acc))
     far_o = send(up_o, UP2)
-    acc = step([up_o, send(up_o, PARTNER), down_o, send(down_o, PARTNER)], acc)
-    down_c = after(down_c, acc)
+    swap_uo, swap_do = send(up_o, PARTNER), send(down_o, PARTNER)
+    acc = step([up_o, swap_uo, down_o, swap_do], acc)
+    down_c, up_c, _ = lax.optimization_barrier((down_c, up_c, acc))
     far_c = send(down_c, DOWN2)
-    acc = step([down_c, send(down_c, PARTNER)], acc)
-    far_o = after(far_o, acc)
-    acc = step([far_o, send(far_o, PARTNER)], acc)
-    up_c = after(up_c, acc)
-    acc = step([up_c, send(up_c, PARTNER)], acc)
-    out = step([far_c, send(far_c, PARTNER)], acc, last=True)
+    swap_dc, swap_uc = send(down_c, PARTNER), send(up_c, PARTNER)
+    acc = step([down_c, up_c], acc)
+    acc = step([swap_dc, swap_uc], acc)
+    far_o, far_c, _ = lax.optimization_barrier((far_o, far_c, acc))
+    swap_fo, swap_fc = send(far_o, PARTNER), send(far_c, PARTNER)
+    acc = step([far_o, far_c], acc)
+    out = step([swap_fo, swap_fc], acc, last=True)
     collision = out.reshape(pair_list.shape[0], lines, cells, coeffs)
     return (advanced, collision)
 

time: 136 us -> 115 us (0.85)
  waiting for transfers between devices: 54.6 us -> 35.2 us
  Pallas kernels: 53.9 us -> 49.8 us
  starting transfers between devices: 26.6 us -> 29 us
    ppermute x22, waiting for transfers between devices: 54.6 us -> 35.2 us  [send(): return lax.ppermute(array, AXES, pairs)]
    pallas_call x7, Pallas kernels: 41.9 us -> 39 us  [collide(): pl.pallas_call(functools.partial(collide_kernel, len(groups), acc is None...]
    ppermute x22, starting transfers between devices: 26.6 us -> 29 us  [send(): return lax.ppermute(array, AXES, pairs)]
    pallas_call x1, Pallas kernels: 9.5 us -> 8.12 us  [transport(): pl.pallas_call(transport_kernel, in_specs=[SMEM, VMEM, VMEM, VMEM, HBM],...]
  transfers between devices with their start and end apart: 22 -> 22, of which waited for: 13 -> 10; matrix products, arithmetic and copies ran while one was open for 0% -> 0% of each run, Pallas kernels for 35% -> 38%
where the time goes in v1:
time: 115 us
  Pallas kernels  49.8 us (43%)
  waiting for transfers between devices  35.2 us (31%)
  starting transfers between devices  29 us (25%)
    pallas_call x7, Pallas kernels, collide(): pl.pallas_call(functools.partial(collide_kernel, len(groups), acc is None...  39 us
    ppermute x22, waiting for transfers between devices, send(): return lax.ppermute(array, AXES, pairs)  35.2 us
    ppermute x22, starting transfers between devices, send(): return lax.ppermute(array, AXES, pairs)  29 us
    pallas_call x1, Pallas kernels, transport(): pl.pallas_call(transport_kernel, in_specs=[SMEM, VMEM, VMEM, VMEM, HBM],...  8.12 us
    pallas_call x1, Pallas kernels, packet_of(): pl.pallas_call(packet_kernel, in_specs=[SMEM, HBM, HBM], out_specs=VMEM,...  2.4 us
  transfers between devices with their start and end apart: 22, of which 10 were waited for; matrix products, arithmetic and copies ran while one was open for 0% of the time, Pallas kernels for 38%

profile of v1, /device:TPU:1, one launch (start us, length us, event | category | flops | bytes accessed | tf_op | source)
XLA Modules:
  0.0 115.0 jit_solution(9692796714029645141)
XLA Ops:
  0.6 3.6 %collective-permute-start.6 = (bf16[1,3,32,2048]{3,2,1,0:T(8,128)(2,1)}, bf16[1,3,32,2048]{3,2,1,0:T(8,128)(2,1)S(1)}, u32[]{:S(2)}, u32[]{:S(2)}) collective-permute-start(bf16[1,3,32,2048]{3,2,1,0:T(8,128)(2,1)} %bitcast.14), channel_id=1, source_target_pairs={{0,17},{2,19},{4,21},{6,23},{8,25},{10,27},{12,29},{14,31},{1,16},... | collective-permute-start | bytes 1179656 | tf_op jit(solution)/shard_map/ppermute | solution.py:321
  4.3 1.6 %collective-permute-start.1 = (bf16[1,3,32,2048]{3,2,1,0:T(8,128)(2,1)}, bf16[1,3,32,2048]{3,2,1,0:T(8,128)(2,1)S(1)}, u32[]{:S(2)}, u32[]{:S(2)}) collective-permute-start(bf16[1,3,32,2048]{3,2,1,0:T(8,128)(2,1)} %bitcast.15), channel_id=1, source_target_pairs={{0,4},{2,34},{4,8},{6,38},{8,12},{10,42},{12,0},{14,46},{1,5},{3,3... | collective-permute-start | bytes 1179656 | tf_op jit(solution)/shard_map/ppermute | solution.py:321
  5.9 2.1 %collective-permute-start.2 = (bf16[1,3,32,2048]{3,2,1,0:T(8,128)(2,1)}, bf16[1,3,32,2048]{3,2,1,0:T(8,128)(2,1)S(1)}, u32[]{:S(2)}, u32[]{:S(2)}) collective-permute-start(bf16[1,3,32,2048]{3,2,1,0:T(8,128)(2,1)} %bitcast.16), channel_id=1, source_target_pairs={{0,12},{2,98},{4,0},{6,102},{8,4},{10,106},{12,8},{14,110},{1,13},... | collective-permute-start | bytes 1179656 | tf_op jit(solution)/shard_map/ppermute | solution.py:321
  8.0 1.3 %collective-permute-start.3 = (bf16[1,3,32,2048]{3,2,1,0:T(8,128)(2,1)}, bf16[1,3,32,2048]{3,2,1,0:T(8,128)(2,1)S(1)}, u32[]{:S(2)}, u32[]{:S(2)}) collective-permute-start(bf16[1,3,32,2048]{3,2,1,0:T(8,128)(2,1)} %bitcast.17), channel_id=1, source_target_pairs={{0,8},{2,66},{4,12},{6,70},{8,0},{10,74},{12,4},{14,78},{1,9},{3,6... | collective-permute-start | bytes 1179656 | tf_op jit(solution)/shard_map/ppermute | solution.py:321
  9.3 2.4 %packet.1 = bf16[2,64,2048]{2,1,0:T(8,128)(2,1)S(1)} custom-call(s32[1]{0:T(128)} %bitcast.where_ref, s32[16,28]{1,0:T(8,128)} %bitcast.26, bf16[2,28,16,2048]{3,2,1,0:T(8,128)(2,1)} %cells_hbm.1), custom_call_target="tpu_custom_call" | custom-call | flops 1835008 | bytes 1835008 | tf_op jit(solution)/shard_map/packet/pallas_call | solution.py:87
  11.7 0.0 copy-start.2
  11.8 0.0 copy-start.4
  11.8 0.1 collective-permute-start
  11.9 1.3 %collective-permute-done.6.refs_0_ = bf16[1,3,32,2048]{3,2,1,0:T(8,128)(2,1)S(1)} collective-permute-done((bf16[1,3,32,2048]{3,2,1,0:T(8,128)(2,1)}, bf16[1,3,32,2048]{3,2,1,0:T(8,128)(2,1)S(1)}, u32[]{:S(2)}, u32[]{:S(2)}) %collective-permute-start.6) | collective-permute-done | bytes 393248 | tf_op jit(solution)/shard_map/ppermute | solution.py:321
  13.2 1.5 %collective-permute-start.7 = (bf16[1,3,32,2048]{3,2,1,0:T(8,128)(2,1)S(1)}, bf16[1,3,32,2048]{3,2,1,0:T(8,128)(2,1)S(1)}, u32[]{:S(2)}, u32[]{:S(2)}) collective-permute-start(bf16[1,3,32,2048]{3,2,1,0:T(8,128)(2,1)S(1)} %collective-permute-done.6.refs_0_), channel_id=1, source_target_pairs={{0,4},{2,34},{4,8},{6,38},{8,12},{10,42},{12,0},{14,46},{1,5},{3,3... | collective-permute-start | bytes 1179656 | tf_op jit(solution)/shard_map/ppermute | solution.py:321
  14.7 0.0 collective-permute-done.1.refs_1_
  14.7 2.1 %collective-permute-start.8 = (bf16[1,3,32,2048]{3,2,1,0:T(8,128)(2,1)S(1)}, bf16[1,3,32,2048]{3,2,1,0:T(8,128)(2,1)S(1)}, u32[]{:S(2)}, u32[]{:S(2)}) collective-permute-start(bf16[1,3,32,2048]{3,2,1,0:T(8,128)(2,1)S(1)} %collective-permute-done.6.refs_0_), channel_id=1, source_target_pairs={{0,12},{2,98},{4,0},{6,102},{8,4},{10,106},{12,8},{14,110},{1,13},... | collective-permute-start | bytes 1179656 | tf_op jit(solution)/shard_map/ppermute | solution.py:321
  16.8 0.5 collective-permute-done.2.refs_2_
  17.3 1.9 %collective-permute-start.9 = (bf16[1,3,32,2048]{3,2,1,0:T(8,128)(2,1)S(1)}, bf16[1,3,32,2048]{3,2,1,0:T(8,128)(2,1)S(1)}, u32[]{:S(2)}, u32[]{:S(2)}) collective-permute-start(bf16[1,3,32,2048]{3,2,1,0:T(8,128)(2,1)S(1)} %collective-permute-done.6.refs_0_), channel_id=1, source_target_pairs={{0,8},{2,66},{4,12},{6,70},{8,0},{10,74},{12,4},{14,78},{1,9},{3,6... | collective-permute-start | bytes 1179656 | tf_op jit(solution)/shard_map/ppermute | solution.py:321
  19.2 0.1 join.2.refs_0_
  19.3 0.5 collective-permute-start.11
  19.8 4.6 %collective-permute-done.packet_ref = bf16[2,64,2048]{2,1,0:T(8,128)(2,1)S(1)} collective-permute-done((bf16[2,64,2048]{2,1,0:T(8,128)(2,1)S(1)}, bf16[2,64,2048]{2,1,0:T(8,128)(2,1)S(1)}, u32[]{:S(2)}, u32[]{:S(2)}) %collective-permute-start) | collective-permute-done | bytes 524320 | tf_op jit(solution)/shard_map/ppermute | solution.py:321
  24.4 8.1 %transport.1 = (bf16[2,28,16,2048]{3,2,1,0:T(8,128)(2,1)S(1)}, bf16[2,28,16,2048]{3,2,1,0:T(8,128)(2,1)}) custom-call(s32[1]{0:T(128)} %bitcast.where_ref, f32[1,2048]{1,0:T(1,128)S(1)} %bitcast.28, s32[16,28]{1,0:T(8,128)S(1)} %bitcast.27, bf16[2,64,2048]{2,1,0:T(8,128)(2,1)S(1)} %collective-permute-done.packet_ref, bf16[2,28,16,2048]{3,2,1,0:T(8,128)(2,1)} %cells_hbm.1), custom_call_target="tpu_custom_call" | custom-call | flops 55050240 | bytes 7340032 | tf_op jit(solution)/shard_map/transport/pallas_call | solution.py:197
  32.5 0.0 copy-start.1
  32.5 0.0 copy-start.3
  32.6 0.1 join.3.refs_0_
  32.7 1.9 %collective-permute-start.10 = (bf16[4,3,32,2048]{3,2,1,0:T(8,128)(2,1)S(1)}, bf16[4,3,32,2048]{3,2,1,0:T(8,128)(2,1)S(1)}, u32[]{:S(2)}, u32[]{:S(2)}) collective-permute-start(bf16[4,3,32,2048]{3,2,1,0:T(8,128)(2,1)S(1)} %join.3.refs_0_), channel_id=1, source_target_pairs={{0,2},{2,0},{4,6},{6,4},{8,10},{10,8},{12,14},{14,12},{1,3},{3,1},... | collective-permute-start | bytes 4718600 | tf_op jit(solution)/shard_map/ppermute | solution.py:321
  34.6 1.2 %collective-permute-start.4 = (bf16[4,3,32,2048]{3,2,1,0:T(8,128)(2,1)S(1)}, bf16[4,3,32,2048]{3,2,1,0:T(8,128)(2,1)S(1)}, u32[]{:S(2)}, u32[]{:S(2)}) collective-permute-start(bf16[4,3,32,2048]{3,2,1,0:T(8,128)(2,1)S(1)} %join.2.refs_0_), channel_id=1, source_target_pairs={{0,32},{2,6},{4,36},{6,10},{8,40},{10,14},{12,44},{14,2},{1,33},{3... | collective-permute-start | bytes 4718600 | tf_op jit(solution)/shard_map/ppermute | solution.py:321
  35.8 1.5 %collective-permute-start.5 = (bf16[4,3,32,2048]{3,2,1,0:T(8,128)(2,1)S(1)}, bf16[4,3,32,2048]{3,2,1,0:T(8,128)(2,1)S(1)}, u32[]{:S(2)}, u32[]{:S(2)}) collective-permute-start(bf16[4,3,32,2048]{3,2,1,0:T(8,128)(2,1)S(1)} %join.2.refs_0_), channel_id=1, source_target_pairs={{0,96},{2,14},{4,100},{6,2},{8,104},{10,6},{12,108},{14,10},{1,97}... | collective-permute-start | bytes 4718600 | tf_op jit(solution)/shard_map/ppermute | solution.py:321
  37.2 4.2 %collide.7.refs_2_ = f32[3,448,2048]{2,1,0:T(8,128)S(1)} custom-call(f32[3]{0:T(128)S(1)} %copy-done.3, s32[2,3]{1,0:T(2,128)S(1)} %bitcast.19, bf16[2,448,2048]{2,1,0:T(8,128)(2,1)S(1)} %bitcast.7, bf16[4,3,32,2048]{3,2,1,0:T(8,128)(2,1)S(1)} %join.2.refs_0_, bf16[4,3,32,2048]{3,2,1,0:T(8,128)(2,1)S(1)} %collective-permute-done.11.refs_1_), custom_call_target="tpu_custom_call" | custom-call | flops 3288334336 | bytes 6815744 | tf_op jit(solution)/shard_map/collide/pallas_call | solution.py:304
  41.4 5.2 %collide.8.refs_4_ = f32[3,448,2048]{2,1,0:T(8,128)S(1)} custom-call(f32[3]{0:T(128)S(1)} %copy-done.3, s32[2,3]{1,0:T(2,128)S(1)} %bitcast.20, bf16[2,448,2048]{2,1,0:T(8,128)(2,1)S(1)} %bitcast.8, bf16[4,3,32,2048]{3,2,1,0:T(8,128)(2,1)S(1)} %join.3.refs_0_, ...), custom_call_target="tpu_custom_call", output_to_operand_aliasing={{}: (5, {})} | custom-call | flops 3288334336 | bytes 6815744 | tf_op jit(solution)/shard_map/collide/pallas_call | solution.py:304
  46.6 8.7 %collective-permute-done.4.refs_0_ = bf16[4,3,32,2048]{3,2,1,0:T(8,128)(2,1)S(1)} collective-permute-done((bf16[4,3,32,2048]{3,2,1,0:T(8,128)(2,1)S(1)}, bf16[4,3,32,2048]{3,2,1,0:T(8,128)(2,1)S(1)}, u32[]{:S(2)}, u32[]{:S(2)}) %collective-permute-start.4) | collective-permute-done | bytes 1572896 | tf_op jit(solution)/shard_map/ppermute | solution.py:321
  55.3 0.9 collective-permute-start.15
  56.3 0.0 collective-permute-start.16
  56.3 2.3 %collective-permute-start.13 = (bf16[4,3,32,2048]{3,2,1,0:T(8,128)(2,1)S(1)}, bf16[4,3,32,2048]{3,2,1,0:T(8,128)(2,1)S(1)}, u32[]{:S(2)}, u32[]{:S(2)}) collective-permute-start(bf16[4,3,32,2048]{3,2,1,0:T(8,128)(2,1)S(1)} %join.3.refs_0_), channel_id=1, source_target_pairs={{0,96},{2,14},{4,100},{6,2},{8,104},{10,6},{12,108},{14,10},{1,97}... | collective-permute-start | bytes 4718600 | tf_op jit(solution)/shard_map/ppermute | solution.py:321
  58.6 0.0 collective-permute-start.14
  58.6 0.7 collective-permute-done.15.refs_1_
  59.3 2.2 %collective-permute-done.16.refs_3_ = bf16[4,3,32,2048]{3,2,1,0:T(8,128)(2,1)S(1)} collective-permute-done((bf16[4,3,32,2048]{3,2,1,0:T(8,128)(2,1)S(1)}, bf16[4,3,32,2048]{3,2,1,0:T(8,128)(2,1)S(1)}, u32[]{:S(2)}, u32[]{:S(2)}) %collective-permute-start.16) | collective-permute-done | bytes 1572896 | tf_op jit(solution)/shard_map/ppermute | solution.py:321
  61.6 8.5 %collide.9.refs_2_ = f32[3,448,2048]{2,1,0:T(8,128)S(1)} custom-call(f32[3]{0:T(128)S(1)} %copy-done.3, s32[2,3]{1,0:T(2,128)S(1)} %bitcast.21, bf16[2,448,2048]{2,1,0:T(8,128)(2,1)S(1)} %bitcast.9, bf16[4,3,32,2048]{3,2,1,0:T(8,128)(2,1)S(1)} %collective-permute-done.4.refs_0_, ...), custom_call_target="tpu_custom_call", output_to_operand_aliasing={{}: (7, {})} | custom-call | flops 6576668672 | bytes 9961472 | tf_op jit(solution)/shard_map/collide/pallas_call | solution.py:304
  70.1 5.9 %collective-permute-done.13.refs_0_ = bf16[4,3,32,2048]{3,2,1,0:T(8,128)(2,1)S(1)} collective-permute-done((bf16[4,3,32,2048]{3,2,1,0:T(8,128)(2,1)S(1)}, bf16[4,3,32,2048]{3,2,1,0:T(8,128)(2,1)S(1)}, u32[]{:S(2)}, u32[]{:S(2)}) %collective-permute-start.13) | collective-permute-done | bytes 1572896 | tf_op jit(solution)/shard_map/ppermute | solution.py:321
  75.9 3.4 %collective-permute-done.14.refs_1_ = bf16[4,3,32,2048]{3,2,1,0:T(8,128)(2,1)S(1)} collective-permute-done((bf16[4,3,32,2048]{3,2,1,0:T(8,128)(2,1)S(1)}, bf16[4,3,32,2048]{3,2,1,0:T(8,128)(2,1)S(1)}, u32[]{:S(2)}, u32[]{:S(2)}) %collective-permute-start.14) | collective-permute-done | bytes 1572896 | tf_op jit(solution)/shard_map/ppermute | solution.py:321
  79.3 2.3 %collective-permute-start.18 = (bf16[4,3,32,2048]{3,2,1,0:T(8,128)(2,1)S(1)}, bf16[4,3,32,2048]{3,2,1,0:T(8,128)(2,1)S(1)}, u32[]{:S(2)}, u32[]{:S(2)}) collective-permute-start(bf16[4,3,32,2048]{3,2,1,0:T(8,128)(2,1)S(1)} %collective-permute-done.13.refs_0_), channel_id=1, source_target_pairs={{0,2},{2,0},{4,6},{6,4},{8,10},{10,8},{12,14},{14,12},{1,3},{3,1},... | collective-permute-start | bytes 4718600 | tf_op jit(solution)/shard_map/ppermute | solution.py:321
  81.6 0.0 collective-permute-start.19
  81.7 1.2 %collective-permute-start.12 = (bf16[4,3,32,2048]{3,2,1,0:T(8,128)(2,1)S(1)}, bf16[4,3,32,2048]{3,2,1,0:T(8,128)(2,1)S(1)}, u32[]{:S(2)}, u32[]{:S(2)}) collective-permute-start(bf16[4,3,32,2048]{3,2,1,0:T(8,128)(2,1)S(1)} %collective-permute-done.4.refs_0_), channel_id=1, source_target_pairs={{0,32},{2,6},{4,36},{6,10},{8,40},{10,14},{12,44},{14,2},{1,33},{3... | collective-permute-start | bytes 4718600 | tf_op jit(solution)/shard_map/ppermute | solution.py:321
  82.9 1.5 %collective-permute-start.17 = (bf16[4,3,32,2048]{3,2,1,0:T(8,128)(2,1)S(1)}, bf16[4,3,32,2048]{3,2,1,0:T(8,128)(2,1)S(1)}, u32[]{:S(2)}, u32[]{:S(2)}) collective-permute-start(bf16[4,3,32,2048]{3,2,1,0:T(8,128)(2,1)S(1)} %collective-permute-done.13.refs_0_), channel_id=1, source_target_pairs={{0,96},{2,14},{4,100},{6,2},{8,104},{10,6},{12,108},{14,10},{1,97}... | collective-permute-start | bytes 4718600 | tf_op jit(solution)/shard_map/ppermute | solution.py:321
  84.3 5.2 %collide.10.refs_2_ = f32[3,448,2048]{2,1,0:T(8,128)S(1)} custom-call(f32[3]{0:T(128)S(1)} %copy-done.3, s32[2,3]{1,0:T(2,128)S(1)} %bitcast.22, bf16[2,448,2048]{2,1,0:T(8,128)(2,1)S(1)} %bitcast.10, bf16[4,3,32,2048]{3,2,1,0:T(8,128)(2,1)S(1)} %collective-permute-done.13.refs_0_, ...), custom_call_target="tpu_custom_call", output_to_operand_aliasing={{}: (5, {})} | custom-call | flops 3288334336 | bytes 6815744 | tf_op jit(solution)/shard_map/collide/pallas_call | solution.py:304
  89.5 5.2 %collide.11.refs_2_ = f32[3,448,2048]{2,1,0:T(8,128)S(1)} custom-call(f32[3]{0:T(128)S(1)} %copy-done.3, s32[2,3]{1,0:T(2,128)S(1)} %bitcast.23, bf16[2,448,2048]{2,1,0:T(8,128)(2,1)S(1)} %bitcast.11, bf16[4,3,32,2048]{3,2,1,0:T(8,128)(2,1)S(1)} %collective-permute-done.18.refs_0_, ...), custom_call_target="tpu_custom_call", output_to_operand_aliasing={{}: (5, {})} | custom-call | flops 3288334336 | bytes 6815744 | tf_op jit(solution)/shard_map/collide/pallas_call | solution.py:304
  94.7 7.7 %collective-permute-done.12.refs_0_ = bf16[4,3,32,2048]{3,2,1,0:T(8,128)(2,1)S(1)} collective-permute-done((bf16[4,3,32,2048]{3,2,1,0:T(8,128)(2,1)S(1)}, bf16[4,3,32,2048]{3,2,1,0:T(8,128)(2,1)S(1)}, u32[]{:S(2)}, u32[]{:S(2)}) %collective-permute-start.12) | collective-permute-done | bytes 1572896 | tf_op jit(solution)/shard_map/ppermute | solution.py:321
  102.4 1.4 %collective-permute-start.20 = (bf16[4,3,32,2048]{3,2,1,0:T(8,128)(2,1)S(1)}, bf16[4,3,32,2048]{3,2,1,0:T(8,128)(2,1)S(1)}, u32[]{:S(2)}, u32[]{:S(2)}) collective-permute-start(bf16[4,3,32,2048]{3,2,1,0:T(8,128)(2,1)S(1)} %collective-permute-done.12.refs_0_), channel_id=1, source_target_pairs={{0,2},{2,0},{4,6},{6,4},{8,10},{10,8},{12,14},{14,12},{1,3},{3,1},... | collective-permute-start | bytes 4718600 | tf_op jit(solution)/shard_map/ppermute | solution.py:321
  103.8 0.0 collective-permute-start.21
  103.8 5.2 %collide.12.refs_2_ = f32[3,448,2048]{2,1,0:T(8,128)S(1)} custom-call(f32[3]{0:T(128)S(1)} %copy-done.3, s32[2,3]{1,0:T(2,128)S(1)} %bitcast.24, bf16[2,448,2048]{2,1,0:T(8,128)(2,1)S(1)} %bitcast.12, bf16[4,3,32,2048]{3,2,1,0:T(8,128)(2,1)S(1)} %collective-permute-done.12.refs_0_, ...), custom_call_target="tpu_custom_call", output_to_operand_aliasing={{}: (5, {})} | custom-call | flops 3288334336 | bytes 6815744 | tf_op jit(solution)/shard_map/collide/pallas_call | solution.py:304
  109.0 0.1 collective-permute-done.21.refs_1_
  109.1 5.7 %collide.13 = bf16[3,448,2048]{2,1,0:T(8,128)(2,1)} custom-call(f32[3]{0:T(128)S(1)} %copy-done.3, s32[2,3]{1,0:T(2,128)S(1)} %bitcast.25, bf16[2,448,2048]{2,1,0:T(8,128)(2,1)S(1)} %bitcast.13, bf16[4,3,32,2048]{3,2,1,0:T(8,128)(2,1)S(1)} %collective-permute-done.20.refs_0_, bf16[4,3,32,2048]{3,2,1,0:T(8,128)(2,1)S(1)} %collective-permute-done.21.refs_1_, ...), custom_call_target="tpu_custom_call" | custom-call | flops 3288334336 | bytes 6815744 | tf_op jit(solution)/shard_map/collide/pallas_call | solution.py:304
  (17 shorter events, 0.0 us)
Async XLA Ops:
  0.6 12.6 %collective-permute-start.6 = (bf16[1,3,32,2048]{3,2,1,0:T(8,128)(2,1)}, bf16[1,3,32,2048]{3,2,1,0:T(8,128)(2,1)S(1)}, u32[]{:S(2)}, u32[]{:S(2)}) collective-permute-start(bf16[1,3,32,2048]{3,2,1,0:T(8,128)(2,1)} %bitcast.14), channel_id=1, source_target_pairs={{0,17},{2,19},{4,21},{6,23},{8,25},{10,27},{12,29},{14,31},{1,16},... | collective-permute-start | bytes 1179656 | tf_op jit(solution)/shard_map/ppermute | solution.py:321
  4.3 10.5 %collective-permute-start.1 = (bf16[1,3,32,2048]{3,2,1,0:T(8,128)(2,1)}, bf16[1,3,32,2048]{3,2,1,0:T(8,128)(2,1)S(1)}, u32[]{:S(2)}, u32[]{:S(2)}) collective-permute-start(bf16[1,3,32,2048]{3,2,1,0:T(8,128)(2,1)} %bitcast.15), channel_id=1, source_target_pairs={{0,4},{2,34},{4,8},{6,38},{8,12},{10,42},{12,0},{14,46},{1,5},{3,3... | collective-permute-start | bytes 1179656 | tf_op jit(solution)/shard_map/ppermute | solution.py:321
  5.9 11.4 %collective-permute-start.2 = (bf16[1,3,32,2048]{3,2,1,0:T(8,128)(2,1)}, bf16[1,3,32,2048]{3,2,1,0:T(8,128)(2,1)S(1)}, u32[]{:S(2)}, u32[]{:S(2)}) collective-permute-start(bf16[1,3,32,2048]{3,2,1,0:T(8,128)(2,1)} %bitcast.16), channel_id=1, source_target_pairs={{0,12},{2,98},{4,0},{6,102},{8,4},{10,106},{12,8},{14,110},{1,13},... | collective-permute-start | bytes 1179656 | tf_op jit(solution)/shard_map/ppermute | solution.py:321
  8.0 11.2 %collective-permute-start.3 = (bf16[1,3,32,2048]{3,2,1,0:T(8,128)(2,1)}, bf16[1,3,32,2048]{3,2,1,0:T(8,128)(2,1)S(1)}, u32[]{:S(2)}, u32[]{:S(2)}) collective-permute-start(bf16[1,3,32,2048]{3,2,1,0:T(8,128)(2,1)} %bitcast.17), channel_id=1, source_target_pairs={{0,8},{2,66},{4,12},{6,70},{8,0},{10,74},{12,4},{14,78},{1,9},{3,6... | collective-permute-start | bytes 1179656 | tf_op jit(solution)/shard_map/ppermute | solution.py:321
  9.3 9.9 %copy-start = (bf16[3,32,2048]{2,1,0:T(8,128)(2,1)S(1)}, bf16[3,32,2048]{2,1,0:T(8,128)(2,1)}, u32[]{:S(2)}) copy-start(bf16[3,32,2048]{2,1,0:T(8,128)(2,1)} %param.9) | copy-start | bytes 1179652
  11.7 12.6 %copy-start.2 = (s32[28,16]{0,1:T(8,128)S(1)}, s32[28,16]{0,1:T(8,128)}, u32[]{:S(2)}) copy-start(s32[28,16]{0,1:T(8,128)} %param.7) | copy-start | bytes 5380
  11.8 12.6 %copy-start.4 = (f32[2048]{0:T(1024)S(1)}, f32[2048]{0:T(1024)}, u32[]{:S(2)}) copy-start(f32[2048]{0:T(1024)} %param.8) | copy-start | bytes 24580
  11.8 12.6 %collective-permute-start = (bf16[2,64,2048]{2,1,0:T(8,128)(2,1)S(1)}, bf16[2,64,2048]{2,1,0:T(8,128)(2,1)S(1)}, u32[]{:S(2)}, u32[]{:S(2)}) collective-permute-start(bf16[2,64,2048]{2,1,0:T(8,128)(2,1)S(1)} %packet.1), channel_id=1, source_target_pairs={{0,1},{2,3},{4,5},{6,7},{8,9},{10,11},{12,13},{14,15},{1,0},{3,2},... | collective-permute-start | bytes 1572872 | tf_op jit(solution)/shard_map/ppermute | solution.py:321
  13.2 19.4 %collective-permute-start.7 = (bf16[1,3,32,2048]{3,2,1,0:T(8,128)(2,1)S(1)}, bf16[1,3,32,2048]{3,2,1,0:T(8,128)(2,1)S(1)}, u32[]{:S(2)}, u32[]{:S(2)}) collective-permute-start(bf16[1,3,32,2048]{3,2,1,0:T(8,128)(2,1)S(1)} %collective-permute-done.6.refs_0_), channel_id=1, source_target_pairs={{0,4},{2,34},{4,8},{6,38},{8,12},{10,42},{12,0},{14,46},{1,5},{3,3... | collective-permute-start | bytes 1179656 | tf_op jit(solution)/shard_map/ppermute | solution.py:321
  14.7 17.8 %collective-permute-start.8 = (bf16[1,3,32,2048]{3,2,1,0:T(8,128)(2,1)S(1)}, bf16[1,3,32,2048]{3,2,1,0:T(8,128)(2,1)S(1)}, u32[]{:S(2)}, u32[]{:S(2)}) collective-permute-start(bf16[1,3,32,2048]{3,2,1,0:T(8,128)(2,1)S(1)} %collective-permute-done.6.refs_0_), channel_id=1, source_target_pairs={{0,12},{2,98},{4,0},{6,102},{8,4},{10,106},{12,8},{14,110},{1,13},... | collective-permute-start | bytes 1179656 | tf_op jit(solution)/shard_map/ppermute | solution.py:321
  17.3 15.3 %collective-permute-start.9 = (bf16[1,3,32,2048]{3,2,1,0:T(8,128)(2,1)S(1)}, bf16[1,3,32,2048]{3,2,1,0:T(8,128)(2,1)S(1)}, u32[]{:S(2)}, u32[]{:S(2)}) collective-permute-start(bf16[1,3,32,2048]{3,2,1,0:T(8,128)(2,1)S(1)} %collective-permute-done.6.refs_0_), channel_id=1, source_target_pairs={{0,8},{2,66},{4,12},{6,70},{8,0},{10,74},{12,4},{14,78},{1,9},{3,6... | collective-permute-start | bytes 1179656 | tf_op jit(solution)/shard_map/ppermute | solution.py:321
  19.3 17.9 %collective-permute-start.11 = (bf16[4,3,32,2048]{3,2,1,0:T(8,128)(2,1)S(1)}, bf16[4,3,32,2048]{3,2,1,0:T(8,128)(2,1)S(1)}, u32[]{:S(2)}, u32[]{:S(2)}) collective-permute-start(bf16[4,3,32,2048]{3,2,1,0:T(8,128)(2,1)S(1)} %join.2.refs_0_), channel_id=1, source_target_pairs={{0,2},{2,0},{4,6},{6,4},{8,10},{10,8},{12,14},{14,12},{1,3},{3,1},... | collective-permute-start | bytes 4718600 | tf_op jit(solution)/shard_map/ppermute | solution.py:321
  32.5 4.7 %copy-start.1 = (s32[3,2]{0,1:T(2,128)S(1)}, s32[3,2]{0,1:T(2,128)}, u32[]{:S(2)}) copy-start(s32[3,2]{0,1:T(2,128)} %param.10) | copy-start | bytes 76
  32.5 4.7 %copy-start.3 = (f32[3]{0:T(128)S(1)}, f32[3]{0:T(128)}, u32[]{:S(2)}) copy-start(f32[3]{0:T(128)} %freq_ref.13) | copy-start | bytes 40
  32.7 8.8 %collective-permute-start.10 = (bf16[4,3,32,2048]{3,2,1,0:T(8,128)(2,1)S(1)}, bf16[4,3,32,2048]{3,2,1,0:T(8,128)(2,1)S(1)}, u32[]{:S(2)}, u32[]{:S(2)}) collective-permute-start(bf16[4,3,32,2048]{3,2,1,0:T(8,128)(2,1)S(1)} %join.3.refs_0_), channel_id=1, source_target_pairs={{0,2},{2,0},{4,6},{6,4},{8,10},{10,8},{12,14},{14,12},{1,3},{3,1},... | collective-permute-start | bytes 4718600 | tf_op jit(solution)/shard_map/ppermute | solution.py:321
  34.6 20.8 %collective-permute-start.4 = (bf16[4,3,32,2048]{3,2,1,0:T(8,128)(2,1)S(1)}, bf16[4,3,32,2048]{3,2,1,0:T(8,128)(2,1)S(1)}, u32[]{:S(2)}, u32[]{:S(2)}) collective-permute-start(bf16[4,3,32,2048]{3,2,1,0:T(8,128)(2,1)S(1)} %join.2.refs_0_), channel_id=1, source_target_pairs={{0,32},{2,6},{4,36},{6,10},{8,40},{10,14},{12,44},{14,2},{1,33},{3... | collective-permute-start | bytes 4718600 | tf_op jit(solution)/shard_map/ppermute | solution.py:321
  35.8 19.6 %collective-permute-start.5 = (bf16[4,3,32,2048]{3,2,1,0:T(8,128)(2,1)S(1)}, bf16[4,3,32,2048]{3,2,1,0:T(8,128)(2,1)S(1)}, u32[]{:S(2)}, u32[]{:S(2)}) collective-permute-start(bf16[4,3,32,2048]{3,2,1,0:T(8,128)(2,1)S(1)} %join.2.refs_0_), channel_id=1, source_target_pairs={{0,96},{2,14},{4,100},{6,2},{8,104},{10,6},{12,108},{14,10},{1,97}... | collective-permute-start | bytes 4718600 | tf_op jit(solution)/shard_map/ppermute | solution.py:321
  55.3 4.0 %collective-permute-start.15 = (bf16[4,3,32,2048]{3,2,1,0:T(8,128)(2,1)S(1)}, bf16[4,3,32,2048]{3,2,1,0:T(8,128)(2,1)S(1)}, u32[]{:S(2)}, u32[]{:S(2)}) collective-permute-start(bf16[4,3,32,2048]{3,2,1,0:T(8,128)(2,1)S(1)} %collective-permute-done.4.refs_0_), channel_id=1, source_target_pairs={{0,2},{2,0},{4,6},{6,4},{8,10},{10,8},{12,14},{14,12},{1,3},{3,1},... | collective-permute-start | bytes 4718600 | tf_op jit(solution)/shard_map/ppermute | solution.py:321
  56.3 5.3 %collective-permute-start.16 = (bf16[4,3,32,2048]{3,2,1,0:T(8,128)(2,1)S(1)}, bf16[4,3,32,2048]{3,2,1,0:T(8,128)(2,1)S(1)}, u32[]{:S(2)}, u32[]{:S(2)}) collective-permute-start(bf16[4,3,32,2048]{3,2,1,0:T(8,128)(2,1)S(1)} %collective-permute-done.5.refs_2_), channel_id=1, source_target_pairs={{0,2},{2,0},{4,6},{6,4},{8,10},{10,8},{12,14},{14,12},{1,3},{3,1},... | collective-permute-start | bytes 4718600 | tf_op jit(solution)/shard_map/ppermute | solution.py:321
  56.3 19.7 %collective-permute-start.13 = (bf16[4,3,32,2048]{3,2,1,0:T(8,128)(2,1)S(1)}, bf16[4,3,32,2048]{3,2,1,0:T(8,128)(2,1)S(1)}, u32[]{:S(2)}, u32[]{:S(2)}) collective-permute-start(bf16[4,3,32,2048]{3,2,1,0:T(8,128)(2,1)S(1)} %join.3.refs_0_), channel_id=1, source_target_pairs={{0,96},{2,14},{4,100},{6,2},{8,104},{10,6},{12,108},{14,10},{1,97}... | collective-permute-start | bytes 4718600 | tf_op jit(solution)/shard_map/ppermute | solution.py:321
  58.6 20.8 %collective-permute-start.14 = (bf16[4,3,32,2048]{3,2,1,0:T(8,128)(2,1)S(1)}, bf16[4,3,32,2048]{3,2,1,0:T(8,128)(2,1)S(1)}, u32[]{:S(2)}, u32[]{:S(2)}) collective-permute-start(bf16[4,3,32,2048]{3,2,1,0:T(8,128)(2,1)S(1)} %join.3.refs_0_), channel_id=1, source_target_pairs={{0,32},{2,6},{4,36},{6,10},{8,40},{10,14},{12,44},{14,2},{1,33},{3... | collective-permute-start | bytes 4718600 | tf_op jit(solution)/shard_map/ppermute | solution.py:321
  79.3 10.2 %collective-permute-start.18 = (bf16[4,3,32,2048]{3,2,1,0:T(8,128)(2,1)S(1)}, bf16[4,3,32,2048]{3,2,1,0:T(8,128)(2,1)S(1)}, u32[]{:S(2)}, u32[]{:S(2)}) collective-permute-start(bf16[4,3,32,2048]{3,2,1,0:T(8,128)(2,1)S(1)} %collective-permute-done.13.refs_0_), channel_id=1, source_target_pairs={{0,2},{2,0},{4,6},{6,4},{8,10},{10,8},{12,14},{14,12},{1,3},{3,1},... | collective-permute-start | bytes 4718600 | tf_op jit(solution)/shard_map/ppermute | solution.py:321
  81.6 7.9 %collective-permute-start.19 = (bf16[4,3,32,2048]{3,2,1,0:T(8,128)(2,1)S(1)}, bf16[4,3,32,2048]{3,2,1,0:T(8,128)(2,1)S(1)}, u32[]{:S(2)}, u32[]{:S(2)}) collective-permute-start(bf16[4,3,32,2048]{3,2,1,0:T(8,128)(2,1)S(1)} %collective-permute-done.14.refs_1_), channel_id=1, source_target_pairs={{0,2},{2,0},{4,6},{6,4},{8,10},{10,8},{12,14},{14,12},{1,3},{3,1},... | collective-permute-start | bytes 4718600 | tf_op jit(solution)/shard_map/ppermute | solution.py:321
  81.7 20.8 %collective-permute-start.12 = (bf16[4,3,32,2048]{3,2,1,0:T(8,128)(2,1)S(1)}, bf16[4,3,32,2048]{3,2,1,0:T(8,128)(2,1)S(1)}, u32[]{:S(2)}, u32[]{:S(2)}) collective-permute-start(bf16[4,3,32,2048]{3,2,1,0:T(8,128)(2,1)S(1)} %collective-permute-done.4.refs_0_), channel_id=1, source_target_pairs={{0,32},{2,6},{4,36},{6,10},{8,40},{10,14},{12,44},{14,2},{1,33},{3... | collective-permute-start | bytes 4718600 | tf_op jit(solution)/shard_map/ppermute | solution.py:321
  82.9 19.6 %collective-permute-start.17 = (bf16[4,3,32,2048]{3,2,1,0:T(8,128)(2,1)S(1)}, bf16[4,3,32,2048]{3,2,1,0:T(8,128)(2,1)S(1)}, u32[]{:S(2)}, u32[]{:S(2)}) collective-permute-start(bf16[4,3,32,2048]{3,2,1,0:T(8,128)(2,1)S(1)} %collective-permute-done.13.refs_0_), channel_id=1, source_target_pairs={{0,96},{2,14},{4,100},{6,2},{8,104},{10,6},{12,108},{14,10},{1,97}... | collective-permute-start | bytes 4718600 | tf_op jit(solution)/shard_map/ppermute | solution.py:321
  102.4 6.5 %collective-permute-start.20 = (bf16[4,3,32,2048]{3,2,1,0:T(8,128)(2,1)S(1)}, bf16[4,3,32,2048]{3,2,1,0:T(8,128)(2,1)S(1)}, u32[]{:S(2)}, u32[]{:S(2)}) collective-permute-start(bf16[4,3,32,2048]{3,2,1,0:T(8,128)(2,1)S(1)} %collective-permute-done.12.refs_0_), channel_id=1, source_target_pairs={{0,2},{2,0},{4,6},{6,4},{8,10},{10,8},{12,14},{14,12},{1,3},{3,1},... | collective-permute-start | bytes 4718600 | tf_op jit(solution)/shard_map/ppermute | solution.py:321
  103.8 5.3 %collective-permute-start.21 = (bf16[4,3,32,2048]{3,2,1,0:T(8,128)(2,1)S(1)}, bf16[4,3,32,2048]{3,2,1,0:T(8,128)(2,1)S(1)}, u32[]{:S(2)}, u32[]{:S(2)}) collective-permute-start(bf16[4,3,32,2048]{3,2,1,0:T(8,128)(2,1)S(1)} %collective-permute-done.17.refs_1_), channel_id=1, source_target_pairs={{0,2},{2,0},{4,6},{6,4},{8,10},{10,8},{12,14},{14,12},{1,3},{3,1},... | collective-permute-start | bytes 4718600 | tf_op jit(solution)/shard_map/ppermute | solution.py:321

commit v2 on v1

--- a/solution.py
+++ b/solution.py
@@ -102,7 +102,7 @@
     )(where, stay(signs), stay(cells))
 
 
-CHUNKS = 4
+CHUNKS = 7
 
 
 def transport_kernel(
@@ -160,9 +160,10 @@
     def one(l, carry):
         d0, d1, df = dirs[l, 0], dirs[l, 1], dirs[l, 2]
         p0, p1, pf = d0 > 0, d1 > 0, df > 0
+        h0, h1 = jnp.where(p0, 0.5, -0.5), jnp.where(p1, 0.5, -0.5)
         for c in range(coeffs // 128):
             at = slice(c * 128, (c + 1) * 128)
-            speed = jnp.broadcast_to(speed_ref[:, at], (8, 128))
+            speed = courant * jnp.broadcast_to(speed_ref[:, at], (8, 128))
             v0, v1, vf = d0 * speed, d1 * speed, df * speed
             for s in range(species):
                 f = cells_ref[s, l, :, at].astype(jnp.float32)
@@ -174,20 +175,21 @@
                 b0, b1 = down(f0, f1, left)
                 n0, n1 = a0 - f0, a1 - f1
                 m0, m1 = up(n0, n1, diff)
-                upper0, upper1 = f0 + 0.5 * (f0 - b0), f1 + 0.5 * (f1 - b1)
-                lower0, lower1 = a0 - 0.5 * m0, a1 - 0.5 * m1
-                flux0 = v0 * jnp.where(p0, upper0, lower0)
-                flux1 = v1 * jnp.where(p1, upper1, lower1)
+                flux0 = v0 * (jnp.where(p0, f0, a0) + h0 * jnp.where(p0, f0 - b0, m0))
+                flux1 = v1 * (jnp.where(p1, f1, a1) + h1 * jnp.where(p1, f1 - b1, m1))
                 first = vf * jnp.where(pf, ext, f0 - 0.5 * n0)
                 g0, g1 = down(flux0, flux1, first)
-                new = jnp.concatenate([f0 - courant * (flux0 - g0), f1 - courant * (flux1 - g1)], axis=0)
+                new = jnp.concatenate([f0 - (flux0 - g0), f1 - (flux1 - g1)], axis=0)
                 out_ref[s, l, :, at] = new.astype(jnp.bfloat16)
         return carry
 
-    for c in range(CHUNKS):
+    def part(c, carry):
         arriving(c).wait()
         lax.fori_loop(c * chunk, (c + 1) * chunk, one, 0)
         leaving(c).start()
+        return carry
+
+    lax.fori_loop(0, CHUNKS, part, 0)
     for c in range(CHUNKS):
         leaving(c).wait()
 
@@ -234,79 +236,69 @@
     )(*parts)
 
 
-def collide_kernel(count, first, last, freq_ref, pair_ref, adv_ref, *refs):
+def collide_kernel(units, first, last, freq_ref, pair_ref, adv_ref, *refs):
+    count = sum(units)
     groups, refs = refs[:count], refs[count:]
     acc_ref, refs = (None, refs) if first else (refs[0], refs[1:])
     out_ref = refs[0]
-    species, rows, coeffs = adv_ref.shape
+    species, _, coeffs = adv_ref.shape
     pair_count = out_ref.shape[0]
-    blocks = 2 if last else 1
-    block = rows // blocks
     nt = (((1,), (1,)), ((), ()))
-
-    def leaving(i, p):
+    ends = [sum(units[: k + 1]) for k in range(len(units))]
+    held = [groups[end - n : end] for n, end in zip(units, ends)]
+
+    def leaving(p):
         staged, out_sem = refs[1:]
-        at = pl.ds(pl.multiple_of(i * block, block), block)
-        return pltpu.make_async_copy(staged.at[p, at, :], out_ref.at[p, at, :], out_sem.at[i, p])
-
-    def part(g, which):
-        return groups[g][:, which].reshape(-1, coeffs)
-
-    for t in range(count // 2):
-        mine, other = 2 * t, 2 * t + 1
-
-        def step(i, carry, t=t, mine=mine, other=other):
-            at = pl.ds(pl.multiple_of(i * block, block), block)
-            a = adv_ref[:, at, :].reshape(species * block, coeffs)
-            lefts, rights = [], []
-            for g in (mine, other):
-                w = jnp.concatenate([part(g, 0), part(g, 1)], axis=0)
-                both = lax.dot_general(a, w, nt, preferred_element_type=jnp.float32)
-                n = both.shape[1] // 2
-                lefts.append(both[:, :n])
-                rights.append(both[:, n:])
-            left = jnp.concatenate(lefts, axis=1)
-            right = jnp.concatenate(rights, axis=1)
-            down = jnp.concatenate([part(mine, 2), part(other, 2)], axis=0)
-            for p in range(pair_count):
-                lp = jnp.where(pair_ref[0, p] == 1, left[block:], left[:block])
-                rp = jnp.where(pair_ref[1, p] == 1, right[block:], right[:block])
-                product = (freq_ref[p] * lp * rp).astype(jnp.bfloat16)
-                term = jnp.dot(product, down, preferred_element_type=jnp.float32)
-                if last:
-                    refs[1][p, at, :] = (acc_ref[p, at, :] + term).astype(jnp.bfloat16)
-                    leaving(i, p).start()
-                    continue
-                if t > 0:
-                    term = out_ref[p, at, :] + term
-                elif not first:
-                    term = acc_ref[p, at, :] + term
-                out_ref[p, at, :] = term
-            return carry
-
-        lax.fori_loop(0, blocks, step, 0)
+        return pltpu.make_async_copy(staged.at[p], out_ref.at[p], out_sem.at[p])
+
+    def ranks_of(arrays, which):
+        return jnp.concatenate([ref[:, which].reshape(-1, coeffs) for ref in arrays], axis=0)
+
+    left, right = [], []
+    for s in range(species):
+        both = [
+            lax.dot_general(
+                adv_ref[s],
+                jnp.concatenate([ranks_of(h, 0), ranks_of(h, 1)], axis=0),
+                nt,
+                preferred_element_type=jnp.float32,
+            )
+            for h in held
+        ]
+        half = both[0].shape[1] // 2
+        left.append(jnp.concatenate([b[:, :half] for b in both], axis=1))
+        right.append(jnp.concatenate([b[:, half:] for b in both], axis=1))
+    down = jnp.concatenate([ranks_of(h, 2) for h in held], axis=0)
+    for p in range(pair_count):
+        lp = jnp.where(pair_ref[0, p] == 1, left[1], left[0])
+        rp = jnp.where(pair_ref[1, p] == 1, right[1], right[0])
+        product = (freq_ref[p] * lp * rp).astype(jnp.bfloat16)
+        term = jnp.dot(product, down, preferred_element_type=jnp.float32)
+        if not first:
+            term = (acc_ref if last else out_ref)[p] + term
+        if last:
+            refs[1][p] = term.astype(jnp.bfloat16)
+            leaving(p).start()
+        else:
+            out_ref[p] = term
     if last:
-        for i in range(blocks):
-            for p in range(pair_count):
-                leaving(i, p).wait()
-
-
-def collide(adv, frequency, pairs, groups, acc, last=False):
+        for p in range(pair_count):
+            leaving(p).wait()
+
+
+def collide(adv, frequency, pairs, held, acc, last=False):
     species, rows, coeffs = adv.shape
     pair_count = pairs.shape[1]
+    groups = [array for unit in held for array in unit]
     ranks = sum(a.shape[0] * a.shape[2] for a in groups)
-    assert not last or len(groups) == 2
     shape = (pair_count, rows, coeffs)
     operands = [frequency, pairs, adv] + groups + ([] if acc is None else [acc])
-    scratch = []
-    if last:
-        scratch = [pltpu.VMEM(shape, jnp.bfloat16), DMA((2, pair_count))]
     return pl.pallas_call(
-        functools.partial(collide_kernel, len(groups), acc is None, last),
+        functools.partial(collide_kernel, [len(unit) for unit in held], acc is None, last),
         in_specs=[SMEM, SMEM] + [VMEM] * (len(operands) - 2),
         out_specs=HBM if last else VMEM,
         out_shape=jax.ShapeDtypeStruct(shape, jnp.bfloat16) if last else pltpu.VMEM(shape, jnp.float32),
-        scratch_shapes=scratch,
+        scratch_shapes=[pltpu.VMEM(shape, jnp.bfloat16), DMA((pair_count,))] if last else [],
         input_output_aliases={} if acc is None or last else {len(operands) - 1: 0},
         cost_estimate=cost(
             2 * ranks * coeffs * rows * (2 * species + pair_count),
@@ -322,7 +314,16 @@
 
 
 def phase(mine):
-    return [mine, send(mine, UP1), send(mine, DOWN1), send(mine, FAR1)]
+    return [mine, send(mine, UP1), send(mine, DOWN1)]
+
+
+def relay(up, down):
+    half = up.shape[0] // 2
+    return [send(up[:half], UP2), send(down[half:], DOWN2)]
+
+
+def swap(arrays):
+    return [send(array, PARTNER) for array in arrays]
 
 
 def after(array, *others):
@@ -336,40 +337,43 @@
     signs, pairs = face_signs.T, pair_list.T
 
     cross = send(mine, CROSS)
-    parts_o = phase(mine)
-    parts_c = phase(cross)
+    parts_o = phase(mine) + [send(mine, FAR1)]
+    parts_c = phase(cross) + [send(parts_o[3], CROSS)]
     packet = packet_of(distribution, signs, here)
     got = send(packet, SIDE)
     parts_o[0] = after(mine, packet)
     group_o = join(parts_o)
     up_o, down_o = send(group_o, UP2), send(group_o, DOWN2)
-    swap_o = send(group_o, PARTNER)
+    swap_o = swap([group_o])
     adv_near, advanced = transport(distribution, got, signs, stream_speed[None], here)
     parts_c[0] = after(parts_c[0], adv_near)
     group_c = join(parts_c)
     up_c, down_c = send(group_c, UP2), send(group_c, DOWN2)
-    swap_c = send(group_c, PARTNER)
+    swap_c = swap([group_c])
 
     adv = adv_near.reshape(species, lines * cells, coeffs)
 
-    def step(groups, acc, last=False):
-        return collide(adv, frequency, pairs, groups, acc, last)
-
-    acc = step([after(group_o, group_c), swap_o], None)
-    acc = step([group_c, swap_c], acc)
+    def step(held, acc, last=False):
+        return collide(adv, frequency, pairs, held, acc, last)
+
+    acc = step([[after(group_o, group_c)], swap_o], None)
+    acc = step([[group_c], swap_c], acc)
     up_o, down_o, _ = lax.optimization_barrier((up_o, down_o, acc))
-    far_o = send(up_o, UP2)
-    swap_uo, swap_do = send(up_o, PARTNER), send(down_o, PARTNER)
-    acc = step([up_o, swap_uo, down_o, swap_do], acc)
+    far_o = relay(up_o, down_o)
+    swap_uo, swap_do = swap([up_o]), swap([down_o])
+    acc = step([[up_o], [down_o]], acc)
+    acc = step([swap_uo, swap_do], acc)
     down_c, up_c, _ = lax.optimization_barrier((down_c, up_c, acc))
-    far_c = send(down_c, DOWN2)
-    swap_dc, swap_uc = send(down_c, PARTNER), send(up_c, PARTNER)
-    acc = step([down_c, up_c], acc)
+    far_c = relay(up_c, down_c)
+    swap_dc, swap_uc = swap([down_c]), swap([up_c])
+    acc = step([[down_c], [up_c]], acc)
+    *far_o, _ = lax.optimization_barrier((*far_o, acc))
+    swap_fo = swap(far_o)
     acc = step([swap_dc, swap_uc], acc)
-    far_o, far_c, _ = lax.optimization_barrier((far_o, far_c, acc))
-    swap_fo, swap_fc = send(far_o, PARTNER), send(far_c, PARTNER)
-    acc = step([far_o, far_c], acc)
-    out = step([swap_fo, swap_fc], acc, last=True)
+    *far_c, _ = lax.optimization_barrier((*far_c, acc))
+    swap_fc = swap(far_c)
+    acc = step([far_o, swap_fo], acc)
+    out = step([far_c, swap_fc], acc, last=True)
     collision = out.reshape(pair_list.shape[0], lines, cells, coeffs)
     return (advanced, collision)
 

time: 115 us -> 119 us (1.035)
  starting transfers between devices: 29 us -> 33.4 us
  Pallas kernels: 49.8 us -> 46 us
  waiting for transfers between devices: 35.2 us -> 37.7 us
    ppermute x22 -> x26, starting transfers between devices: 29 us -> 33.4 us  [send(): return lax.ppermute(array, AXES, pairs)]
    pallas_call x7 -> x8, Pallas kernels: 39 us -> 35.8 us  [collide(): pl.pallas_call(functools.partial(collide_kernel, [len(unit) for unit in h...]
    ppermute x22 -> x26, waiting for transfers between devices: 35.2 us -> 37.7 us  [send(): return lax.ppermute(array, AXES, pairs)]
  transfers between devices with their start and end apart: 22 -> 26, of which waited for: 10 -> 8; matrix products, arithmetic and copies ran while one was open for 0% -> 0% of each run, Pallas kernels for 38% -> 34%
where the time goes in v2:
time: 119 us; the launch traced here: 118 us
  Pallas kernels  46 us (39%)
  waiting for transfers between devices  37.7 us (32%)
  starting transfers between devices  33.4 us (28%)
    ppermute x26, waiting for transfers between devices, send(): return lax.ppermute(array, AXES, pairs)  37.7 us
    pallas_call x8, Pallas kernels, collide(): pl.pallas_call(functools.partial(collide_kernel, [len(unit) for unit in h...  35.8 us
    ppermute x26, starting transfers between devices, send(): return lax.ppermute(array, AXES, pairs)  33.4 us
    pallas_call x1, Pallas kernels, transport(): pl.pallas_call(transport_kernel, in_specs=[SMEM, VMEM, VMEM, VMEM, HBM],...  7.51 us
    pallas_call x1, Pallas kernels, packet_of(): pl.pallas_call(packet_kernel, in_specs=[SMEM, HBM, HBM], out_specs=VMEM,...  2.4 us
  transfers between devices with their start and end apart: 26, of which 8 were waited for; matrix products, arithmetic and copies ran while one was open for 0% of the time, Pallas kernels for 34%

profile of v2, /device:TPU:1, one launch (start us, length us, event | category | flops | bytes accessed | tf_op | source)
XLA Modules:
  0.0 118.4 jit_solution(7909559902901330180)
XLA Ops:
  0.6 3.6 %collective-permute-start.1 = (bf16[1,3,32,2048]{3,2,1,0:T(8,128)(2,1)}, bf16[1,3,32,2048]{3,2,1,0:T(8,128)(2,1)S(1)}, u32[]{:S(2)}, u32[]{:S(2)}) collective-permute-start(bf16[1,3,32,2048]{3,2,1,0:T(8,128)(2,1)} %bitcast.15), channel_id=1, source_target_pairs={{0,17},{2,19},{4,21},{6,23},{8,25},{10,27},{12,29},{14,31},{1,16},... | collective-permute-start | bytes 1179656 | tf_op jit(solution)/shard_map/ppermute | solution.py:313
  4.3 3.6 %collective-permute-start.4 = (bf16[1,3,32,2048]{3,2,1,0:T(8,128)(2,1)}, bf16[1,3,32,2048]{3,2,1,0:T(8,128)(2,1)S(1)}, u32[]{:S(2)}, u32[]{:S(2)}) collective-permute-start(bf16[1,3,32,2048]{3,2,1,0:T(8,128)(2,1)} %bitcast.16), channel_id=1, source_target_pairs={{0,8},{2,66},{4,12},{6,70},{8,0},{10,74},{12,4},{14,78},{1,9},{3,6... | collective-permute-start | bytes 1179656 | tf_op jit(solution)/shard_map/ppermute | solution.py:313
  7.9 0.7 collective-permute-start.8
  8.6 1.9 %collective-permute-start.9 = (bf16[1,3,32,2048]{3,2,1,0:T(8,128)(2,1)}, bf16[1,3,32,2048]{3,2,1,0:T(8,128)(2,1)S(1)}, u32[]{:S(2)}, u32[]{:S(2)}) collective-permute-start(bf16[1,3,32,2048]{3,2,1,0:T(8,128)(2,1)} %bitcast.18), channel_id=1, source_target_pairs={{0,12},{2,98},{4,0},{6,102},{8,4},{10,106},{12,8},{14,110},{1,13},... | collective-permute-start | bytes 1179656 | tf_op jit(solution)/shard_map/ppermute | solution.py:313
  10.5 2.4 %packet.1 = bf16[2,64,2048]{2,1,0:T(8,128)(2,1)S(1)} custom-call(s32[1]{0:T(128)} %bitcast.where_ref, s32[16,28]{1,0:T(8,128)} %bitcast.28, bf16[2,28,16,2048]{3,2,1,0:T(8,128)(2,1)} %cells_hbm.1), custom_call_target="tpu_custom_call" | custom-call | flops 1835008 | bytes 1835008 | tf_op jit(solution)/shard_map/packet/pallas_call | solution.py:87
  12.9 0.0 copy-start.3
  13.0 0.0 copy-start.4
  13.0 0.1 collective-permute-start
  13.1 0.1 collective-permute-done.1.refs_0_
  13.2 1.5 %collective-permute-start.2 = (bf16[1,3,32,2048]{3,2,1,0:T(8,128)(2,1)S(1)}, bf16[1,3,32,2048]{3,2,1,0:T(8,128)(2,1)S(1)}, u32[]{:S(2)}, u32[]{:S(2)}) collective-permute-start(bf16[1,3,32,2048]{3,2,1,0:T(8,128)(2,1)S(1)} %collective-permute-done.1.refs_0_), channel_id=1, source_target_pairs={{0,4},{2,34},{4,8},{6,38},{8,12},{10,42},{12,0},{14,46},{1,5},{3,3... | collective-permute-start | bytes 1179656 | tf_op jit(solution)/shard_map/ppermute | solution.py:313
  14.7 2.1 %collective-permute-start.3 = (bf16[1,3,32,2048]{3,2,1,0:T(8,128)(2,1)S(1)}, bf16[1,3,32,2048]{3,2,1,0:T(8,128)(2,1)S(1)}, u32[]{:S(2)}, u32[]{:S(2)}) collective-permute-start(bf16[1,3,32,2048]{3,2,1,0:T(8,128)(2,1)S(1)} %collective-permute-done.1.refs_0_), channel_id=1, source_target_pairs={{0,12},{2,98},{4,0},{6,102},{8,4},{10,106},{12,8},{14,110},{1,13},... | collective-permute-start | bytes 1179656 | tf_op jit(solution)/shard_map/ppermute | solution.py:313
  16.8 0.9 collective-permute-done.8.refs_1_
  17.8 1.7 %collective-permute-start.5 = (bf16[1,3,32,2048]{3,2,1,0:T(8,128)(2,1)S(1)}, bf16[1,3,32,2048]{3,2,1,0:T(8,128)(2,1)S(1)}, u32[]{:S(2)}, u32[]{:S(2)}) collective-permute-start(bf16[1,3,32,2048]{3,2,1,0:T(8,128)(2,1)S(1)} %collective-permute-done.4.refs_3_), channel_id=1, source_target_pairs={{0,17},{2,19},{4,21},{6,23},{8,25},{10,27},{12,29},{14,31},{1,16},... | collective-permute-start | bytes 1179656 | tf_op jit(solution)/shard_map/ppermute | solution.py:313
  19.5 0.1 join.3.refs_0_
  19.6 1.4 %collective-permute-start.13 = (bf16[4,3,32,2048]{3,2,1,0:T(8,128)(2,1)S(1)}, bf16[4,3,32,2048]{3,2,1,0:T(8,128)(2,1)S(1)}, u32[]{:S(2)}, u32[]{:S(2)}) collective-permute-start(bf16[4,3,32,2048]{3,2,1,0:T(8,128)(2,1)S(1)} %join.3.refs_0_), channel_id=1, source_target_pairs={{0,2},{2,0},{4,6},{6,4},{8,10},{10,8},{12,14},{14,12},{1,3},{3,1},... | collective-permute-start | bytes 4718600 | tf_op jit(solution)/shard_map/ppermute | solution.py:313
  20.9 4.7 %collective-permute-done.packet_ref = bf16[2,64,2048]{2,1,0:T(8,128)(2,1)S(1)} collective-permute-done((bf16[2,64,2048]{2,1,0:T(8,128)(2,1)S(1)}, bf16[2,64,2048]{2,1,0:T(8,128)(2,1)S(1)}, u32[]{:S(2)}, u32[]{:S(2)}) %collective-permute-start) | collective-permute-done | bytes 524320 | tf_op jit(solution)/shard_map/ppermute | solution.py:313
  25.6 7.5 %transport.1 = (bf16[2,28,16,2048]{3,2,1,0:T(8,128)(2,1)S(1)}, bf16[2,28,16,2048]{3,2,1,0:T(8,128)(2,1)}) custom-call(s32[1]{0:T(128)} %bitcast.where_ref, f32[1,2048]{1,0:T(1,128)S(1)} %bitcast.30, s32[16,28]{1,0:T(8,128)S(1)} %bitcast.29, bf16[2,64,2048]{2,1,0:T(8,128)(2,1)S(1)} %collective-permute-done.packet_ref, bf16[2,28,16,2048]{3,2,1,0:T(8,128)(2,1)} %cells_hbm.1), custom_call_target="tpu_custom_call" | custom-call | flops 55050240 | bytes 7340032 | tf_op jit(solution)/shard_map/transport/pallas_call | solution.py:199
  33.1 0.0 copy-start.2
  33.2 0.1 join.2.refs_0_
  33.3 1.9 %collective-permute-start.12 = (bf16[4,3,32,2048]{3,2,1,0:T(8,128)(2,1)S(1)}, bf16[4,3,32,2048]{3,2,1,0:T(8,128)(2,1)S(1)}, u32[]{:S(2)}, u32[]{:S(2)}) collective-permute-start(bf16[4,3,32,2048]{3,2,1,0:T(8,128)(2,1)S(1)} %join.2.refs_0_), channel_id=1, source_target_pairs={{0,2},{2,0},{4,6},{6,4},{8,10},{10,8},{12,14},{14,12},{1,3},{3,1},... | collective-permute-start | bytes 4718600 | tf_op jit(solution)/shard_map/ppermute | solution.py:313
  35.2 0.2 collective-permute-start.10
  35.4 2.5 %collective-permute-start.11 = (bf16[4,3,32,2048]{3,2,1,0:T(8,128)(2,1)S(1)}, bf16[4,3,32,2048]{3,2,1,0:T(8,128)(2,1)S(1)}, u32[]{:S(2)}, u32[]{:S(2)}) collective-permute-start(bf16[4,3,32,2048]{3,2,1,0:T(8,128)(2,1)S(1)} %join.3.refs_0_), channel_id=1, source_target_pairs={{0,96},{2,14},{4,100},{6,2},{8,104},{10,6},{12,108},{14,10},{1,97}... | collective-permute-start | bytes 4718600 | tf_op jit(solution)/shard_map/ppermute | solution.py:313
  37.9 4.2 %collide.8.refs_2_ = f32[3,448,2048]{2,1,0:T(8,128)S(1)} custom-call(f32[3]{0:T(128)S(1)} %copy-done.2, s32[2,3]{1,0:T(2,128)S(1)} %bitcast.20, bf16[2,448,2048]{2,1,0:T(8,128)(2,1)S(1)} %bitcast.7, bf16[4,3,32,2048]{3,2,1,0:T(8,128)(2,1)S(1)} %join.3.refs_0_, bf16[4,3,32,2048]{3,2,1,0:T(8,128)(2,1)S(1)} %collective-permute-done.13.refs_1_), custom_call_target="tpu_custom_call" | custom-call | flops 3288334336 | bytes 6815744 | tf_op jit(solution)/shard_map/collide/pallas_call | solution.py:296
  42.1 4.3 %collide.9.refs_2_ = f32[3,448,2048]{2,1,0:T(8,128)S(1)} custom-call(f32[3]{0:T(128)S(1)} %copy-done.2, s32[2,3]{1,0:T(2,128)S(1)} %bitcast.21, bf16[2,448,2048]{2,1,0:T(8,128)(2,1)S(1)} %bitcast.8, bf16[4,3,32,2048]{3,2,1,0:T(8,128)(2,1)S(1)} %join.2.refs_0_, ...), custom_call_target="tpu_custom_call", output_to_operand_aliasing={{}: (5, {})} | custom-call | flops 3288334336 | bytes 6815744 | tf_op jit(solution)/shard_map/collide/pallas_call | solution.py:296
  46.4 9.5 %collective-permute-done.10.refs_0_ = bf16[4,3,32,2048]{3,2,1,0:T(8,128)(2,1)S(1)} collective-permute-done((bf16[4,3,32,2048]{3,2,1,0:T(8,128)(2,1)S(1)}, bf16[4,3,32,2048]{3,2,1,0:T(8,128)(2,1)S(1)}, u32[]{:S(2)}, u32[]{:S(2)}) %collective-permute-start.10) | collective-permute-done | bytes 1572896 | tf_op jit(solution)/shard_map/ppermute | solution.py:313
  55.9 0.9 collective-permute-start.14
  56.9 1.9 %collective-permute-start.6 = (bf16[4,3,32,2048]{3,2,1,0:T(8,128)(2,1)S(1)}, bf16[4,3,32,2048]{3,2,1,0:T(8,128)(2,1)S(1)}, u32[]{:S(2)}, u32[]{:S(2)}) collective-permute-start(bf16[4,3,32,2048]{3,2,1,0:T(8,128)(2,1)S(1)} %join.2.refs_0_), channel_id=1, source_target_pairs={{0,96},{2,14},{4,100},{6,2},{8,104},{10,6},{12,108},{14,10},{1,97}... | collective-permute-start | bytes 4718600 | tf_op jit(solution)/shard_map/ppermute | solution.py:313
  58.8 4.3 %collide.10.refs_2_ = f32[3,448,2048]{2,1,0:T(8,128)S(1)} custom-call(f32[3]{0:T(128)S(1)} %copy-done.2, s32[2,3]{1,0:T(2,128)S(1)} %bitcast.22, bf16[2,448,2048]{2,1,0:T(8,128)(2,1)S(1)} %bitcast.9, bf16[4,3,32,2048]{3,2,1,0:T(8,128)(2,1)S(1)} %collective-permute-done.10.refs_0_, ...), custom_call_target="tpu_custom_call", output_to_operand_aliasing={{}: (5, {})} | custom-call | flops 3288334336 | bytes 6815744 | tf_op jit(solution)/shard_map/collide/pallas_call | solution.py:296
  63.2 4.3 %collide.11.refs_2_ = f32[3,448,2048]{2,1,0:T(8,128)S(1)} custom-call(f32[3]{0:T(128)S(1)} %copy-done.2, s32[2,3]{1,0:T(2,128)S(1)} %bitcast.23, bf16[2,448,2048]{2,1,0:T(8,128)(2,1)S(1)} %bitcast.10, bf16[4,3,32,2048]{3,2,1,0:T(8,128)(2,1)S(1)} %collective-permute-done.14.refs_0_, ...), custom_call_target="tpu_custom_call", output_to_operand_aliasing={{}: (5, {})} | custom-call | flops 3288334336 | bytes 6815744 | tf_op jit(solution)/shard_map/collide/pallas_call | solution.py:296
  67.5 8.9 %collective-permute-done.6.refs_0_ = bf16[4,3,32,2048]{3,2,1,0:T(8,128)(2,1)S(1)} collective-permute-done((bf16[4,3,32,2048]{3,2,1,0:T(8,128)(2,1)S(1)}, bf16[4,3,32,2048]{3,2,1,0:T(8,128)(2,1)S(1)}, u32[]{:S(2)}, u32[]{:S(2)}) %collective-permute-start.6) | collective-permute-done | bytes 1572896 | tf_op jit(solution)/shard_map/ppermute | solution.py:313
  76.4 3.2 %collective-permute-done.7.refs_1_ = bf16[4,3,32,2048]{3,2,1,0:T(8,128)(2,1)S(1)} collective-permute-done((bf16[4,3,32,2048]{3,2,1,0:T(8,128)(2,1)S(1)}, bf16[4,3,32,2048]{3,2,1,0:T(8,128)(2,1)S(1)}, u32[]{:S(2)}, u32[]{:S(2)}) %collective-permute-start.7) | collective-permute-done | bytes 1572896 | tf_op jit(solution)/shard_map/ppermute | solution.py:313
  79.6 2.6 %collective-permute-start.18 = (bf16[4,3,32,2048]{3,2,1,0:T(8,128)(2,1)S(1)}, bf16[4,3,32,2048]{3,2,1,0:T(8,128)(2,1)S(1)}, u32[]{:S(2)}, u32[]{:S(2)}) collective-permute-start(bf16[4,3,32,2048]{3,2,1,0:T(8,128)(2,1)S(1)} %collective-permute-done.6.refs_0_), channel_id=1, source_target_pairs={{0,2},{2,0},{4,6},{6,4},{8,10},{10,8},{12,14},{14,12},{1,3},{3,1},... | collective-permute-start | bytes 4718600 | tf_op jit(solution)/shard_map/ppermute | solution.py:313
  82.3 0.1 slice.14
  82.3 0.6 collective-permute-start.22
  82.9 0.1 slice.15
  83.0 2.2 %collective-permute-start.23 = (bf16[2,3,32,2048]{3,2,1,0:T(8,128)(2,1)S(1)}, bf16[2,3,32,2048]{3,2,1,0:T(8,128)(2,1)S(1)}, u32[]{:S(2)}, u32[]{:S(2)}) collective-permute-start(bf16[2,3,32,2048]{3,2,1,0:T(8,128)(2,1)S(1)} %slice.15), channel_id=1, source_target_pairs={{0,96},{2,14},{4,100},{6,2},{8,104},{10,6},{12,108},{14,10},{1,97}... | collective-permute-start | bytes 2359304 | tf_op jit(solution)/shard_map/ppermute | solution.py:313
  85.2 0.1 slice.12
  85.3 0.1 slice.13
  85.3 0.1 collective-permute-start.16
  85.4 9.3 %collective-permute-done.22.refs_0_ = bf16[2,3,32,2048]{3,2,1,0:T(8,128)(2,1)S(1)} collective-permute-done((bf16[2,3,32,2048]{3,2,1,0:T(8,128)(2,1)S(1)}, bf16[2,3,32,2048]{3,2,1,0:T(8,128)(2,1)S(1)}, u32[]{:S(2)}, u32[]{:S(2)}) %collective-permute-start.22) | collective-permute-done | bytes 786464 | tf_op jit(solution)/shard_map/ppermute | solution.py:313
  94.8 4.3 %collide.12.refs_2_ = f32[3,448,2048]{2,1,0:T(8,128)S(1)} custom-call(f32[3]{0:T(128)S(1)} %copy-done.2, s32[2,3]{1,0:T(2,128)S(1)} %bitcast.24, bf16[2,448,2048]{2,1,0:T(8,128)(2,1)S(1)} %bitcast.11, bf16[4,3,32,2048]{3,2,1,0:T(8,128)(2,1)S(1)} %collective-permute-done.6.refs_0_, ...), custom_call_target="tpu_custom_call", output_to_operand_aliasing={{}: (5, {})} | custom-call | flops 3288334336 | bytes 6815744 | tf_op jit(solution)/shard_map/collide/pallas_call | solution.py:296
  99.1 1.4 %collective-permute-start.24 = (bf16[2,3,32,2048]{3,2,1,0:T(8,128)(2,1)S(1)}, bf16[2,3,32,2048]{3,2,1,0:T(8,128)(2,1)S(1)}, u32[]{:S(2)}, u32[]{:S(2)}) collective-permute-start(bf16[2,3,32,2048]{3,2,1,0:T(8,128)(2,1)S(1)} %collective-permute-done.22.refs_0_), channel_id=1, source_target_pairs={{0,2},{2,0},{4,6},{6,4},{8,10},{10,8},{12,14},{14,12},{1,3},{3,1},... | collective-permute-start | bytes 2359304 | tf_op jit(solution)/shard_map/ppermute | solution.py:313
  100.5 0.1 collective-permute-start.25
  100.6 4.3 %collide.13.refs_4_ = f32[3,448,2048]{2,1,0:T(8,128)S(1)} custom-call(f32[3]{0:T(128)S(1)} %copy-done.2, s32[2,3]{1,0:T(2,128)S(1)} %bitcast.25, bf16[2,448,2048]{2,1,0:T(8,128)(2,1)S(1)} %bitcast.12, bf16[4,3,32,2048]{3,2,1,0:T(8,128)(2,1)S(1)} %collective-permute-done.18.refs_0_, ...), custom_call_target="tpu_custom_call", output_to_operand_aliasing={{}: (5, {})} | custom-call | flops 3288334336 | bytes 6815744 | tf_op jit(solution)/shard_map/collide/pallas_call | solution.py:296
  105.0 0.9 collective-permute-done.17.refs_1_
  105.9 2.2 %collective-permute-start.20 = (bf16[2,3,32,2048]{3,2,1,0:T(8,128)(2,1)S(1)}, bf16[2,3,32,2048]{3,2,1,0:T(8,128)(2,1)S(1)}, u32[]{:S(2)}, u32[]{:S(2)}) collective-permute-start(bf16[2,3,32,2048]{3,2,1,0:T(8,128)(2,1)S(1)} %collective-permute-done.16.refs_0_), channel_id=1, source_target_pairs={{0,2},{2,0},{4,6},{6,4},{8,10},{10,8},{12,14},{14,12},{1,3},{3,1},... | collective-permute-start | bytes 2359304 | tf_op jit(solution)/shard_map/ppermute | solution.py:313
  108.1 4.3 %collide.14.refs_4_ = f32[3,448,2048]{2,1,0:T(8,128)S(1)} custom-call(f32[3]{0:T(128)S(1)} %copy-done.2, s32[2,3]{1,0:T(2,128)S(1)} %bitcast.26, bf16[2,448,2048]{2,1,0:T(8,128)(2,1)S(1)} %bitcast.13, bf16[2,3,32,2048]{3,2,1,0:T(8,128)(2,1)S(1)} %collective-permute-done.22.refs_0_, ...), custom_call_target="tpu_custom_call", output_to_operand_aliasing={{}: (7, {})} | custom-call | flops 3288334336 | bytes 6815744 | tf_op jit(solution)/shard_map/collide/pallas_call | solution.py:296
  112.5 5.8 %collide.15 = bf16[3,448,2048]{2,1,0:T(8,128)(2,1)} custom-call(f32[3]{0:T(128)S(1)} %copy-done.2, s32[2,3]{1,0:T(2,128)S(1)} %bitcast.27, bf16[2,448,2048]{2,1,0:T(8,128)(2,1)S(1)} %bitcast.14, bf16[2,3,32,2048]{3,2,1,0:T(8,128)(2,1)S(1)} %collective-permute-done.16.refs_0_, bf16[2,3,32,2048]{3,2,1,0:T(8,128)(2,1)S(1)} %collective-permute-done.17.refs_1_, ...), custom_call_target="tpu_custom_call" | custom-call | flops 3288334336 | bytes 6815744 | tf_op jit(solution)/shard_map/collide/pallas_call | solution.py:296
  (30 shorter events, 0.1 us)
Async XLA Ops:
  0.6 12.6 %collective-permute-start.1 = (bf16[1,3,32,2048]{3,2,1,0:T(8,128)(2,1)}, bf16[1,3,32,2048]{3,2,1,0:T(8,128)(2,1)S(1)}, u32[]{:S(2)}, u32[]{:S(2)}) collective-permute-start(bf16[1,3,32,2048]{3,2,1,0:T(8,128)(2,1)} %bitcast.15), channel_id=1, source_target_pairs={{0,17},{2,19},{4,21},{6,23},{8,25},{10,27},{12,29},{14,31},{1,16},... | collective-permute-start | bytes 1179656 | tf_op jit(solution)/shard_map/ppermute | solution.py:313
  4.3 10.5 %collective-permute-start.4 = (bf16[1,3,32,2048]{3,2,1,0:T(8,128)(2,1)}, bf16[1,3,32,2048]{3,2,1,0:T(8,128)(2,1)S(1)}, u32[]{:S(2)}, u32[]{:S(2)}) collective-permute-start(bf16[1,3,32,2048]{3,2,1,0:T(8,128)(2,1)} %bitcast.16), channel_id=1, source_target_pairs={{0,8},{2,66},{4,12},{6,70},{8,0},{10,74},{12,4},{14,78},{1,9},{3,6... | collective-permute-start | bytes 1179656 | tf_op jit(solution)/shard_map/ppermute | solution.py:313
  7.9 9.9 %collective-permute-start.8 = (bf16[1,3,32,2048]{3,2,1,0:T(8,128)(2,1)}, bf16[1,3,32,2048]{3,2,1,0:T(8,128)(2,1)S(1)}, u32[]{:S(2)}, u32[]{:S(2)}) collective-permute-start(bf16[1,3,32,2048]{3,2,1,0:T(8,128)(2,1)} %bitcast.17), channel_id=1, source_target_pairs={{0,4},{2,34},{4,8},{6,38},{8,12},{10,42},{12,0},{14,46},{1,5},{3,3... | collective-permute-start | bytes 1179656 | tf_op jit(solution)/shard_map/ppermute | solution.py:313
  8.6 10.9 %collective-permute-start.9 = (bf16[1,3,32,2048]{3,2,1,0:T(8,128)(2,1)}, bf16[1,3,32,2048]{3,2,1,0:T(8,128)(2,1)S(1)}, u32[]{:S(2)}, u32[]{:S(2)}) collective-permute-start(bf16[1,3,32,2048]{3,2,1,0:T(8,128)(2,1)} %bitcast.18), channel_id=1, source_target_pairs={{0,12},{2,98},{4,0},{6,102},{8,4},{10,106},{12,8},{14,110},{1,13},... | collective-permute-start | bytes 1179656 | tf_op jit(solution)/shard_map/ppermute | solution.py:313
  10.5 8.9 %copy-start = (bf16[3,32,2048]{2,1,0:T(8,128)(2,1)S(1)}, bf16[3,32,2048]{2,1,0:T(8,128)(2,1)}, u32[]{:S(2)}) copy-start(bf16[3,32,2048]{2,1,0:T(8,128)(2,1)} %param.9) | copy-start | bytes 1179652
  12.9 12.6 %copy-start.3 = (s32[28,16]{0,1:T(8,128)S(1)}, s32[28,16]{0,1:T(8,128)}, u32[]{:S(2)}) copy-start(s32[28,16]{0,1:T(8,128)} %param.7) | copy-start | bytes 5380
  13.0 12.6 %copy-start.4 = (f32[2048]{0:T(1024)S(1)}, f32[2048]{0:T(1024)}, u32[]{:S(2)}) copy-start(f32[2048]{0:T(1024)} %param.8) | copy-start | bytes 24580
  13.0 12.6 %collective-permute-start = (bf16[2,64,2048]{2,1,0:T(8,128)(2,1)S(1)}, bf16[2,64,2048]{2,1,0:T(8,128)(2,1)S(1)}, u32[]{:S(2)}, u32[]{:S(2)}) collective-permute-start(bf16[2,64,2048]{2,1,0:T(8,128)(2,1)S(1)} %packet.1), channel_id=1, source_target_pairs={{0,1},{2,3},{4,5},{6,7},{8,9},{10,11},{12,13},{14,15},{1,0},{3,2},... | collective-permute-start | bytes 1572872 | tf_op jit(solution)/shard_map/ppermute | solution.py:313
  13.2 20.0 %collective-permute-start.2 = (bf16[1,3,32,2048]{3,2,1,0:T(8,128)(2,1)S(1)}, bf16[1,3,32,2048]{3,2,1,0:T(8,128)(2,1)S(1)}, u32[]{:S(2)}, u32[]{:S(2)}) collective-permute-start(bf16[1,3,32,2048]{3,2,1,0:T(8,128)(2,1)S(1)} %collective-permute-done.1.refs_0_), channel_id=1, source_target_pairs={{0,4},{2,34},{4,8},{6,38},{8,12},{10,42},{12,0},{14,46},{1,5},{3,3... | collective-permute-start | bytes 1179656 | tf_op jit(solution)/shard_map/ppermute | solution.py:313
  14.7 18.4 %collective-permute-start.3 = (bf16[1,3,32,2048]{3,2,1,0:T(8,128)(2,1)S(1)}, bf16[1,3,32,2048]{3,2,1,0:T(8,128)(2,1)S(1)}, u32[]{:S(2)}, u32[]{:S(2)}) collective-permute-start(bf16[1,3,32,2048]{3,2,1,0:T(8,128)(2,1)S(1)} %collective-permute-done.1.refs_0_), channel_id=1, source_target_pairs={{0,12},{2,98},{4,0},{6,102},{8,4},{10,106},{12,8},{14,110},{1,13},... | collective-permute-start | bytes 1179656 | tf_op jit(solution)/shard_map/ppermute | solution.py:313
  17.8 15.4 %collective-permute-start.5 = (bf16[1,3,32,2048]{3,2,1,0:T(8,128)(2,1)S(1)}, bf16[1,3,32,2048]{3,2,1,0:T(8,128)(2,1)S(1)}, u32[]{:S(2)}, u32[]{:S(2)}) collective-permute-start(bf16[1,3,32,2048]{3,2,1,0:T(8,128)(2,1)S(1)} %collective-permute-done.4.refs_3_), channel_id=1, source_target_pairs={{0,17},{2,19},{4,21},{6,23},{8,25},{10,27},{12,29},{14,31},{1,16},... | collective-permute-start | bytes 1179656 | tf_op jit(solution)/shard_map/ppermute | solution.py:313
  19.6 18.3 %collective-permute-start.13 = (bf16[4,3,32,2048]{3,2,1,0:T(8,128)(2,1)S(1)}, bf16[4,3,32,2048]{3,2,1,0:T(8,128)(2,1)S(1)}, u32[]{:S(2)}, u32[]{:S(2)}) collective-permute-start(bf16[4,3,32,2048]{3,2,1,0:T(8,128)(2,1)S(1)} %join.3.refs_0_), channel_id=1, source_target_pairs={{0,2},{2,0},{4,6},{6,4},{8,10},{10,8},{12,14},{14,12},{1,3},{3,1},... | collective-permute-start | bytes 4718600 | tf_op jit(solution)/shard_map/ppermute | solution.py:313
  33.1 4.7 %copy-start.1 = (s32[3,2]{0,1:T(2,128)S(1)}, s32[3,2]{0,1:T(2,128)}, u32[]{:S(2)}) copy-start(s32[3,2]{0,1:T(2,128)} %param.10) | copy-start | bytes 76
  33.1 4.7 %copy-start.2 = (f32[3]{0:T(128)S(1)}, f32[3]{0:T(128)}, u32[]{:S(2)}) copy-start(f32[3]{0:T(128)} %freq_ref.15) | copy-start | bytes 40
  33.3 8.8 %collective-permute-start.12 = (bf16[4,3,32,2048]{3,2,1,0:T(8,128)(2,1)S(1)}, bf16[4,3,32,2048]{3,2,1,0:T(8,128)(2,1)S(1)}, u32[]{:S(2)}, u32[]{:S(2)}) collective-permute-start(bf16[4,3,32,2048]{3,2,1,0:T(8,128)(2,1)S(1)} %join.2.refs_0_), channel_id=1, source_target_pairs={{0,2},{2,0},{4,6},{6,4},{8,10},{10,8},{12,14},{14,12},{1,3},{3,1},... | collective-permute-start | bytes 4718600 | tf_op jit(solution)/shard_map/ppermute | solution.py:313
  35.2 20.8 %collective-permute-start.10 = (bf16[4,3,32,2048]{3,2,1,0:T(8,128)(2,1)S(1)}, bf16[4,3,32,2048]{3,2,1,0:T(8,128)(2,1)S(1)}, u32[]{:S(2)}, u32[]{:S(2)}) collective-permute-start(bf16[4,3,32,2048]{3,2,1,0:T(8,128)(2,1)S(1)} %join.3.refs_0_), channel_id=1, source_target_pairs={{0,32},{2,6},{4,36},{6,10},{8,40},{10,14},{12,44},{14,2},{1,33},{3... | collective-permute-start | bytes 4718600 | tf_op jit(solution)/shard_map/ppermute | solution.py:313
  35.4 20.6 %collective-permute-start.11 = (bf16[4,3,32,2048]{3,2,1,0:T(8,128)(2,1)S(1)}, bf16[4,3,32,2048]{3,2,1,0:T(8,128)(2,1)S(1)}, u32[]{:S(2)}, u32[]{:S(2)}) collective-permute-start(bf16[4,3,32,2048]{3,2,1,0:T(8,128)(2,1)S(1)} %join.3.refs_0_), channel_id=1, source_target_pairs={{0,96},{2,14},{4,100},{6,2},{8,104},{10,6},{12,108},{14,10},{1,97}... | collective-permute-start | bytes 4718600 | tf_op jit(solution)/shard_map/ppermute | solution.py:313
  55.9 7.2 %collective-permute-start.14 = (bf16[4,3,32,2048]{3,2,1,0:T(8,128)(2,1)S(1)}, bf16[4,3,32,2048]{3,2,1,0:T(8,128)(2,1)S(1)}, u32[]{:S(2)}, u32[]{:S(2)}) collective-permute-start(bf16[4,3,32,2048]{3,2,1,0:T(8,128)(2,1)S(1)} %collective-permute-done.10.refs_0_), channel_id=1, source_target_pairs={{0,2},{2,0},{4,6},{6,4},{8,10},{10,8},{12,14},{14,12},{1,3},{3,1},... | collective-permute-start | bytes 4718600 | tf_op jit(solution)/shard_map/ppermute | solution.py:313
  56.9 6.3 %collective-permute-start.15 = (bf16[4,3,32,2048]{3,2,1,0:T(8,128)(2,1)S(1)}, bf16[4,3,32,2048]{3,2,1,0:T(8,128)(2,1)S(1)}, u32[]{:S(2)}, u32[]{:S(2)}) collective-permute-start(bf16[4,3,32,2048]{3,2,1,0:T(8,128)(2,1)S(1)} %collective-permute-done.11.refs_1_), channel_id=1, source_target_pairs={{0,2},{2,0},{4,6},{6,4},{8,10},{10,8},{12,14},{14,12},{1,3},{3,1},... | collective-permute-start | bytes 4718600 | tf_op jit(solution)/shard_map/ppermute | solution.py:313
  56.9 19.6 %collective-permute-start.6 = (bf16[4,3,32,2048]{3,2,1,0:T(8,128)(2,1)S(1)}, bf16[4,3,32,2048]{3,2,1,0:T(8,128)(2,1)S(1)}, u32[]{:S(2)}, u32[]{:S(2)}) collective-permute-start(bf16[4,3,32,2048]{3,2,1,0:T(8,128)(2,1)S(1)} %join.2.refs_0_), channel_id=1, source_target_pairs={{0,96},{2,14},{4,100},{6,2},{8,104},{10,6},{12,108},{14,10},{1,97}... | collective-permute-start | bytes 4718600 | tf_op jit(solution)/shard_map/ppermute | solution.py:313
  58.8 20.8 %collective-permute-start.7 = (bf16[4,3,32,2048]{3,2,1,0:T(8,128)(2,1)S(1)}, bf16[4,3,32,2048]{3,2,1,0:T(8,128)(2,1)S(1)}, u32[]{:S(2)}, u32[]{:S(2)}) collective-permute-start(bf16[4,3,32,2048]{3,2,1,0:T(8,128)(2,1)S(1)} %join.2.refs_0_), channel_id=1, source_target_pairs={{0,32},{2,6},{4,36},{6,10},{8,40},{10,14},{12,44},{14,2},{1,33},{3... | collective-permute-start | bytes 4718600 | tf_op jit(solution)/shard_map/ppermute | solution.py:313
  79.6 20.9 %collective-permute-start.18 = (bf16[4,3,32,2048]{3,2,1,0:T(8,128)(2,1)S(1)}, bf16[4,3,32,2048]{3,2,1,0:T(8,128)(2,1)S(1)}, u32[]{:S(2)}, u32[]{:S(2)}) collective-permute-start(bf16[4,3,32,2048]{3,2,1,0:T(8,128)(2,1)S(1)} %collective-permute-done.6.refs_0_), channel_id=1, source_target_pairs={{0,2},{2,0},{4,6},{6,4},{8,10},{10,8},{12,14},{14,12},{1,3},{3,1},... | collective-permute-start | bytes 4718600 | tf_op jit(solution)/shard_map/ppermute | solution.py:313
  82.3 18.4 %collective-permute-start.19 = (bf16[4,3,32,2048]{3,2,1,0:T(8,128)(2,1)S(1)}, bf16[4,3,32,2048]{3,2,1,0:T(8,128)(2,1)S(1)}, u32[]{:S(2)}, u32[]{:S(2)}) collective-permute-start(bf16[4,3,32,2048]{3,2,1,0:T(8,128)(2,1)S(1)} %collective-permute-done.7.refs_1_), channel_id=1, source_target_pairs={{0,2},{2,0},{4,6},{6,4},{8,10},{10,8},{12,14},{14,12},{1,3},{3,1},... | collective-permute-start | bytes 4718600 | tf_op jit(solution)/shard_map/ppermute | solution.py:313
  82.3 12.4 %collective-permute-start.22 = (bf16[2,3,32,2048]{3,2,1,0:T(8,128)(2,1)S(1)}, bf16[2,3,32,2048]{3,2,1,0:T(8,128)(2,1)S(1)}, u32[]{:S(2)}, u32[]{:S(2)}) collective-permute-start(bf16[2,3,32,2048]{3,2,1,0:T(8,128)(2,1)S(1)} %slice.14), channel_id=1, source_target_pairs={{0,32},{2,6},{4,36},{6,10},{8,40},{10,14},{12,44},{14,2},{1,33},{3... | collective-permute-start | bytes 2359304 | tf_op jit(solution)/shard_map/ppermute | solution.py:313
  83.0 16.1 %collective-permute-start.23 = (bf16[2,3,32,2048]{3,2,1,0:T(8,128)(2,1)S(1)}, bf16[2,3,32,2048]{3,2,1,0:T(8,128)(2,1)S(1)}, u32[]{:S(2)}, u32[]{:S(2)}) collective-permute-start(bf16[2,3,32,2048]{3,2,1,0:T(8,128)(2,1)S(1)} %slice.15), channel_id=1, source_target_pairs={{0,96},{2,14},{4,100},{6,2},{8,104},{10,6},{12,108},{14,10},{1,97}... | collective-permute-start | bytes 2359304 | tf_op jit(solution)/shard_map/ppermute | solution.py:313
  85.3 19.6 %collective-permute-start.16 = (bf16[2,3,32,2048]{3,2,1,0:T(8,128)(2,1)S(1)}, bf16[2,3,32,2048]{3,2,1,0:T(8,128)(2,1)S(1)}, u32[]{:S(2)}, u32[]{:S(2)}) collective-permute-start(bf16[2,3,32,2048]{3,2,1,0:T(8,128)(2,1)S(1)} %slice.12), channel_id=1, source_target_pairs={{0,32},{2,6},{4,36},{6,10},{8,40},{10,14},{12,44},{14,2},{1,33},{3... | collective-permute-start | bytes 2359304 | tf_op jit(solution)/shard_map/ppermute | solution.py:313
  94.7 11.1 %collective-permute-start.17 = (bf16[2,3,32,2048]{3,2,1,0:T(8,128)(2,1)S(1)}, bf16[2,3,32,2048]{3,2,1,0:T(8,128)(2,1)S(1)}, u32[]{:S(2)}, u32[]{:S(2)}) collective-permute-start(bf16[2,3,32,2048]{3,2,1,0:T(8,128)(2,1)S(1)} %slice.13), channel_id=1, source_target_pairs={{0,96},{2,14},{4,100},{6,2},{8,104},{10,6},{12,108},{14,10},{1,97}... | collective-permute-start | bytes 2359304 | tf_op jit(solution)/shard_map/ppermute | solution.py:313
  99.1 9.0 %collective-permute-start.24 = (bf16[2,3,32,2048]{3,2,1,0:T(8,128)(2,1)S(1)}, bf16[2,3,32,2048]{3,2,1,0:T(8,128)(2,1)S(1)}, u32[]{:S(2)}, u32[]{:S(2)}) collective-permute-start(bf16[2,3,32,2048]{3,2,1,0:T(8,128)(2,1)S(1)} %collective-permute-done.22.refs_0_), channel_id=1, source_target_pairs={{0,2},{2,0},{4,6},{6,4},{8,10},{10,8},{12,14},{14,12},{1,3},{3,1},... | collective-permute-start | bytes 2359304 | tf_op jit(solution)/shard_map/ppermute | solution.py:313
  100.5 7.6 %collective-permute-start.25 = (bf16[2,3,32,2048]{3,2,1,0:T(8,128)(2,1)S(1)}, bf16[2,3,32,2048]{3,2,1,0:T(8,128)(2,1)S(1)}, u32[]{:S(2)}, u32[]{:S(2)}) collective-permute-start(bf16[2,3,32,2048]{3,2,1,0:T(8,128)(2,1)S(1)} %collective-permute-done.23.refs_1_), channel_id=1, source_target_pairs={{0,2},{2,0},{4,6},{6,4},{8,10},{10,8},{12,14},{14,12},{1,3},{3,1},... | collective-permute-start | bytes 2359304 | tf_op jit(solution)/shard_map/ppermute | solution.py:313
  105.9 6.6 %collective-permute-start.20 = (bf16[2,3,32,2048]{3,2,1,0:T(8,128)(2,1)S(1)}, bf16[2,3,32,2048]{3,2,1,0:T(8,128)(2,1)S(1)}, u32[]{:S(2)}, u32[]{:S(2)}) collective-permute-start(bf16[2,3,32,2048]{3,2,1,0:T(8,128)(2,1)S(1)} %collective-permute-done.16.refs_0_), channel_id=1, source_target_pairs={{0,2},{2,0},{4,6},{6,4},{8,10},{10,8},{12,14},{14,12},{1,3},{3,1},... | collective-permute-start | bytes 2359304 | tf_op jit(solution)/shard_map/ppermute | solution.py:313
  108.1 4.3 %collective-permute-start.21 = (bf16[2,3,32,2048]{3,2,1,0:T(8,128)(2,1)S(1)}, bf16[2,3,32,2048]{3,2,1,0:T(8,128)(2,1)S(1)}, u32[]{:S(2)}, u32[]{:S(2)}) collective-permute-start(bf16[2,3,32,2048]{3,2,1,0:T(8,128)(2,1)S(1)} %collective-permute-done.17.refs_1_), channel_id=1, source_target_pairs={{0,2},{2,0},{4,6},{6,4},{8,10},{10,8},{12,14},{14,12},{1,3},{3,1},... | collective-permute-start | bytes 2359304 | tf_op jit(solution)/shard_map/ppermute | solution.py:313

commit v3 on v2

--- a/solution.py
+++ b/solution.py
@@ -247,9 +247,12 @@
     ends = [sum(units[: k + 1]) for k in range(len(units))]
     held = [groups[end - n : end] for n, end in zip(units, ends)]
 
-    def leaving(p):
+    width = coeffs // 2 if last else coeffs
+
+    def leaving(p, c):
         staged, out_sem = refs[1:]
-        return pltpu.make_async_copy(staged.at[p], out_ref.at[p], out_sem.at[p])
+        at = pl.ds(c * width, width)
+        return pltpu.make_async_copy(staged.at[p, :, at], out_ref.at[p, :, at], out_sem.at[p, c])
 
     def ranks_of(arrays, which):
         return jnp.concatenate([ref[:, which].reshape(-1, coeffs) for ref in arrays], axis=0)
@@ -273,17 +276,20 @@
         lp = jnp.where(pair_ref[0, p] == 1, left[1], left[0])
         rp = jnp.where(pair_ref[1, p] == 1, right[1], right[0])
         product = (freq_ref[p] * lp * rp).astype(jnp.bfloat16)
-        term = jnp.dot(product, down, preferred_element_type=jnp.float32)
-        if not first:
-            term = (acc_ref if last else out_ref)[p] + term
-        if last:
-            refs[1][p] = term.astype(jnp.bfloat16)
-            leaving(p).start()
-        else:
-            out_ref[p] = term
+        for c in range(coeffs // width):
+            at = slice(c * width, (c + 1) * width)
+            term = jnp.dot(product, down[:, at], preferred_element_type=jnp.float32)
+            if not first:
+                term = (acc_ref if last else out_ref)[p, :, at] + term
+            if last:
+                refs[1][p, :, at] = term.astype(jnp.bfloat16)
+                leaving(p, c).start()
+            else:
+                out_ref[p, :, at] = term
     if last:
         for p in range(pair_count):
-            leaving(p).wait()
+            for c in range(coeffs // width):
+                leaving(p, c).wait()
 
 
 def collide(adv, frequency, pairs, held, acc, last=False):
@@ -298,7 +304,7 @@
         in_specs=[SMEM, SMEM] + [VMEM] * (len(operands) - 2),
         out_specs=HBM if last else VMEM,
         out_shape=jax.ShapeDtypeStruct(shape, jnp.bfloat16) if last else pltpu.VMEM(shape, jnp.float32),
-        scratch_shapes=[pltpu.VMEM(shape, jnp.bfloat16), DMA((pair_count,))] if last else [],
+        scratch_shapes=[pltpu.VMEM(shape, jnp.bfloat16), DMA((pair_count, 2))] if last else [],
         input_output_aliases={} if acc is None or last else {len(operands) - 1: 0},
         cost_estimate=cost(
             2 * ranks * coeffs * rows * (2 * species + pair_count),
@@ -370,9 +376,9 @@
     *far_o, _ = lax.optimization_barrier((*far_o, acc))
     swap_fo = swap(far_o)
     acc = step([swap_dc, swap_uc], acc)
+    acc = step([far_o, swap_fo], acc)
     *far_c, _ = lax.optimization_barrier((*far_c, acc))
     swap_fc = swap(far_c)
-    acc = step([far_o, swap_fo], acc)
     out = step([far_c, swap_fc], acc, last=True)
     collision = out.reshape(pair_list.shape[0], lines, cells, coeffs)
     return (advanced, collision)

time: 119 us -> 119 us (level)
  starting transfers between devices: 33.4 us -> 35 us
    ppermute x26, starting transfers between devices: 33.4 us -> 35 us  [send(): return lax.ppermute(array, AXES, pairs)]
  transfers between devices with their start and end apart: 26 -> 26, of which waited for: 8 -> 10; matrix products, arithmetic and copies ran while one was open for 0% -> 0% of each run, Pallas kernels for 34% -> 34%
where the time goes in v3:
time: 119 us
  Pallas kernels  45.7 us (38%)
  waiting for transfers between devices  36.8 us (31%)
  starting transfers between devices  35 us (29%)
    ppermute x26, waiting for transfers between devices, send(): return lax.ppermute(array, AXES, pairs)  36.8 us
    pallas_call x8, Pallas kernels, collide(): pl.pallas_call(functools.partial(collide_kernel, [len(unit) for unit in h...  35.6 us
    ppermute x26, starting transfers between devices, send(): return lax.ppermute(array, AXES, pairs)  35 us
    pallas_call x1, Pallas kernels, transport(): pl.pallas_call(transport_kernel, in_specs=[SMEM, VMEM, VMEM, VMEM, HBM],...  7.51 us
    pallas_call x1, Pallas kernels, packet_of(): pl.pallas_call(packet_kernel, in_specs=[SMEM, HBM, HBM], out_specs=VMEM,...  2.4 us
  transfers between devices with their start and end apart: 26, of which 10 were waited for; matrix products, arithmetic and copies ran while one was open for 0% of the time, Pallas kernels for 34%

profile of v3, /device:TPU:1, one launch (start us, length us, event | category | flops | bytes accessed | tf_op | source)
XLA Modules:
  0.0 118.9 jit_solution(16277379321851508447)
XLA Ops:
  0.6 3.6 %collective-permute-start.1 = (bf16[1,3,32,2048]{3,2,1,0:T(8,128)(2,1)}, bf16[1,3,32,2048]{3,2,1,0:T(8,128)(2,1)S(1)}, u32[]{:S(2)}, u32[]{:S(2)}) collective-permute-start(bf16[1,3,32,2048]{3,2,1,0:T(8,128)(2,1)} %bitcast.15), channel_id=1, source_target_pairs={{0,17},{2,19},{4,21},{6,23},{8,25},{10,27},{12,29},{14,31},{1,16},... | collective-permute-start | bytes 1179656 | tf_op jit(solution)/shard_map/ppermute | solution.py:319
  4.3 3.6 %collective-permute-start.4 = (bf16[1,3,32,2048]{3,2,1,0:T(8,128)(2,1)}, bf16[1,3,32,2048]{3,2,1,0:T(8,128)(2,1)S(1)}, u32[]{:S(2)}, u32[]{:S(2)}) collective-permute-start(bf16[1,3,32,2048]{3,2,1,0:T(8,128)(2,1)} %bitcast.16), channel_id=1, source_target_pairs={{0,8},{2,66},{4,12},{6,70},{8,0},{10,74},{12,4},{14,78},{1,9},{3,6... | collective-permute-start | bytes 1179656 | tf_op jit(solution)/shard_map/ppermute | solution.py:319
  7.9 0.7 collective-permute-start.8
  8.6 1.9 %collective-permute-start.9 = (bf16[1,3,32,2048]{3,2,1,0:T(8,128)(2,1)}, bf16[1,3,32,2048]{3,2,1,0:T(8,128)(2,1)S(1)}, u32[]{:S(2)}, u32[]{:S(2)}) collective-permute-start(bf16[1,3,32,2048]{3,2,1,0:T(8,128)(2,1)} %bitcast.18), channel_id=1, source_target_pairs={{0,12},{2,98},{4,0},{6,102},{8,4},{10,106},{12,8},{14,110},{1,13},... | collective-permute-start | bytes 1179656 | tf_op jit(solution)/shard_map/ppermute | solution.py:319
  10.5 2.4 %packet.1 = bf16[2,64,2048]{2,1,0:T(8,128)(2,1)S(1)} custom-call(s32[1]{0:T(128)} %bitcast.where_ref, s32[16,28]{1,0:T(8,128)} %bitcast.28, bf16[2,28,16,2048]{3,2,1,0:T(8,128)(2,1)} %cells_hbm.1), custom_call_target="tpu_custom_call" | custom-call | flops 1835008 | bytes 1835008 | tf_op jit(solution)/shard_map/packet/pallas_call | solution.py:87
  12.9 0.0 copy-start.3
  13.0 0.1 collective-permute-start
  13.1 0.1 collective-permute-done.1.refs_0_
  13.2 1.5 %collective-permute-start.2 = (bf16[1,3,32,2048]{3,2,1,0:T(8,128)(2,1)S(1)}, bf16[1,3,32,2048]{3,2,1,0:T(8,128)(2,1)S(1)}, u32[]{:S(2)}, u32[]{:S(2)}) collective-permute-start(bf16[1,3,32,2048]{3,2,1,0:T(8,128)(2,1)S(1)} %collective-permute-done.1.refs_0_), channel_id=1, source_target_pairs={{0,4},{2,34},{4,8},{6,38},{8,12},{10,42},{12,0},{14,46},{1,5},{3,3... | collective-permute-start | bytes 1179656 | tf_op jit(solution)/shard_map/ppermute | solution.py:319
  14.7 2.1 %collective-permute-start.3 = (bf16[1,3,32,2048]{3,2,1,0:T(8,128)(2,1)S(1)}, bf16[1,3,32,2048]{3,2,1,0:T(8,128)(2,1)S(1)}, u32[]{:S(2)}, u32[]{:S(2)}) collective-permute-start(bf16[1,3,32,2048]{3,2,1,0:T(8,128)(2,1)S(1)} %collective-permute-done.1.refs_0_), channel_id=1, source_target_pairs={{0,12},{2,98},{4,0},{6,102},{8,4},{10,106},{12,8},{14,110},{1,13},... | collective-permute-start | bytes 1179656 | tf_op jit(solution)/shard_map/ppermute | solution.py:319
  16.8 0.9 collective-permute-done.8.refs_1_
  17.8 1.7 %collective-permute-start.5 = (bf16[1,3,32,2048]{3,2,1,0:T(8,128)(2,1)S(1)}, bf16[1,3,32,2048]{3,2,1,0:T(8,128)(2,1)S(1)}, u32[]{:S(2)}, u32[]{:S(2)}) collective-permute-start(bf16[1,3,32,2048]{3,2,1,0:T(8,128)(2,1)S(1)} %collective-permute-done.4.refs_3_), channel_id=1, source_target_pairs={{0,17},{2,19},{4,21},{6,23},{8,25},{10,27},{12,29},{14,31},{1,16},... | collective-permute-start | bytes 1179656 | tf_op jit(solution)/shard_map/ppermute | solution.py:319
  19.5 0.1 join.3.refs_0_
  19.6 1.4 %collective-permute-start.13 = (bf16[4,3,32,2048]{3,2,1,0:T(8,128)(2,1)S(1)}, bf16[4,3,32,2048]{3,2,1,0:T(8,128)(2,1)S(1)}, u32[]{:S(2)}, u32[]{:S(2)}) collective-permute-start(bf16[4,3,32,2048]{3,2,1,0:T(8,128)(2,1)S(1)} %join.3.refs_0_), channel_id=1, source_target_pairs={{0,2},{2,0},{4,6},{6,4},{8,10},{10,8},{12,14},{14,12},{1,3},{3,1},... | collective-permute-start | bytes 4718600 | tf_op jit(solution)/shard_map/ppermute | solution.py:319
  20.9 4.7 %collective-permute-done.packet_ref = bf16[2,64,2048]{2,1,0:T(8,128)(2,1)S(1)} collective-permute-done((bf16[2,64,2048]{2,1,0:T(8,128)(2,1)S(1)}, bf16[2,64,2048]{2,1,0:T(8,128)(2,1)S(1)}, u32[]{:S(2)}, u32[]{:S(2)}) %collective-permute-start) | collective-permute-done | bytes 524320 | tf_op jit(solution)/shard_map/ppermute | solution.py:319
  25.6 7.5 %transport.1 = (bf16[2,28,16,2048]{3,2,1,0:T(8,128)(2,1)S(1)}, bf16[2,28,16,2048]{3,2,1,0:T(8,128)(2,1)}) custom-call(s32[1]{0:T(128)} %bitcast.where_ref, f32[1,2048]{1,0:T(1,128)S(1)} %bitcast.30, s32[16,28]{1,0:T(8,128)S(1)} %bitcast.29, bf16[2,64,2048]{2,1,0:T(8,128)(2,1)S(1)} %collective-permute-done.packet_ref, bf16[2,28,16,2048]{3,2,1,0:T(8,128)(2,1)} %cells_hbm.1), custom_call_target="tpu_custom_call" | custom-call | flops 55050240 | bytes 7340032 | tf_op jit(solution)/shard_map/transport/pallas_call | solution.py:199
  33.2 0.1 join.2.refs_0_
  33.3 1.9 %collective-permute-start.12 = (bf16[4,3,32,2048]{3,2,1,0:T(8,128)(2,1)S(1)}, bf16[4,3,32,2048]{3,2,1,0:T(8,128)(2,1)S(1)}, u32[]{:S(2)}, u32[]{:S(2)}) collective-permute-start(bf16[4,3,32,2048]{3,2,1,0:T(8,128)(2,1)S(1)} %join.2.refs_0_), channel_id=1, source_target_pairs={{0,2},{2,0},{4,6},{6,4},{8,10},{10,8},{12,14},{14,12},{1,3},{3,1},... | collective-permute-start | bytes 4718600 | tf_op jit(solution)/shard_map/ppermute | solution.py:319
  35.2 0.2 collective-permute-start.10
  35.4 2.5 %collective-permute-start.11 = (bf16[4,3,32,2048]{3,2,1,0:T(8,128)(2,1)S(1)}, bf16[4,3,32,2048]{3,2,1,0:T(8,128)(2,1)S(1)}, u32[]{:S(2)}, u32[]{:S(2)}) collective-permute-start(bf16[4,3,32,2048]{3,2,1,0:T(8,128)(2,1)S(1)} %join.3.refs_0_), channel_id=1, source_target_pairs={{0,96},{2,14},{4,100},{6,2},{8,104},{10,6},{12,108},{14,10},{1,97}... | collective-permute-start | bytes 4718600 | tf_op jit(solution)/shard_map/ppermute | solution.py:319
  37.9 4.2 %collide.8.refs_2_ = f32[3,448,2048]{2,1,0:T(8,128)S(1)} custom-call(f32[3]{0:T(128)S(1)} %copy-done.2, s32[2,3]{1,0:T(2,128)S(1)} %bitcast.20, bf16[2,448,2048]{2,1,0:T(8,128)(2,1)S(1)} %bitcast.7, bf16[4,3,32,2048]{3,2,1,0:T(8,128)(2,1)S(1)} %join.3.refs_0_, bf16[4,3,32,2048]{3,2,1,0:T(8,128)(2,1)S(1)} %collective-permute-done.13.refs_1_), custom_call_target="tpu_custom_call" | custom-call | flops 3288334336 | bytes 6815744 | tf_op jit(solution)/shard_map/collide/pallas_call | solution.py:302
  42.1 4.3 %collide.9.refs_2_ = f32[3,448,2048]{2,1,0:T(8,128)S(1)} custom-call(f32[3]{0:T(128)S(1)} %copy-done.2, s32[2,3]{1,0:T(2,128)S(1)} %bitcast.21, bf16[2,448,2048]{2,1,0:T(8,128)(2,1)S(1)} %bitcast.8, bf16[4,3,32,2048]{3,2,1,0:T(8,128)(2,1)S(1)} %join.2.refs_0_, ...), custom_call_target="tpu_custom_call", output_to_operand_aliasing={{}: (5, {})} | custom-call | flops 3288334336 | bytes 6815744 | tf_op jit(solution)/shard_map/collide/pallas_call | solution.py:302
  46.4 9.5 %collective-permute-done.10.refs_0_ = bf16[4,3,32,2048]{3,2,1,0:T(8,128)(2,1)S(1)} collective-permute-done((bf16[4,3,32,2048]{3,2,1,0:T(8,128)(2,1)S(1)}, bf16[4,3,32,2048]{3,2,1,0:T(8,128)(2,1)S(1)}, u32[]{:S(2)}, u32[]{:S(2)}) %collective-permute-start.10) | collective-permute-done | bytes 1572896 | tf_op jit(solution)/shard_map/ppermute | solution.py:319
  55.9 0.9 collective-permute-start.14
  56.9 1.9 %collective-permute-start.6 = (bf16[4,3,32,2048]{3,2,1,0:T(8,128)(2,1)S(1)}, bf16[4,3,32,2048]{3,2,1,0:T(8,128)(2,1)S(1)}, u32[]{:S(2)}, u32[]{:S(2)}) collective-permute-start(bf16[4,3,32,2048]{3,2,1,0:T(8,128)(2,1)S(1)} %join.2.refs_0_), channel_id=1, source_target_pairs={{0,96},{2,14},{4,100},{6,2},{8,104},{10,6},{12,108},{14,10},{1,97}... | collective-permute-start | bytes 4718600 | tf_op jit(solution)/shard_map/ppermute | solution.py:319
  58.8 4.3 %collide.10.refs_2_ = f32[3,448,2048]{2,1,0:T(8,128)S(1)} custom-call(f32[3]{0:T(128)S(1)} %copy-done.2, s32[2,3]{1,0:T(2,128)S(1)} %bitcast.22, bf16[2,448,2048]{2,1,0:T(8,128)(2,1)S(1)} %bitcast.9, bf16[4,3,32,2048]{3,2,1,0:T(8,128)(2,1)S(1)} %collective-permute-done.10.refs_0_, ...), custom_call_target="tpu_custom_call", output_to_operand_aliasing={{}: (5, {})} | custom-call | flops 3288334336 | bytes 6815744 | tf_op jit(solution)/shard_map/collide/pallas_call | solution.py:302
  63.2 4.3 %collide.11.refs_2_ = f32[3,448,2048]{2,1,0:T(8,128)S(1)} custom-call(f32[3]{0:T(128)S(1)} %copy-done.2, s32[2,3]{1,0:T(2,128)S(1)} %bitcast.23, bf16[2,448,2048]{2,1,0:T(8,128)(2,1)S(1)} %bitcast.10, bf16[4,3,32,2048]{3,2,1,0:T(8,128)(2,1)S(1)} %collective-permute-done.14.refs_0_, ...), custom_call_target="tpu_custom_call", output_to_operand_aliasing={{}: (5, {})} | custom-call | flops 3288334336 | bytes 6815744 | tf_op jit(solution)/shard_map/collide/pallas_call | solution.py:302
  67.5 8.9 %collective-permute-done.6.refs_0_ = bf16[4,3,32,2048]{3,2,1,0:T(8,128)(2,1)S(1)} collective-permute-done((bf16[4,3,32,2048]{3,2,1,0:T(8,128)(2,1)S(1)}, bf16[4,3,32,2048]{3,2,1,0:T(8,128)(2,1)S(1)}, u32[]{:S(2)}, u32[]{:S(2)}) %collective-permute-start.6) | collective-permute-done | bytes 1572896 | tf_op jit(solution)/shard_map/ppermute | solution.py:319
  76.4 3.2 %collective-permute-done.7.refs_1_ = bf16[4,3,32,2048]{3,2,1,0:T(8,128)(2,1)S(1)} collective-permute-done((bf16[4,3,32,2048]{3,2,1,0:T(8,128)(2,1)S(1)}, bf16[4,3,32,2048]{3,2,1,0:T(8,128)(2,1)S(1)}, u32[]{:S(2)}, u32[]{:S(2)}) %collective-permute-start.7) | collective-permute-done | bytes 1572896 | tf_op jit(solution)/shard_map/ppermute | solution.py:319
  79.6 2.6 %collective-permute-start.22 = (bf16[4,3,32,2048]{3,2,1,0:T(8,128)(2,1)S(1)}, bf16[4,3,32,2048]{3,2,1,0:T(8,128)(2,1)S(1)}, u32[]{:S(2)}, u32[]{:S(2)}) collective-permute-start(bf16[4,3,32,2048]{3,2,1,0:T(8,128)(2,1)S(1)} %collective-permute-done.6.refs_0_), channel_id=1, source_target_pairs={{0,2},{2,0},{4,6},{6,4},{8,10},{10,8},{12,14},{14,12},{1,3},{3,1},... | collective-permute-start | bytes 4718600 | tf_op jit(solution)/shard_map/ppermute | solution.py:319
  82.3 0.1 slice.14
  82.3 0.1 slice.15
  82.4 0.6 collective-permute-start.18
  83.0 2.1 %collective-permute-start.19 = (bf16[2,3,32,2048]{3,2,1,0:T(8,128)(2,1)S(1)}, bf16[2,3,32,2048]{3,2,1,0:T(8,128)(2,1)S(1)}, u32[]{:S(2)}, u32[]{:S(2)}) collective-permute-start(bf16[2,3,32,2048]{3,2,1,0:T(8,128)(2,1)S(1)} %slice.15), channel_id=1, source_target_pairs={{0,96},{2,14},{4,100},{6,2},{8,104},{10,6},{12,108},{14,10},{1,97}... | collective-permute-start | bytes 2359304 | tf_op jit(solution)/shard_map/ppermute | solution.py:319
  85.2 4.3 %collide.12.refs_2_ = f32[3,448,2048]{2,1,0:T(8,128)S(1)} custom-call(f32[3]{0:T(128)S(1)} %copy-done.2, s32[2,3]{1,0:T(2,128)S(1)} %bitcast.24, bf16[2,448,2048]{2,1,0:T(8,128)(2,1)S(1)} %bitcast.11, bf16[4,3,32,2048]{3,2,1,0:T(8,128)(2,1)S(1)} %collective-permute-done.6.refs_0_, ...), custom_call_target="tpu_custom_call", output_to_operand_aliasing={{}: (5, {})} | custom-call | flops 3288334336 | bytes 6815744 | tf_op jit(solution)/shard_map/collide/pallas_call | solution.py:302
  89.5 5.3 %collective-permute-done.18.refs_0_ = bf16[2,3,32,2048]{3,2,1,0:T(8,128)(2,1)S(1)} collective-permute-done((bf16[2,3,32,2048]{3,2,1,0:T(8,128)(2,1)S(1)}, bf16[2,3,32,2048]{3,2,1,0:T(8,128)(2,1)S(1)}, u32[]{:S(2)}, u32[]{:S(2)}) %collective-permute-start.18) | collective-permute-done | bytes 786464 | tf_op jit(solution)/shard_map/ppermute | solution.py:319
  94.8 1.4 %collective-permute-start.20 = (bf16[2,3,32,2048]{3,2,1,0:T(8,128)(2,1)S(1)}, bf16[2,3,32,2048]{3,2,1,0:T(8,128)(2,1)S(1)}, u32[]{:S(2)}, u32[]{:S(2)}) collective-permute-start(bf16[2,3,32,2048]{3,2,1,0:T(8,128)(2,1)S(1)} %collective-permute-done.18.refs_0_), channel_id=1, source_target_pairs={{0,2},{2,0},{4,6},{6,4},{8,10},{10,8},{12,14},{14,12},{1,3},{3,1},... | collective-permute-start | bytes 2359304 | tf_op jit(solution)/shard_map/ppermute | solution.py:319
  96.2 0.1 slice.12
  96.3 0.1 slice.13
  96.3 0.6 collective-permute-start.16
  96.9 2.1 %collective-permute-start.17 = (bf16[2,3,32,2048]{3,2,1,0:T(8,128)(2,1)S(1)}, bf16[2,3,32,2048]{3,2,1,0:T(8,128)(2,1)S(1)}, u32[]{:S(2)}, u32[]{:S(2)}) collective-permute-start(bf16[2,3,32,2048]{3,2,1,0:T(8,128)(2,1)S(1)} %slice.13), channel_id=1, source_target_pairs={{0,96},{2,14},{4,100},{6,2},{8,104},{10,6},{12,108},{14,10},{1,97}... | collective-permute-start | bytes 2359304 | tf_op jit(solution)/shard_map/ppermute | solution.py:319
  99.1 4.3 %collide.13.refs_4_ = f32[3,448,2048]{2,1,0:T(8,128)S(1)} custom-call(f32[3]{0:T(128)S(1)} %copy-done.2, s32[2,3]{1,0:T(2,128)S(1)} %bitcast.25, bf16[2,448,2048]{2,1,0:T(8,128)(2,1)S(1)} %bitcast.12, bf16[4,3,32,2048]{3,2,1,0:T(8,128)(2,1)S(1)} %collective-permute-done.22.refs_0_, ...), custom_call_target="tpu_custom_call", output_to_operand_aliasing={{}: (5, {})} | custom-call | flops 3288334336 | bytes 6815744 | tf_op jit(solution)/shard_map/collide/pallas_call | solution.py:302
  103.4 4.3 %collide.14.refs_4_ = f32[3,448,2048]{2,1,0:T(8,128)S(1)} custom-call(f32[3]{0:T(128)S(1)} %copy-done.2, s32[2,3]{1,0:T(2,128)S(1)} %bitcast.26, bf16[2,448,2048]{2,1,0:T(8,128)(2,1)S(1)} %bitcast.13, bf16[2,3,32,2048]{3,2,1,0:T(8,128)(2,1)S(1)} %collective-permute-done.18.refs_0_, ...), custom_call_target="tpu_custom_call", output_to_operand_aliasing={{}: (7, {})} | custom-call | flops 3288334336 | bytes 6815744 | tf_op jit(solution)/shard_map/collide/pallas_call | solution.py:302
  107.7 1.0 collective-permute-done.16.refs_0_
  108.7 1.4 %collective-permute-start.24 = (bf16[2,3,32,2048]{3,2,1,0:T(8,128)(2,1)S(1)}, bf16[2,3,32,2048]{3,2,1,0:T(8,128)(2,1)S(1)}, u32[]{:S(2)}, u32[]{:S(2)}) collective-permute-start(bf16[2,3,32,2048]{3,2,1,0:T(8,128)(2,1)S(1)} %collective-permute-done.16.refs_0_), channel_id=1, source_target_pairs={{0,2},{2,0},{4,6},{6,4},{8,10},{10,8},{12,14},{14,12},{1,3},{3,1},... | collective-permute-start | bytes 2359304 | tf_op jit(solution)/shard_map/ppermute | solution.py:319
  110.1 1.9 %collective-permute-done.24.refs_2_ = bf16[2,3,32,2048]{3,2,1,0:T(8,128)(2,1)S(1)} collective-permute-done((bf16[2,3,32,2048]{3,2,1,0:T(8,128)(2,1)S(1)}, bf16[2,3,32,2048]{3,2,1,0:T(8,128)(2,1)S(1)}, u32[]{:S(2)}, u32[]{:S(2)}) %collective-permute-start.24) | collective-permute-done | bytes 786464 | tf_op jit(solution)/shard_map/ppermute | solution.py:319
  112.0 1.1 collective-permute-done.25.refs_3_
  113.2 5.5 %collide.15 = bf16[3,448,2048]{2,1,0:T(8,128)(2,1)} custom-call(f32[3]{0:T(128)S(1)} %copy-done.2, s32[2,3]{1,0:T(2,128)S(1)} %bitcast.27, bf16[2,448,2048]{2,1,0:T(8,128)(2,1)S(1)} %bitcast.14, bf16[2,3,32,2048]{3,2,1,0:T(8,128)(2,1)S(1)} %collective-permute-done.16.refs_0_, bf16[2,3,32,2048]{3,2,1,0:T(8,128)(2,1)S(1)} %collective-permute-done.17.refs_1_, ...), custom_call_target="tpu_custom_call" | custom-call | flops 3288334336 | bytes 6815744 | tf_op jit(solution)/shard_map/collide/pallas_call | solution.py:302
  (30 shorter events, 0.1 us)
Async XLA Ops:
  0.6 12.6 %collective-permute-start.1 = (bf16[1,3,32,2048]{3,2,1,0:T(8,128)(2,1)}, bf16[1,3,32,2048]{3,2,1,0:T(8,128)(2,1)S(1)}, u32[]{:S(2)}, u32[]{:S(2)}) collective-permute-start(bf16[1,3,32,2048]{3,2,1,0:T(8,128)(2,1)} %bitcast.15), channel_id=1, source_target_pairs={{0,17},{2,19},{4,21},{6,23},{8,25},{10,27},{12,29},{14,31},{1,16},... | collective-permute-start | bytes 1179656 | tf_op jit(solution)/shard_map/ppermute | solution.py:319
  4.3 10.5 %collective-permute-start.4 = (bf16[1,3,32,2048]{3,2,1,0:T(8,128)(2,1)}, bf16[1,3,32,2048]{3,2,1,0:T(8,128)(2,1)S(1)}, u32[]{:S(2)}, u32[]{:S(2)}) collective-permute-start(bf16[1,3,32,2048]{3,2,1,0:T(8,128)(2,1)} %bitcast.16), channel_id=1, source_target_pairs={{0,8},{2,66},{4,12},{6,70},{8,0},{10,74},{12,4},{14,78},{1,9},{3,6... | collective-permute-start | bytes 1179656 | tf_op jit(solution)/shard_map/ppermute | solution.py:319
  7.9 9.9 %collective-permute-start.8 = (bf16[1,3,32,2048]{3,2,1,0:T(8,128)(2,1)}, bf16[1,3,32,2048]{3,2,1,0:T(8,128)(2,1)S(1)}, u32[]{:S(2)}, u32[]{:S(2)}) collective-permute-start(bf16[1,3,32,2048]{3,2,1,0:T(8,128)(2,1)} %bitcast.17), channel_id=1, source_target_pairs={{0,4},{2,34},{4,8},{6,38},{8,12},{10,42},{12,0},{14,46},{1,5},{3,3... | collective-permute-start | bytes 1179656 | tf_op jit(solution)/shard_map/ppermute | solution.py:319
  8.6 10.9 %collective-permute-start.9 = (bf16[1,3,32,2048]{3,2,1,0:T(8,128)(2,1)}, bf16[1,3,32,2048]{3,2,1,0:T(8,128)(2,1)S(1)}, u32[]{:S(2)}, u32[]{:S(2)}) collective-permute-start(bf16[1,3,32,2048]{3,2,1,0:T(8,128)(2,1)} %bitcast.18), channel_id=1, source_target_pairs={{0,12},{2,98},{4,0},{6,102},{8,4},{10,106},{12,8},{14,110},{1,13},... | collective-permute-start | bytes 1179656 | tf_op jit(solution)/shard_map/ppermute | solution.py:319
  10.5 8.9 %copy-start = (bf16[3,32,2048]{2,1,0:T(8,128)(2,1)S(1)}, bf16[3,32,2048]{2,1,0:T(8,128)(2,1)}, u32[]{:S(2)}) copy-start(bf16[3,32,2048]{2,1,0:T(8,128)(2,1)} %param.9) | copy-start | bytes 1179652
  12.9 12.6 %copy-start.3 = (s32[28,16]{0,1:T(8,128)S(1)}, s32[28,16]{0,1:T(8,128)}, u32[]{:S(2)}) copy-start(s32[28,16]{0,1:T(8,128)} %param.7) | copy-start | bytes 5380
  13.0 12.6 %copy-start.4 = (f32[2048]{0:T(1024)S(1)}, f32[2048]{0:T(1024)}, u32[]{:S(2)}) copy-start(f32[2048]{0:T(1024)} %param.8) | copy-start | bytes 24580
  13.0 12.6 %collective-permute-start = (bf16[2,64,2048]{2,1,0:T(8,128)(2,1)S(1)}, bf16[2,64,2048]{2,1,0:T(8,128)(2,1)S(1)}, u32[]{:S(2)}, u32[]{:S(2)}) collective-permute-start(bf16[2,64,2048]{2,1,0:T(8,128)(2,1)S(1)} %packet.1), channel_id=1, source_target_pairs={{0,1},{2,3},{4,5},{6,7},{8,9},{10,11},{12,13},{14,15},{1,0},{3,2},... | collective-permute-start | bytes 1572872 | tf_op jit(solution)/shard_map/ppermute | solution.py:319
  13.2 20.0 %collective-permute-start.2 = (bf16[1,3,32,2048]{3,2,1,0:T(8,128)(2,1)S(1)}, bf16[1,3,32,2048]{3,2,1,0:T(8,128)(2,1)S(1)}, u32[]{:S(2)}, u32[]{:S(2)}) collective-permute-start(bf16[1,3,32,2048]{3,2,1,0:T(8,128)(2,1)S(1)} %collective-permute-done.1.refs_0_), channel_id=1, source_target_pairs={{0,4},{2,34},{4,8},{6,38},{8,12},{10,42},{12,0},{14,46},{1,5},{3,3... | collective-permute-start | bytes 1179656 | tf_op jit(solution)/shard_map/ppermute | solution.py:319
  14.7 18.4 %collective-permute-start.3 = (bf16[1,3,32,2048]{3,2,1,0:T(8,128)(2,1)S(1)}, bf16[1,3,32,2048]{3,2,1,0:T(8,128)(2,1)S(1)}, u32[]{:S(2)}, u32[]{:S(2)}) collective-permute-start(bf16[1,3,32,2048]{3,2,1,0:T(8,128)(2,1)S(1)} %collective-permute-done.1.refs_0_), channel_id=1, source_target_pairs={{0,12},{2,98},{4,0},{6,102},{8,4},{10,106},{12,8},{14,110},{1,13},... | collective-permute-start | bytes 1179656 | tf_op jit(solution)/shard_map/ppermute | solution.py:319
  17.8 15.4 %collective-permute-start.5 = (bf16[1,3,32,2048]{3,2,1,0:T(8,128)(2,1)S(1)}, bf16[1,3,32,2048]{3,2,1,0:T(8,128)(2,1)S(1)}, u32[]{:S(2)}, u32[]{:S(2)}) collective-permute-start(bf16[1,3,32,2048]{3,2,1,0:T(8,128)(2,1)S(1)} %collective-permute-done.4.refs_3_), channel_id=1, source_target_pairs={{0,17},{2,19},{4,21},{6,23},{8,25},{10,27},{12,29},{14,31},{1,16},... | collective-permute-start | bytes 1179656 | tf_op jit(solution)/shard_map/ppermute | solution.py:319
  19.6 18.3 %collective-permute-start.13 = (bf16[4,3,32,2048]{3,2,1,0:T(8,128)(2,1)S(1)}, bf16[4,3,32,2048]{3,2,1,0:T(8,128)(2,1)S(1)}, u32[]{:S(2)}, u32[]{:S(2)}) collective-permute-start(bf16[4,3,32,2048]{3,2,1,0:T(8,128)(2,1)S(1)} %join.3.refs_0_), channel_id=1, source_target_pairs={{0,2},{2,0},{4,6},{6,4},{8,10},{10,8},{12,14},{14,12},{1,3},{3,1},... | collective-permute-start | bytes 4718600 | tf_op jit(solution)/shard_map/ppermute | solution.py:319
  33.1 4.7 %copy-start.1 = (s32[3,2]{0,1:T(2,128)S(1)}, s32[3,2]{0,1:T(2,128)}, u32[]{:S(2)}) copy-start(s32[3,2]{0,1:T(2,128)} %param.10) | copy-start | bytes 76
  33.1 4.7 %copy-start.2 = (f32[3]{0:T(128)S(1)}, f32[3]{0:T(128)}, u32[]{:S(2)}) copy-start(f32[3]{0:T(128)} %freq_ref.15) | copy-start | bytes 40
  33.3 8.8 %collective-permute-start.12 = (bf16[4,3,32,2048]{3,2,1,0:T(8,128)(2,1)S(1)}, bf16[4,3,32,2048]{3,2,1,0:T(8,128)(2,1)S(1)}, u32[]{:S(2)}, u32[]{:S(2)}) collective-permute-start(bf16[4,3,32,2048]{3,2,1,0:T(8,128)(2,1)S(1)} %join.2.refs_0_), channel_id=1, source_target_pairs={{0,2},{2,0},{4,6},{6,4},{8,10},{10,8},{12,14},{14,12},{1,3},{3,1},... | collective-permute-start | bytes 4718600 | tf_op jit(solution)/shard_map/ppermute | solution.py:319
  35.2 20.8 %collective-permute-start.10 = (bf16[4,3,32,2048]{3,2,1,0:T(8,128)(2,1)S(1)}, bf16[4,3,32,2048]{3,2,1,0:T(8,128)(2,1)S(1)}, u32[]{:S(2)}, u32[]{:S(2)}) collective-permute-start(bf16[4,3,32,2048]{3,2,1,0:T(8,128)(2,1)S(1)} %join.3.refs_0_), channel_id=1, source_target_pairs={{0,32},{2,6},{4,36},{6,10},{8,40},{10,14},{12,44},{14,2},{1,33},{3... | collective-permute-start | bytes 4718600 | tf_op jit(solution)/shard_map/ppermute | solution.py:319
  35.4 20.6 %collective-permute-start.11 = (bf16[4,3,32,2048]{3,2,1,0:T(8,128)(2,1)S(1)}, bf16[4,3,32,2048]{3,2,1,0:T(8,128)(2,1)S(1)}, u32[]{:S(2)}, u32[]{:S(2)}) collective-permute-start(bf16[4,3,32,2048]{3,2,1,0:T(8,128)(2,1)S(1)} %join.3.refs_0_), channel_id=1, source_target_pairs={{0,96},{2,14},{4,100},{6,2},{8,104},{10,6},{12,108},{14,10},{1,97}... | collective-permute-start | bytes 4718600 | tf_op jit(solution)/shard_map/ppermute | solution.py:319
  55.9 7.2 %collective-permute-start.14 = (bf16[4,3,32,2048]{3,2,1,0:T(8,128)(2,1)S(1)}, bf16[4,3,32,2048]{3,2,1,0:T(8,128)(2,1)S(1)}, u32[]{:S(2)}, u32[]{:S(2)}) collective-permute-start(bf16[4,3,32,2048]{3,2,1,0:T(8,128)(2,1)S(1)} %collective-permute-done.10.refs_0_), channel_id=1, source_target_pairs={{0,2},{2,0},{4,6},{6,4},{8,10},{10,8},{12,14},{14,12},{1,3},{3,1},... | collective-permute-start | bytes 4718600 | tf_op jit(solution)/shard_map/ppermute | solution.py:319
  56.9 6.3 %collective-permute-start.15 = (bf16[4,3,32,2048]{3,2,1,0:T(8,128)(2,1)S(1)}, bf16[4,3,32,2048]{3,2,1,0:T(8,128)(2,1)S(1)}, u32[]{:S(2)}, u32[]{:S(2)}) collective-permute-start(bf16[4,3,32,2048]{3,2,1,0:T(8,128)(2,1)S(1)} %collective-permute-done.11.refs_1_), channel_id=1, source_target_pairs={{0,2},{2,0},{4,6},{6,4},{8,10},{10,8},{12,14},{14,12},{1,3},{3,1},... | collective-permute-start | bytes 4718600 | tf_op jit(solution)/shard_map/ppermute | solution.py:319
  56.9 19.6 %collective-permute-start.6 = (bf16[4,3,32,2048]{3,2,1,0:T(8,128)(2,1)S(1)}, bf16[4,3,32,2048]{3,2,1,0:T(8,128)(2,1)S(1)}, u32[]{:S(2)}, u32[]{:S(2)}) collective-permute-start(bf16[4,3,32,2048]{3,2,1,0:T(8,128)(2,1)S(1)} %join.2.refs_0_), channel_id=1, source_target_pairs={{0,96},{2,14},{4,100},{6,2},{8,104},{10,6},{12,108},{14,10},{1,97}... | collective-permute-start | bytes 4718600 | tf_op jit(solution)/shard_map/ppermute | solution.py:319
  58.8 20.8 %collective-permute-start.7 = (bf16[4,3,32,2048]{3,2,1,0:T(8,128)(2,1)S(1)}, bf16[4,3,32,2048]{3,2,1,0:T(8,128)(2,1)S(1)}, u32[]{:S(2)}, u32[]{:S(2)}) collective-permute-start(bf16[4,3,32,2048]{3,2,1,0:T(8,128)(2,1)S(1)} %join.2.refs_0_), channel_id=1, source_target_pairs={{0,32},{2,6},{4,36},{6,10},{8,40},{10,14},{12,44},{14,2},{1,33},{3... | collective-permute-start | bytes 4718600 | tf_op jit(solution)/shard_map/ppermute | solution.py:319
  79.6 17.3 %collective-permute-start.22 = (bf16[4,3,32,2048]{3,2,1,0:T(8,128)(2,1)S(1)}, bf16[4,3,32,2048]{3,2,1,0:T(8,128)(2,1)S(1)}, u32[]{:S(2)}, u32[]{:S(2)}) collective-permute-start(bf16[4,3,32,2048]{3,2,1,0:T(8,128)(2,1)S(1)} %collective-permute-done.6.refs_0_), channel_id=1, source_target_pairs={{0,2},{2,0},{4,6},{6,4},{8,10},{10,8},{12,14},{14,12},{1,3},{3,1},... | collective-permute-start | bytes 4718600 | tf_op jit(solution)/shard_map/ppermute | solution.py:319
  82.3 16.8 %collective-permute-start.23 = (bf16[4,3,32,2048]{3,2,1,0:T(8,128)(2,1)S(1)}, bf16[4,3,32,2048]{3,2,1,0:T(8,128)(2,1)S(1)}, u32[]{:S(2)}, u32[]{:S(2)}) collective-permute-start(bf16[4,3,32,2048]{3,2,1,0:T(8,128)(2,1)S(1)} %collective-permute-done.7.refs_1_), channel_id=1, source_target_pairs={{0,2},{2,0},{4,6},{6,4},{8,10},{10,8},{12,14},{14,12},{1,3},{3,1},... | collective-permute-start | bytes 4718600 | tf_op jit(solution)/shard_map/ppermute | solution.py:319
  82.4 12.4 %collective-permute-start.18 = (bf16[2,3,32,2048]{3,2,1,0:T(8,128)(2,1)S(1)}, bf16[2,3,32,2048]{3,2,1,0:T(8,128)(2,1)S(1)}, u32[]{:S(2)}, u32[]{:S(2)}) collective-permute-start(bf16[2,3,32,2048]{3,2,1,0:T(8,128)(2,1)S(1)} %slice.14), channel_id=1, source_target_pairs={{0,32},{2,6},{4,36},{6,10},{8,40},{10,14},{12,44},{14,2},{1,33},{3... | collective-permute-start | bytes 2359304 | tf_op jit(solution)/shard_map/ppermute | solution.py:319
  83.0 11.8 %collective-permute-start.19 = (bf16[2,3,32,2048]{3,2,1,0:T(8,128)(2,1)S(1)}, bf16[2,3,32,2048]{3,2,1,0:T(8,128)(2,1)S(1)}, u32[]{:S(2)}, u32[]{:S(2)}) collective-permute-start(bf16[2,3,32,2048]{3,2,1,0:T(8,128)(2,1)S(1)} %slice.15), channel_id=1, source_target_pairs={{0,96},{2,14},{4,100},{6,2},{8,104},{10,6},{12,108},{14,10},{1,97}... | collective-permute-start | bytes 2359304 | tf_op jit(solution)/shard_map/ppermute | solution.py:319
  94.8 8.6 %collective-permute-start.20 = (bf16[2,3,32,2048]{3,2,1,0:T(8,128)(2,1)S(1)}, bf16[2,3,32,2048]{3,2,1,0:T(8,128)(2,1)S(1)}, u32[]{:S(2)}, u32[]{:S(2)}) collective-permute-start(bf16[2,3,32,2048]{3,2,1,0:T(8,128)(2,1)S(1)} %collective-permute-done.18.refs_0_), channel_id=1, source_target_pairs={{0,2},{2,0},{4,6},{6,4},{8,10},{10,8},{12,14},{14,12},{1,3},{3,1},... | collective-permute-start | bytes 2359304 | tf_op jit(solution)/shard_map/ppermute | solution.py:319
  96.2 7.2 %collective-permute-start.21 = (bf16[2,3,32,2048]{3,2,1,0:T(8,128)(2,1)S(1)}, bf16[2,3,32,2048]{3,2,1,0:T(8,128)(2,1)S(1)}, u32[]{:S(2)}, u32[]{:S(2)}) collective-permute-start(bf16[2,3,32,2048]{3,2,1,0:T(8,128)(2,1)S(1)} %collective-permute-done.19.refs_1_), channel_id=1, source_target_pairs={{0,2},{2,0},{4,6},{6,4},{8,10},{10,8},{12,14},{14,12},{1,3},{3,1},... | collective-permute-start | bytes 2359304 | tf_op jit(solution)/shard_map/ppermute | solution.py:319
  96.3 12.4 %collective-permute-start.16 = (bf16[2,3,32,2048]{3,2,1,0:T(8,128)(2,1)S(1)}, bf16[2,3,32,2048]{3,2,1,0:T(8,128)(2,1)S(1)}, u32[]{:S(2)}, u32[]{:S(2)}) collective-permute-start(bf16[2,3,32,2048]{3,2,1,0:T(8,128)(2,1)S(1)} %slice.12), channel_id=1, source_target_pairs={{0,32},{2,6},{4,36},{6,10},{8,40},{10,14},{12,44},{14,2},{1,33},{3... | collective-permute-start | bytes 2359304 | tf_op jit(solution)/shard_map/ppermute | solution.py:319
  96.9 11.8 %collective-permute-start.17 = (bf16[2,3,32,2048]{3,2,1,0:T(8,128)(2,1)S(1)}, bf16[2,3,32,2048]{3,2,1,0:T(8,128)(2,1)S(1)}, u32[]{:S(2)}, u32[]{:S(2)}) collective-permute-start(bf16[2,3,32,2048]{3,2,1,0:T(8,128)(2,1)S(1)} %slice.13), channel_id=1, source_target_pairs={{0,96},{2,14},{4,100},{6,2},{8,104},{10,6},{12,108},{14,10},{1,97}... | collective-permute-start | bytes 2359304 | tf_op jit(solution)/shard_map/ppermute | solution.py:319
  108.7 3.3 %collective-permute-start.24 = (bf16[2,3,32,2048]{3,2,1,0:T(8,128)(2,1)S(1)}, bf16[2,3,32,2048]{3,2,1,0:T(8,128)(2,1)S(1)}, u32[]{:S(2)}, u32[]{:S(2)}) collective-permute-start(bf16[2,3,32,2048]{3,2,1,0:T(8,128)(2,1)S(1)} %collective-permute-done.16.refs_0_), channel_id=1, source_target_pairs={{0,2},{2,0},{4,6},{6,4},{8,10},{10,8},{12,14},{14,12},{1,3},{3,1},... | collective-permute-start | bytes 2359304 | tf_op jit(solution)/shard_map/ppermute | solution.py:319
  110.1 3.0 %collective-permute-start.25 = (bf16[2,3,32,2048]{3,2,1,0:T(8,128)(2,1)S(1)}, bf16[2,3,32,2048]{3,2,1,0:T(8,128)(2,1)S(1)}, u32[]{:S(2)}, u32[]{:S(2)}) collective-permute-start(bf16[2,3,32,2048]{3,2,1,0:T(8,128)(2,1)S(1)} %collective-permute-done.17.refs_1_), channel_id=1, source_target_pairs={{0,2},{2,0},{4,6},{6,4},{8,10},{10,8},{12,14},{14,12},{1,3},{3,1},... | collective-permute-start | bytes 2359304 | tf_op jit(solution)/shard_map/ppermute | solution.py:319

commit v4 on v2

--- a/solution.py
+++ b/solution.py
@@ -78,7 +78,13 @@
         return carry
 
     lax.fori_loop(0, lines, one, 0)
-    out_ref[...] = edges[...].astype(jnp.bfloat16)
+
+    def rounded(c, carry):
+        at = pl.ds(pl.multiple_of(c * 256, 256), 256)
+        out_ref[:, :, at] = edges[:, :, at].astype(jnp.bfloat16)
+        return carry
+
+    lax.fori_loop(0, coeffs // 256, rounded, 0)
 
 
 def packet_of(cells, signs, where):
@@ -161,26 +167,32 @@
         d0, d1, df = dirs[l, 0], dirs[l, 1], dirs[l, 2]
         p0, p1, pf = d0 > 0, d1 > 0, df > 0
         h0, h1 = jnp.where(p0, 0.5, -0.5), jnp.where(p1, 0.5, -0.5)
-        for c in range(coeffs // 128):
-            at = slice(c * 128, (c + 1) * 128)
-            speed = courant * jnp.broadcast_to(speed_ref[:, at], (8, 128))
-            v0, v1, vf = d0 * speed, d1 * speed, df * speed
-            for s in range(species):
-                f = cells_ref[s, l, :, at].astype(jnp.float32)
-                f0, f1 = f[0:8], f[8:16]
-                left, right, ext, diff = (
-                    sides[k, c, pl.ds(s * lines + l, 8, stride=0), :] for k in range(4)
-                )
-                a0, a1 = up(f0, f1, right)
-                b0, b1 = down(f0, f1, left)
-                n0, n1 = a0 - f0, a1 - f1
-                m0, m1 = up(n0, n1, diff)
-                flux0 = v0 * (jnp.where(p0, f0, a0) + h0 * jnp.where(p0, f0 - b0, m0))
-                flux1 = v1 * (jnp.where(p1, f1, a1) + h1 * jnp.where(p1, f1 - b1, m1))
-                first = vf * jnp.where(pf, ext, f0 - 0.5 * n0)
-                g0, g1 = down(flux0, flux1, first)
-                new = jnp.concatenate([f0 - (flux0 - g0), f1 - (flux1 - g1)], axis=0)
-                out_ref[s, l, :, at] = new.astype(jnp.bfloat16)
+
+        def some(q, carry):
+            for k in range(8):
+                c = q * 8 + k
+                at = pl.ds(pl.multiple_of(c * 128, 128), 128)
+                speed = courant * jnp.broadcast_to(speed_ref[:, at], (8, 128))
+                v0, v1, vf = d0 * speed, d1 * speed, df * speed
+                for s in range(species):
+                    f = cells_ref[s, l, :, at].astype(jnp.float32)
+                    f0, f1 = f[0:8], f[8:16]
+                    left, right, ext, diff = (
+                        sides[k, c, pl.ds(s * lines + l, 8, stride=0), :] for k in range(4)
+                    )
+                    a0, a1 = up(f0, f1, right)
+                    b0, b1 = down(f0, f1, left)
+                    n0, n1 = a0 - f0, a1 - f1
+                    m0, m1 = up(n0, n1, diff)
+                    flux0 = v0 * (jnp.where(p0, f0, a0) + h0 * jnp.where(p0, f0 - b0, m0))
+                    flux1 = v1 * (jnp.where(p1, f1, a1) + h1 * jnp.where(p1, f1 - b1, m1))
+                    first = vf * jnp.where(pf, ext, f0 - 0.5 * n0)
+                    g0, g1 = down(flux0, flux1, first)
+                    new = jnp.concatenate([f0 - (flux0 - g0), f1 - (flux1 - g1)], axis=0)
+                    out_ref[s, l, :, at] = new.astype(jnp.bfloat16)
+            return carry
+
+        lax.fori_loop(0, coeffs // 1024, some, 0)
         return carry
 
     def part(c, carry):
@@ -241,49 +253,61 @@
     groups, refs = refs[:count], refs[count:]
     acc_ref, refs = (None, refs) if first else (refs[0], refs[1:])
     out_ref = refs[0]
-    species, _, coeffs = adv_ref.shape
+    species, rows, coeffs = adv_ref.shape
     pair_count = out_ref.shape[0]
     nt = (((1,), (1,)), ((), ()))
     ends = [sum(units[: k + 1]) for k in range(len(units))]
     held = [groups[end - n : end] for n, end in zip(units, ends)]
 
-    def leaving(p):
+    blocks = 2 if last else 1
+    block = rows // blocks
+
+    def leaving(p, i):
         staged, out_sem = refs[1:]
-        return pltpu.make_async_copy(staged.at[p], out_ref.at[p], out_sem.at[p])
+        at = pl.ds(pl.multiple_of(i * block, block), block)
+        return pltpu.make_async_copy(staged.at[p, at], out_ref.at[p, at], out_sem.at[p, i])
 
     def ranks_of(arrays, which):
         return jnp.concatenate([ref[:, which].reshape(-1, coeffs) for ref in arrays], axis=0)
 
-    left, right = [], []
-    for s in range(species):
-        both = [
-            lax.dot_general(
-                adv_ref[s],
-                jnp.concatenate([ranks_of(h, 0), ranks_of(h, 1)], axis=0),
-                nt,
-                preferred_element_type=jnp.float32,
-            )
-            for h in held
-        ]
-        half = both[0].shape[1] // 2
-        left.append(jnp.concatenate([b[:, :half] for b in both], axis=1))
-        right.append(jnp.concatenate([b[:, half:] for b in both], axis=1))
-    down = jnp.concatenate([ranks_of(h, 2) for h in held], axis=0)
+    def one(i, carry):
+        at = pl.ds(pl.multiple_of(i * block, block), block)
+        left, right = [], []
+        for s in range(species):
+            both = [
+                lax.dot_general(
+                    adv_ref[s, at, :],
+                    jnp.concatenate([ranks_of(h, 0), ranks_of(h, 1)], axis=0),
+                    nt,
+                    preferred_element_type=jnp.float32,
+                )
+                for h in held
+            ]
+            half = both[0].shape[1] // 2
+            left.append(jnp.concatenate([b[:, :half] for b in both], axis=1))
+            right.append(jnp.concatenate([b[:, half:] for b in both], axis=1))
+        down = jnp.concatenate([ranks_of(h, 2) for h in held], axis=0)
+        for p in range(pair_count):
+            lp = jnp.where(pair_ref[0, p] == 1, left[1], left[0])
+            rp = jnp.where(pair_ref[1, p] == 1, right[1], right[0])
+            product = (freq_ref[p] * lp * rp).astype(jnp.bfloat16)
+            term = jnp.dot(product, down, preferred_element_type=jnp.float32)
+            if not first:
+                term = (acc_ref if last else out_ref)[p, at, :] + term
+            if last:
+                refs[1][p, at, :] = term.astype(jnp.bfloat16)
+                leaving(p, i).start()
+            else:
+                out_ref[p, at, :] = term
+        return carry
+
+    if not last:
+        one(0, 0)
+        return
+    lax.fori_loop(0, blocks, one, 0)
     for p in range(pair_count):
-        lp = jnp.where(pair_ref[0, p] == 1, left[1], left[0])
-        rp = jnp.where(pair_ref[1, p] == 1, right[1], right[0])
-        product = (freq_ref[p] * lp * rp).astype(jnp.bfloat16)
-        term = jnp.dot(product, down, preferred_element_type=jnp.float32)
-        if not first:
-            term = (acc_ref if last else out_ref)[p] + term
-        if last:
-            refs[1][p] = term.astype(jnp.bfloat16)
-            leaving(p).start()
-        else:
-            out_ref[p] = term
-    if last:
-        for p in range(pair_count):
-            leaving(p).wait()
+        for i in range(blocks):
+            leaving(p, i).wait()
 
 
 def collide(adv, frequency, pairs, held, acc, last=False):
@@ -298,7 +322,7 @@
         in_specs=[SMEM, SMEM] + [VMEM] * (len(operands) - 2),
         out_specs=HBM if last else VMEM,
         out_shape=jax.ShapeDtypeStruct(shape, jnp.bfloat16) if last else pltpu.VMEM(shape, jnp.float32),
-        scratch_shapes=[pltpu.VMEM(shape, jnp.bfloat16), DMA((pair_count,))] if last else [],
+        scratch_shapes=[pltpu.VMEM(shape, jnp.bfloat16), DMA((pair_count, 2))] if last else [],
         input_output_aliases={} if acc is None or last else {len(operands) - 1: 0},
         cost_estimate=cost(
             2 * ranks * coeffs * rows * (2 * species + pair_count),
@@ -341,10 +365,12 @@
     parts_c = phase(cross) + [send(parts_o[3], CROSS)]
     packet = packet_of(distribution, signs, here)
     got = send(packet, SIDE)
-    parts_o[0] = after(mine, packet)
-    group_o = join(parts_o)
-    up_o, down_o = send(group_o, UP2), send(group_o, DOWN2)
-    swap_o = swap([group_o])
+    up_m, down_m = send(mine, UP2), send(mine, DOWN2)
+    parts_o[1] = after(parts_o[1], packet)
+    rest_o = join(parts_o[1:])
+    up_r, down_r = send(rest_o, UP2), send(rest_o, DOWN2)
+    group_o = [mine, rest_o]
+    swap_o = swap(group_o)
     adv_near, advanced = transport(distribution, got, signs, stream_speed[None], here)
     parts_c[0] = after(parts_c[0], adv_near)
     group_c = join(parts_c)
@@ -356,12 +382,14 @@
     def step(held, acc, last=False):
         return collide(adv, frequency, pairs, held, acc, last)
 
-    acc = step([[after(group_o, group_c)], swap_o], None)
+    rest_o = after(rest_o, group_c)
+    acc = step([[mine, rest_o], swap_o], None)
     acc = step([[group_c], swap_c], acc)
-    up_o, down_o, _ = lax.optimization_barrier((up_o, down_o, acc))
-    far_o = relay(up_o, down_o)
-    swap_uo, swap_do = swap([up_o]), swap([down_o])
-    acc = step([[up_o], [down_o]], acc)
+    up_r, down_r, _ = lax.optimization_barrier((up_r, down_r, acc))
+    far_o = [send(up_r[:2], UP2), send(jnp.concatenate([down_m, down_r[2:]], axis=0), DOWN2)]
+    up_o, down_o = [up_m, up_r], [down_m, down_r]
+    swap_uo, swap_do = swap(up_o), swap(down_o)
+    acc = step([up_o, down_o], acc)
     acc = step([swap_uo, swap_do], acc)
     down_c, up_c, _ = lax.optimization_barrier((down_c, up_c, acc))
     far_c = relay(up_c, down_c)

time: 119 us -> 123 us (1.034)
  starting transfers between devices: 33.4 us -> 41.3 us
  waiting for transfers between devices: 37.7 us -> 32.8 us
    ppermute x26 -> x31, starting transfers between devices: 33.4 us -> 41.3 us  [send(): return lax.ppermute(array, AXES, pairs)]
    ppermute x26 -> x31, waiting for transfers between devices: 37.7 us -> 32.8 us  [send(): return lax.ppermute(array, AXES, pairs)]
  transfers between devices with their start and end apart: 26 -> 31, of which waited for: 8 -> 6; matrix products, arithmetic and copies ran while one was open for 0% -> 0% of each run, Pallas kernels for 34% -> 31%
where the time goes in v4:
time: 123 us
  Pallas kernels  47 us (38%)
  starting transfers between devices  41.3 us (34%)
  waiting for transfers between devices  32.8 us (27%)
    ppermute x31, starting transfers between devices, send(): return lax.ppermute(array, AXES, pairs)  41.3 us
    pallas_call x8, Pallas kernels, collide(): pl.pallas_call(functools.partial(collide_kernel, [len(unit) for unit in h...  36.2 us
    ppermute x31, waiting for transfers between devices, send(): return lax.ppermute(array, AXES, pairs)  32.8 us
    pallas_call x1, Pallas kernels, transport(): pl.pallas_call(transport_kernel, in_specs=[SMEM, VMEM, VMEM, VMEM, HBM],...  8.12 us
  transfers between devices with their start and end apart: 31, of which 6 were waited for; matrix products, arithmetic and copies ran while one was open for 0% of the time, Pallas kernels for 31%

profile of v4, /device:TPU:1, one launch (start us, length us, event | category | flops | bytes accessed | tf_op | source)
XLA Modules:
  0.0 122.6 jit_solution(364115227167809956)
XLA Ops:
  0.7 2.5 %packet.1 = bf16[2,64,2048]{2,1,0:T(8,128)(2,1)S(1)} custom-call(s32[1]{0:T(128)} %bitcast.where_ref, s32[16,28]{1,0:T(8,128)} %bitcast.31, bf16[2,28,16,2048]{3,2,1,0:T(8,128)(2,1)} %cells_hbm.1), custom_call_target="tpu_custom_call" | custom-call | flops 1835008 | bytes 1835008 | tf_op jit(solution)/shard_map/packet/pallas_call | solution.py:93
  3.1 2.2 %collective-permute-start = (bf16[2,64,2048]{2,1,0:T(8,128)(2,1)S(1)}, bf16[2,64,2048]{2,1,0:T(8,128)(2,1)S(1)}, u32[]{:S(2)}, u32[]{:S(2)}) collective-permute-start(bf16[2,64,2048]{2,1,0:T(8,128)(2,1)S(1)} %packet.1), channel_id=1, source_target_pairs={{0,1},{2,3},{4,5},{6,7},{8,9},{10,11},{12,13},{14,15},{1,0},{3,2},... | collective-permute-start | bytes 1572872 | tf_op jit(solution)/shard_map/ppermute | solution.py:337
  5.3 1.9 %collective-permute-start.1 = (bf16[1,3,32,2048]{3,2,1,0:T(8,128)(2,1)S(1)}, bf16[1,3,32,2048]{3,2,1,0:T(8,128)(2,1)S(1)}, u32[]{:S(2)}, u32[]{:S(2)}) collective-permute-start(bf16[1,3,32,2048]{3,2,1,0:T(8,128)(2,1)S(1)} %bitcast.15), channel_id=1, source_target_pairs={{0,17},{2,19},{4,21},{6,23},{8,25},{10,27},{12,29},{14,31},{1,16},... | collective-permute-start | bytes 1179656 | tf_op jit(solution)/shard_map/ppermute | solution.py:337
  7.2 3.6 %collective-permute-start.4 = (bf16[1,3,32,2048]{3,2,1,0:T(8,128)(2,1)S(1)}, bf16[1,3,32,2048]{3,2,1,0:T(8,128)(2,1)S(1)}, u32[]{:S(2)}, u32[]{:S(2)}) collective-permute-start(bf16[1,3,32,2048]{3,2,1,0:T(8,128)(2,1)S(1)} %bitcast.16), channel_id=1, source_target_pairs={{0,8},{2,66},{4,12},{6,70},{8,0},{10,74},{12,4},{14,78},{1,9},{3,6... | collective-permute-start | bytes 1179656 | tf_op jit(solution)/shard_map/ppermute | solution.py:337
  10.8 5.4 %collective-permute-done.1.refs_0_ = bf16[1,3,32,2048]{3,2,1,0:T(8,128)(2,1)S(1)} collective-permute-done((bf16[1,3,32,2048]{3,2,1,0:T(8,128)(2,1)S(1)}, bf16[1,3,32,2048]{3,2,1,0:T(8,128)(2,1)S(1)}, u32[]{:S(2)}, u32[]{:S(2)}) %collective-permute-start.1) | collective-permute-done | bytes 393248 | tf_op jit(solution)/shard_map/ppermute | solution.py:337
  16.3 1.6 %collective-permute-start.2 = (bf16[1,3,32,2048]{3,2,1,0:T(8,128)(2,1)S(1)}, bf16[1,3,32,2048]{3,2,1,0:T(8,128)(2,1)S(1)}, u32[]{:S(2)}, u32[]{:S(2)}) collective-permute-start(bf16[1,3,32,2048]{3,2,1,0:T(8,128)(2,1)S(1)} %collective-permute-done.1.refs_0_), channel_id=1, source_target_pairs={{0,4},{2,34},{4,8},{6,38},{8,12},{10,42},{12,0},{14,46},{1,5},{3,3... | collective-permute-start | bytes 1179656 | tf_op jit(solution)/shard_map/ppermute | solution.py:337
  17.9 2.1 %collective-permute-start.3 = (bf16[1,3,32,2048]{3,2,1,0:T(8,128)(2,1)S(1)}, bf16[1,3,32,2048]{3,2,1,0:T(8,128)(2,1)S(1)}, u32[]{:S(2)}, u32[]{:S(2)}) collective-permute-start(bf16[1,3,32,2048]{3,2,1,0:T(8,128)(2,1)S(1)} %collective-permute-done.1.refs_0_), channel_id=1, source_target_pairs={{0,12},{2,98},{4,0},{6,102},{8,4},{10,106},{12,8},{14,110},{1,13},... | collective-permute-start | bytes 1179656 | tf_op jit(solution)/shard_map/ppermute | solution.py:337
  20.0 1.9 %collective-permute-start.5 = (bf16[1,3,32,2048]{3,2,1,0:T(8,128)(2,1)S(1)}, bf16[1,3,32,2048]{3,2,1,0:T(8,128)(2,1)S(1)}, u32[]{:S(2)}, u32[]{:S(2)}) collective-permute-start(bf16[1,3,32,2048]{3,2,1,0:T(8,128)(2,1)S(1)} %collective-permute-done.4.refs_2_), channel_id=1, source_target_pairs={{0,17},{2,19},{4,21},{6,23},{8,25},{10,27},{12,29},{14,31},{1,16},... | collective-permute-start | bytes 1179656 | tf_op jit(solution)/shard_map/ppermute | solution.py:337
  21.9 2.7 %collective-permute-start.11 = (bf16[1,3,32,2048]{3,2,1,0:T(8,128)(2,1)S(1)}, bf16[1,3,32,2048]{3,2,1,0:T(8,128)(2,1)S(1)}, u32[]{:S(2)}, u32[]{:S(2)}) collective-permute-start(bf16[1,3,32,2048]{3,2,1,0:T(8,128)(2,1)S(1)} %bitcast.18), channel_id=1, source_target_pairs={{0,12},{2,98},{4,0},{6,102},{8,4},{10,106},{12,8},{14,110},{1,13},... | collective-permute-start | bytes 1179656 | tf_op jit(solution)/shard_map/ppermute | solution.py:337
  24.6 8.1 %transport.1 = (bf16[2,28,16,2048]{3,2,1,0:T(8,128)(2,1)S(1)}, bf16[2,28,16,2048]{3,2,1,0:T(8,128)(2,1)}) custom-call(s32[1]{0:T(128)} %bitcast.where_ref, f32[1,2048]{1,0:T(1,128)S(1)} %bitcast.33, s32[16,28]{1,0:T(8,128)S(1)} %bitcast.32, bf16[2,64,2048]{2,1,0:T(8,128)(2,1)S(1)} %collective-permute-done.packet_ref, bf16[2,28,16,2048]{3,2,1,0:T(8,128)(2,1)} %cells_hbm.1), custom_call_target="tpu_custom_call" | custom-call | flops 55050240 | bytes 7340032 | tf_op jit(solution)/shard_map/transport/pallas_call | solution.py:211
  32.8 0.1 join.2.refs_0_
  32.9 2.2 %collective-permute-start.14 = (bf16[4,3,32,2048]{3,2,1,0:T(8,128)(2,1)S(1)}, bf16[4,3,32,2048]{3,2,1,0:T(8,128)(2,1)S(1)}, u32[]{:S(2)}, u32[]{:S(2)}) collective-permute-start(bf16[4,3,32,2048]{3,2,1,0:T(8,128)(2,1)S(1)} %join.2.refs_0_), channel_id=1, source_target_pairs={{0,2},{2,0},{4,6},{6,4},{8,10},{10,8},{12,14},{14,12},{1,3},{3,1},... | collective-permute-start | bytes 4718600 | tf_op jit(solution)/shard_map/ppermute | solution.py:337
  35.1 0.1 join.3.refs_1_
  35.2 0.1 collective-permute-start.16
  35.4 2.7 %collective-permute-start.13 = (bf16[3,3,32,2048]{3,2,1,0:T(8,128)(2,1)S(1)}, bf16[3,3,32,2048]{3,2,1,0:T(8,128)(2,1)S(1)}, u32[]{:S(2)}, u32[]{:S(2)}) collective-permute-start(bf16[3,3,32,2048]{3,2,1,0:T(8,128)(2,1)S(1)} %join.3.refs_1_), channel_id=1, source_target_pairs={{0,96},{2,14},{4,100},{6,2},{8,104},{10,6},{12,108},{14,10},{1,97}... | collective-permute-start | bytes 3538952 | tf_op jit(solution)/shard_map/ppermute | solution.py:337
  38.0 1.8 %collective-permute-start.15 = (bf16[1,3,32,2048]{3,2,1,0:T(8,128)(2,1)S(1)}, bf16[1,3,32,2048]{3,2,1,0:T(8,128)(2,1)S(1)}, u32[]{:S(2)}, u32[]{:S(2)}) collective-permute-start(bf16[1,3,32,2048]{3,2,1,0:T(8,128)(2,1)S(1)} %bitcast.19), channel_id=1, source_target_pairs={{0,2},{2,0},{4,6},{6,4},{8,10},{10,8},{12,14},{14,12},{1,3},{3,1},... | collective-permute-start | bytes 1179656 | tf_op jit(solution)/shard_map/ppermute | solution.py:337
  39.8 1.3 %collective-permute-done.15.refs_2_ = bf16[1,3,32,2048]{3,2,1,0:T(8,128)(2,1)S(1)} collective-permute-done((bf16[1,3,32,2048]{3,2,1,0:T(8,128)(2,1)S(1)}, bf16[1,3,32,2048]{3,2,1,0:T(8,128)(2,1)S(1)}, u32[]{:S(2)}, u32[]{:S(2)}) %collective-permute-start.15) | collective-permute-done | bytes 393248 | tf_op jit(solution)/shard_map/ppermute | solution.py:337
  41.2 0.5 collective-permute-start.6
  41.8 4.2 %collide.8.refs_2_ = f32[3,448,2048]{2,1,0:T(8,128)S(1)} custom-call(f32[3]{0:T(128)S(1)} %copy-done.2, s32[2,3]{1,0:T(2,128)S(1)} %bitcast.23, bf16[2,448,2048]{2,1,0:T(8,128)(2,1)S(1)} %bitcast.7, bf16[1,3,32,2048]{3,2,1,0:T(8,128)(2,1)S(1)} %bitcast.21, bf16[3,3,32,2048]{3,2,1,0:T(8,128)(2,1)S(1)} %join.3.refs_1_, ...), custom_call_target="tpu_custom_call" | custom-call | flops 3288334336 | bytes 6815744 | tf_op jit(solution)/shard_map/collide/pallas_call | solution.py:320
  46.0 1.2 collective-permute-start.7
  47.2 4.3 %collide.9.refs_4_ = f32[3,448,2048]{2,1,0:T(8,128)S(1)} custom-call(f32[3]{0:T(128)S(1)} %copy-done.2, s32[2,3]{1,0:T(2,128)S(1)} %bitcast.24, bf16[2,448,2048]{2,1,0:T(8,128)(2,1)S(1)} %bitcast.8, bf16[4,3,32,2048]{3,2,1,0:T(8,128)(2,1)S(1)} %join.2.refs_0_, ...), custom_call_target="tpu_custom_call", output_to_operand_aliasing={{}: (5, {})} | custom-call | flops 3288334336 | bytes 6815744 | tf_op jit(solution)/shard_map/collide/pallas_call | solution.py:320
  51.5 0.4 collective-permute-done.12.refs_1_
  51.9 1.1 collective-permute-start.8
  53.0 2.8 %collective-permute-start.17 = (bf16[3,3,32,2048]{3,2,1,0:T(8,128)(2,1)S(1)}, bf16[3,3,32,2048]{3,2,1,0:T(8,128)(2,1)S(1)}, u32[]{:S(2)}, u32[]{:S(2)}) collective-permute-start(bf16[3,3,32,2048]{3,2,1,0:T(8,128)(2,1)S(1)} %collective-permute-done.12.refs_1_), channel_id=1, source_target_pairs={{0,2},{2,0},{4,6},{6,4},{8,10},{10,8},{12,14},{14,12},{1,3},{3,1},... | collective-permute-start | bytes 3538952 | tf_op jit(solution)/shard_map/ppermute | solution.py:337
  55.8 2.3 %collective-permute-start.20 = (bf16[3,3,32,2048]{3,2,1,0:T(8,128)(2,1)S(1)}, bf16[3,3,32,2048]{3,2,1,0:T(8,128)(2,1)S(1)}, u32[]{:S(2)}, u32[]{:S(2)}) collective-permute-start(bf16[3,3,32,2048]{3,2,1,0:T(8,128)(2,1)S(1)} %collective-permute-done.13.refs_3_), channel_id=1, source_target_pairs={{0,2},{2,0},{4,6},{6,4},{8,10},{10,8},{12,14},{14,12},{1,3},{3,1},... | collective-permute-start | bytes 3538952 | tf_op jit(solution)/shard_map/ppermute | solution.py:337
  58.1 14.9 %collective-permute-done.8.refs_0_ = bf16[1,3,32,2048]{3,2,1,0:T(8,128)(2,1)S(1)} collective-permute-done((bf16[1,3,32,2048]{3,2,1,0:T(8,128)(2,1)S(1)}, bf16[1,3,32,2048]{3,2,1,0:T(8,128)(2,1)S(1)}, u32[]{:S(2)}, u32[]{:S(2)}) %collective-permute-start.8) | collective-permute-done | bytes 393248 | tf_op jit(solution)/shard_map/ppermute | solution.py:337
  73.0 2.5 %collective-permute-start.19 = (bf16[1,3,32,2048]{3,2,1,0:T(8,128)(2,1)S(1)}, bf16[1,3,32,2048]{3,2,1,0:T(8,128)(2,1)S(1)}, u32[]{:S(2)}, u32[]{:S(2)}) collective-permute-start(bf16[1,3,32,2048]{3,2,1,0:T(8,128)(2,1)S(1)} %collective-permute-done.18.refs_2_), channel_id=1, source_target_pairs={{0,2},{2,0},{4,6},{6,4},{8,10},{10,8},{12,14},{14,12},{1,3},{3,1},... | collective-permute-start | bytes 1179656 | tf_op jit(solution)/shard_map/ppermute | solution.py:337
  75.5 1.3 %collective-permute-done.19.refs_2_ = bf16[1,3,32,2048]{3,2,1,0:T(8,128)(2,1)S(1)} collective-permute-done((bf16[1,3,32,2048]{3,2,1,0:T(8,128)(2,1)S(1)}, bf16[1,3,32,2048]{3,2,1,0:T(8,128)(2,1)S(1)}, u32[]{:S(2)}, u32[]{:S(2)}) %collective-permute-start.19) | collective-permute-done | bytes 393248 | tf_op jit(solution)/shard_map/ppermute | solution.py:337
  76.9 0.4 collective-permute-start.9
  77.2 4.3 %collide.10.refs_4_ = f32[3,448,2048]{2,1,0:T(8,128)S(1)} custom-call(f32[3]{0:T(128)S(1)} %copy-done.2, s32[2,3]{1,0:T(2,128)S(1)} %bitcast.25, bf16[2,448,2048]{2,1,0:T(8,128)(2,1)S(1)} %bitcast.9, bf16[1,3,32,2048]{3,2,1,0:T(8,128)(2,1)S(1)} %collective-permute-done.8.refs_0_, ...), custom_call_target="tpu_custom_call", output_to_operand_aliasing={{}: (7, {})} | custom-call | flops 3288334336 | bytes 6815744 | tf_op jit(solution)/shard_map/collide/pallas_call | solution.py:320
  81.6 4.3 %collide.11.refs_2_ = f32[3,448,2048]{2,1,0:T(8,128)S(1)} custom-call(f32[3]{0:T(128)S(1)} %copy-done.2, s32[2,3]{1,0:T(2,128)S(1)} %bitcast.26, bf16[2,448,2048]{2,1,0:T(8,128)(2,1)S(1)} %bitcast.10, bf16[1,3,32,2048]{3,2,1,0:T(8,128)(2,1)S(1)} %collective-permute-done.9.refs_0_, ...), custom_call_target="tpu_custom_call", output_to_operand_aliasing={{}: (7, {})} | custom-call | flops 3288334336 | bytes 6815744 | tf_op jit(solution)/shard_map/collide/pallas_call | solution.py:320
  85.9 0.2 collective-permute-start.23
  86.2 0.4 collective-permute-start.24
  86.6 0.1 pad_maximum_fusion
  86.6 0.3 collective-permute-start.28
  87.0 1.5 %collective-permute-start.27 = (bf16[2,3,32,2048]{3,2,1,0:T(8,128)(2,1)S(1)}, bf16[2,3,32,2048]{3,2,1,0:T(8,128)(2,1)S(1)}, u32[]{:S(2)}, u32[]{:S(2)}) collective-permute-start(bf16[2,3,32,2048]{3,2,1,0:T(8,128)(2,1)S(1)} %slice.14), channel_id=1, source_target_pairs={{0,32},{2,6},{4,36},{6,10},{8,40},{10,14},{12,44},{14,2},{1,33},{3... | collective-permute-start | bytes 2359304 | tf_op jit(solution)/shard_map/ppermute | solution.py:337
  88.6 0.1 slice.13
  88.7 0.1 collective-permute-start.21
  88.8 9.3 %collective-permute-done.28.refs_1_ = bf16[2,3,32,2048]{3,2,1,0:T(8,128)(2,1)S(1)} collective-permute-done((bf16[2,3,32,2048]{3,2,1,0:T(8,128)(2,1)S(1)}, bf16[2,3,32,2048]{3,2,1,0:T(8,128)(2,1)S(1)}, u32[]{:S(2)}, u32[]{:S(2)}) %collective-permute-start.28) | collective-permute-done | bytes 786464 | tf_op jit(solution)/shard_map/ppermute | solution.py:337
  98.1 1.3 %collective-permute-start.22 = (bf16[2,3,32,2048]{3,2,1,0:T(8,128)(2,1)S(1)}, bf16[2,3,32,2048]{3,2,1,0:T(8,128)(2,1)S(1)}, u32[]{:S(2)}, u32[]{:S(2)}) collective-permute-start(bf16[2,3,32,2048]{3,2,1,0:T(8,128)(2,1)S(1)} %slice.13), channel_id=1, source_target_pairs={{0,96},{2,14},{4,100},{6,2},{8,104},{10,6},{12,108},{14,10},{1,97}... | collective-permute-start | bytes 2359304 | tf_op jit(solution)/shard_map/ppermute | solution.py:337
  99.3 4.3 %collide.12.refs_2_ = f32[3,448,2048]{2,1,0:T(8,128)S(1)} custom-call(f32[3]{0:T(128)S(1)} %copy-done.2, s32[2,3]{1,0:T(2,128)S(1)} %bitcast.27, bf16[2,448,2048]{2,1,0:T(8,128)(2,1)S(1)} %bitcast.11, bf16[4,3,32,2048]{3,2,1,0:T(8,128)(2,1)S(1)} %collective-permute-done.6.refs_0_, ...), custom_call_target="tpu_custom_call", output_to_operand_aliasing={{}: (5, {})} | custom-call | flops 3288334336 | bytes 6815744 | tf_op jit(solution)/shard_map/collide/pallas_call | solution.py:320
  103.7 2.9 %collective-permute-start.29 = (bf16[2,3,32,2048]{3,2,1,0:T(8,128)(2,1)S(1)}, bf16[2,3,32,2048]{3,2,1,0:T(8,128)(2,1)S(1)}, u32[]{:S(2)}, u32[]{:S(2)}) collective-permute-start(bf16[2,3,32,2048]{3,2,1,0:T(8,128)(2,1)S(1)} %collective-permute-done.27.refs_0_), channel_id=1, source_target_pairs={{0,2},{2,0},{4,6},{6,4},{8,10},{10,8},{12,14},{14,12},{1,3},{3,1},... | collective-permute-start | bytes 2359304 | tf_op jit(solution)/shard_map/ppermute | solution.py:337
  106.5 0.1 collective-permute-start.30
  106.6 4.3 %collide.13.refs_4_ = f32[3,448,2048]{2,1,0:T(8,128)S(1)} custom-call(f32[3]{0:T(128)S(1)} %copy-done.2, s32[2,3]{1,0:T(2,128)S(1)} %bitcast.28, bf16[2,448,2048]{2,1,0:T(8,128)(2,1)S(1)} %bitcast.12, bf16[4,3,32,2048]{3,2,1,0:T(8,128)(2,1)S(1)} %collective-permute-done.23.refs_0_, ...), custom_call_target="tpu_custom_call", output_to_operand_aliasing={{}: (5, {})} | custom-call | flops 3288334336 | bytes 6815744 | tf_op jit(solution)/shard_map/collide/pallas_call | solution.py:320
  111.0 0.7 collective-permute-start.25
  111.6 0.2 collective-permute-start.26
  111.8 4.3 %collide.14.refs_4_ = f32[3,448,2048]{2,1,0:T(8,128)S(1)} custom-call(f32[3]{0:T(128)S(1)} %copy-done.2, s32[2,3]{1,0:T(2,128)S(1)} %bitcast.29, bf16[2,448,2048]{2,1,0:T(8,128)(2,1)S(1)} %bitcast.13, bf16[2,3,32,2048]{3,2,1,0:T(8,128)(2,1)S(1)} %collective-permute-done.27.refs_0_, ...), custom_call_target="tpu_custom_call", output_to_operand_aliasing={{}: (7, {})} | custom-call | flops 3288334336 | bytes 6815744 | tf_op jit(solution)/shard_map/collide/pallas_call | solution.py:320
  116.2 6.2 %collide.15 = bf16[3,448,2048]{2,1,0:T(8,128)(2,1)} custom-call(f32[3]{0:T(128)S(1)} %copy-done.2, s32[2,3]{1,0:T(2,128)S(1)} %bitcast.30, bf16[2,448,2048]{2,1,0:T(8,128)(2,1)S(1)} %bitcast.14, bf16[2,3,32,2048]{3,2,1,0:T(8,128)(2,1)S(1)} %collective-permute-done.21.refs_0_, bf16[2,3,32,2048]{3,2,1,0:T(8,128)(2,1)S(1)} %collective-permute-done.22.refs_1_, ...), custom_call_target="tpu_custom_call" | custom-call | flops 3288334336 | bytes 6815744 | tf_op jit(solution)/shard_map/collide/pallas_call | solution.py:320
  (41 shorter events, 0.4 us)
Async XLA Ops:
  0.6 4.7 %copy-start = (bf16[3,32,2048]{2,1,0:T(8,128)(2,1)S(1)}, bf16[3,32,2048]{2,1,0:T(8,128)(2,1)}, u32[]{:S(2)}) copy-start(bf16[3,32,2048]{2,1,0:T(8,128)(2,1)} %param.9) | copy-start | bytes 1179652
  0.6 24.0 %copy-start.3 = (s32[28,16]{0,1:T(8,128)S(1)}, s32[28,16]{0,1:T(8,128)}, u32[]{:S(2)}) copy-start(s32[28,16]{0,1:T(8,128)} %param.7) | copy-start | bytes 5380
  0.7 24.0 %copy-start.4 = (f32[2048]{0:T(1024)S(1)}, f32[2048]{0:T(1024)}, u32[]{:S(2)}) copy-start(f32[2048]{0:T(1024)} %param.8) | copy-start | bytes 24580
  3.1 18.8 %collective-permute-start = (bf16[2,64,2048]{2,1,0:T(8,128)(2,1)S(1)}, bf16[2,64,2048]{2,1,0:T(8,128)(2,1)S(1)}, u32[]{:S(2)}, u32[]{:S(2)}) collective-permute-start(bf16[2,64,2048]{2,1,0:T(8,128)(2,1)S(1)} %packet.1), channel_id=1, source_target_pairs={{0,1},{2,3},{4,5},{6,7},{8,9},{10,11},{12,13},{14,15},{1,0},{3,2},... | collective-permute-start | bytes 1572872 | tf_op jit(solution)/shard_map/ppermute | solution.py:337
  5.3 10.9 %collective-permute-start.1 = (bf16[1,3,32,2048]{3,2,1,0:T(8,128)(2,1)S(1)}, bf16[1,3,32,2048]{3,2,1,0:T(8,128)(2,1)S(1)}, u32[]{:S(2)}, u32[]{:S(2)}) collective-permute-start(bf16[1,3,32,2048]{3,2,1,0:T(8,128)(2,1)S(1)} %bitcast.15), channel_id=1, source_target_pairs={{0,17},{2,19},{4,21},{6,23},{8,25},{10,27},{12,29},{14,31},{1,16},... | collective-permute-start | bytes 1179656 | tf_op jit(solution)/shard_map/ppermute | solution.py:337
  7.2 12.8 %collective-permute-start.4 = (bf16[1,3,32,2048]{3,2,1,0:T(8,128)(2,1)S(1)}, bf16[1,3,32,2048]{3,2,1,0:T(8,128)(2,1)S(1)}, u32[]{:S(2)}, u32[]{:S(2)}) collective-permute-start(bf16[1,3,32,2048]{3,2,1,0:T(8,128)(2,1)S(1)} %bitcast.16), channel_id=1, source_target_pairs={{0,8},{2,66},{4,12},{6,70},{8,0},{10,74},{12,4},{14,78},{1,9},{3,6... | collective-permute-start | bytes 1179656 | tf_op jit(solution)/shard_map/ppermute | solution.py:337
  16.3 16.5 %collective-permute-start.2 = (bf16[1,3,32,2048]{3,2,1,0:T(8,128)(2,1)S(1)}, bf16[1,3,32,2048]{3,2,1,0:T(8,128)(2,1)S(1)}, u32[]{:S(2)}, u32[]{:S(2)}) collective-permute-start(bf16[1,3,32,2048]{3,2,1,0:T(8,128)(2,1)S(1)} %collective-permute-done.1.refs_0_), channel_id=1, source_target_pairs={{0,4},{2,34},{4,8},{6,38},{8,12},{10,42},{12,0},{14,46},{1,5},{3,3... | collective-permute-start | bytes 1179656 | tf_op jit(solution)/shard_map/ppermute | solution.py:337
  17.9 14.9 %collective-permute-start.3 = (bf16[1,3,32,2048]{3,2,1,0:T(8,128)(2,1)S(1)}, bf16[1,3,32,2048]{3,2,1,0:T(8,128)(2,1)S(1)}, u32[]{:S(2)}, u32[]{:S(2)}) collective-permute-start(bf16[1,3,32,2048]{3,2,1,0:T(8,128)(2,1)S(1)} %collective-permute-done.1.refs_0_), channel_id=1, source_target_pairs={{0,12},{2,98},{4,0},{6,102},{8,4},{10,106},{12,8},{14,110},{1,13},... | collective-permute-start | bytes 1179656 | tf_op jit(solution)/shard_map/ppermute | solution.py:337
  20.0 12.7 %collective-permute-start.5 = (bf16[1,3,32,2048]{3,2,1,0:T(8,128)(2,1)S(1)}, bf16[1,3,32,2048]{3,2,1,0:T(8,128)(2,1)S(1)}, u32[]{:S(2)}, u32[]{:S(2)}) collective-permute-start(bf16[1,3,32,2048]{3,2,1,0:T(8,128)(2,1)S(1)} %collective-permute-done.4.refs_2_), channel_id=1, source_target_pairs={{0,17},{2,19},{4,21},{6,23},{8,25},{10,27},{12,29},{14,31},{1,16},... | collective-permute-start | bytes 1179656 | tf_op jit(solution)/shard_map/ppermute | solution.py:337
  21.9 13.2 %collective-permute-start.10 = (bf16[1,3,32,2048]{3,2,1,0:T(8,128)(2,1)S(1)}, bf16[1,3,32,2048]{3,2,1,0:T(8,128)(2,1)S(1)}, u32[]{:S(2)}, u32[]{:S(2)}) collective-permute-start(bf16[1,3,32,2048]{3,2,1,0:T(8,128)(2,1)S(1)} %bitcast.17), channel_id=1, source_target_pairs={{0,4},{2,34},{4,8},{6,38},{8,12},{10,42},{12,0},{14,46},{1,5},{3,3... | collective-permute-start | bytes 1179656 | tf_op jit(solution)/shard_map/ppermute | solution.py:337
  21.9 13.2 %collective-permute-start.11 = (bf16[1,3,32,2048]{3,2,1,0:T(8,128)(2,1)S(1)}, bf16[1,3,32,2048]{3,2,1,0:T(8,128)(2,1)S(1)}, u32[]{:S(2)}, u32[]{:S(2)}) collective-permute-start(bf16[1,3,32,2048]{3,2,1,0:T(8,128)(2,1)S(1)} %bitcast.18), channel_id=1, source_target_pairs={{0,12},{2,98},{4,0},{6,102},{8,4},{10,106},{12,8},{14,110},{1,13},... | collective-permute-start | bytes 1179656 | tf_op jit(solution)/shard_map/ppermute | solution.py:337
  32.9 8.9 %copy-start.1 = (s32[3,2]{0,1:T(2,128)S(1)}, s32[3,2]{0,1:T(2,128)}, u32[]{:S(2)}) copy-start(s32[3,2]{0,1:T(2,128)} %param.10) | copy-start | bytes 76
  32.9 8.9 %copy-start.2 = (f32[3]{0:T(128)S(1)}, f32[3]{0:T(128)}, u32[]{:S(2)}) copy-start(f32[3]{0:T(128)} %freq_ref.15) | copy-start | bytes 40
  32.9 13.1 %collective-permute-start.14 = (bf16[4,3,32,2048]{3,2,1,0:T(8,128)(2,1)S(1)}, bf16[4,3,32,2048]{3,2,1,0:T(8,128)(2,1)S(1)}, u32[]{:S(2)}, u32[]{:S(2)}) collective-permute-start(bf16[4,3,32,2048]{3,2,1,0:T(8,128)(2,1)S(1)} %join.2.refs_0_), channel_id=1, source_target_pairs={{0,2},{2,0},{4,6},{6,4},{8,10},{10,8},{12,14},{14,12},{1,3},{3,1},... | collective-permute-start | bytes 4718600 | tf_op jit(solution)/shard_map/ppermute | solution.py:337
  35.2 6.0 %collective-permute-start.16 = (bf16[3,3,32,2048]{3,2,1,0:T(8,128)(2,1)S(1)}, bf16[3,3,32,2048]{3,2,1,0:T(8,128)(2,1)S(1)}, u32[]{:S(2)}, u32[]{:S(2)}) collective-permute-start(bf16[3,3,32,2048]{3,2,1,0:T(8,128)(2,1)S(1)} %join.3.refs_1_), channel_id=1, source_target_pairs={{0,2},{2,0},{4,6},{6,4},{8,10},{10,8},{12,14},{14,12},{1,3},{3,1},... | collective-permute-start | bytes 3538952 | tf_op jit(solution)/shard_map/ppermute | solution.py:337
  35.3 16.6 %collective-permute-start.12 = (bf16[3,3,32,2048]{3,2,1,0:T(8,128)(2,1)S(1)}, bf16[3,3,32,2048]{3,2,1,0:T(8,128)(2,1)S(1)}, u32[]{:S(2)}, u32[]{:S(2)}) collective-permute-start(bf16[3,3,32,2048]{3,2,1,0:T(8,128)(2,1)S(1)} %join.3.refs_1_), channel_id=1, source_target_pairs={{0,32},{2,6},{4,36},{6,10},{8,40},{10,14},{12,44},{14,2},{1,33},{3... | collective-permute-start | bytes 3538952 | tf_op jit(solution)/shard_map/ppermute | solution.py:337
  35.4 17.6 %collective-permute-start.13 = (bf16[3,3,32,2048]{3,2,1,0:T(8,128)(2,1)S(1)}, bf16[3,3,32,2048]{3,2,1,0:T(8,128)(2,1)S(1)}, u32[]{:S(2)}, u32[]{:S(2)}) collective-permute-start(bf16[3,3,32,2048]{3,2,1,0:T(8,128)(2,1)S(1)} %join.3.refs_1_), channel_id=1, source_target_pairs={{0,96},{2,14},{4,100},{6,2},{8,104},{10,6},{12,108},{14,10},{1,97}... | collective-permute-start | bytes 3538952 | tf_op jit(solution)/shard_map/ppermute | solution.py:337
  38.0 3.1 %collective-permute-start.15 = (bf16[1,3,32,2048]{3,2,1,0:T(8,128)(2,1)S(1)}, bf16[1,3,32,2048]{3,2,1,0:T(8,128)(2,1)S(1)}, u32[]{:S(2)}, u32[]{:S(2)}) collective-permute-start(bf16[1,3,32,2048]{3,2,1,0:T(8,128)(2,1)S(1)} %bitcast.19), channel_id=1, source_target_pairs={{0,2},{2,0},{4,6},{6,4},{8,10},{10,8},{12,14},{14,12},{1,3},{3,1},... | collective-permute-start | bytes 1179656 | tf_op jit(solution)/shard_map/ppermute | solution.py:337
  41.2 14.6 %collective-permute-start.18 = (bf16[1,3,32,2048]{3,2,1,0:T(8,128)(2,1)S(1)}, bf16[1,3,32,2048]{3,2,1,0:T(8,128)(2,1)S(1)}, u32[]{:S(2)}, u32[]{:S(2)}) collective-permute-start(bf16[1,3,32,2048]{3,2,1,0:T(8,128)(2,1)S(1)} %bitcast.20), channel_id=1, source_target_pairs={{0,96},{2,14},{4,100},{6,2},{8,104},{10,6},{12,108},{14,10},{1,97}... | collective-permute-start | bytes 1179656 | tf_op jit(solution)/shard_map/ppermute | solution.py:337
  41.2 44.7 %collective-permute-start.6 = (bf16[4,3,32,2048]{3,2,1,0:T(8,128)(2,1)S(1)}, bf16[4,3,32,2048]{3,2,1,0:T(8,128)(2,1)S(1)}, u32[]{:S(2)}, u32[]{:S(2)}) collective-permute-start(bf16[4,3,32,2048]{3,2,1,0:T(8,128)(2,1)S(1)} %join.2.refs_0_), channel_id=1, source_target_pairs={{0,96},{2,14},{4,100},{6,2},{8,104},{10,6},{12,108},{14,10},{1,97}... | collective-permute-start | bytes 4718600 | tf_op jit(solution)/shard_map/ppermute | solution.py:337
  46.0 39.9 %collective-permute-start.7 = (bf16[4,3,32,2048]{3,2,1,0:T(8,128)(2,1)S(1)}, bf16[4,3,32,2048]{3,2,1,0:T(8,128)(2,1)S(1)}, u32[]{:S(2)}, u32[]{:S(2)}) collective-permute-start(bf16[4,3,32,2048]{3,2,1,0:T(8,128)(2,1)S(1)} %join.2.refs_0_), channel_id=1, source_target_pairs={{0,32},{2,6},{4,36},{6,10},{8,40},{10,14},{12,44},{14,2},{1,33},{3... | collective-permute-start | bytes 4718600 | tf_op jit(solution)/shard_map/ppermute | solution.py:337
  51.9 21.1 %collective-permute-start.8 = (bf16[1,3,32,2048]{3,2,1,0:T(8,128)(2,1)S(1)}, bf16[1,3,32,2048]{3,2,1,0:T(8,128)(2,1)S(1)}, u32[]{:S(2)}, u32[]{:S(2)}) collective-permute-start(bf16[1,3,32,2048]{3,2,1,0:T(8,128)(2,1)S(1)} %bitcast.22), channel_id=1, source_target_pairs={{0,32},{2,6},{4,36},{6,10},{8,40},{10,14},{12,44},{14,2},{1,33},{3... | collective-permute-start | bytes 1179656 | tf_op jit(solution)/shard_map/ppermute | solution.py:337
  53.0 28.6 %collective-permute-start.17 = (bf16[3,3,32,2048]{3,2,1,0:T(8,128)(2,1)S(1)}, bf16[3,3,32,2048]{3,2,1,0:T(8,128)(2,1)S(1)}, u32[]{:S(2)}, u32[]{:S(2)}) collective-permute-start(bf16[3,3,32,2048]{3,2,1,0:T(8,128)(2,1)S(1)} %collective-permute-done.12.refs_1_), channel_id=1, source_target_pairs={{0,2},{2,0},{4,6},{6,4},{8,10},{10,8},{12,14},{14,12},{1,3},{3,1},... | collective-permute-start | bytes 3538952 | tf_op jit(solution)/shard_map/ppermute | solution.py:337
  55.8 25.8 %collective-permute-start.20 = (bf16[3,3,32,2048]{3,2,1,0:T(8,128)(2,1)S(1)}, bf16[3,3,32,2048]{3,2,1,0:T(8,128)(2,1)S(1)}, u32[]{:S(2)}, u32[]{:S(2)}) collective-permute-start(bf16[3,3,32,2048]{3,2,1,0:T(8,128)(2,1)S(1)} %collective-permute-done.13.refs_3_), channel_id=1, source_target_pairs={{0,2},{2,0},{4,6},{6,4},{8,10},{10,8},{12,14},{14,12},{1,3},{3,1},... | collective-permute-start | bytes 3538952 | tf_op jit(solution)/shard_map/ppermute | solution.py:337
  73.0 3.9 %collective-permute-start.19 = (bf16[1,3,32,2048]{3,2,1,0:T(8,128)(2,1)S(1)}, bf16[1,3,32,2048]{3,2,1,0:T(8,128)(2,1)S(1)}, u32[]{:S(2)}, u32[]{:S(2)}) collective-permute-start(bf16[1,3,32,2048]{3,2,1,0:T(8,128)(2,1)S(1)} %collective-permute-done.18.refs_2_), channel_id=1, source_target_pairs={{0,2},{2,0},{4,6},{6,4},{8,10},{10,8},{12,14},{14,12},{1,3},{3,1},... | collective-permute-start | bytes 1179656 | tf_op jit(solution)/shard_map/ppermute | solution.py:337
  76.9 4.7 %collective-permute-start.9 = (bf16[1,3,32,2048]{3,2,1,0:T(8,128)(2,1)S(1)}, bf16[1,3,32,2048]{3,2,1,0:T(8,128)(2,1)S(1)}, u32[]{:S(2)}, u32[]{:S(2)}) collective-permute-start(bf16[1,3,32,2048]{3,2,1,0:T(8,128)(2,1)S(1)} %collective-permute-done.8.refs_0_), channel_id=1, source_target_pairs={{0,2},{2,0},{4,6},{6,4},{8,10},{10,8},{12,14},{14,12},{1,3},{3,1},... | collective-permute-start | bytes 1179656 | tf_op jit(solution)/shard_map/ppermute | solution.py:337
  85.9 20.6 %collective-permute-start.23 = (bf16[4,3,32,2048]{3,2,1,0:T(8,128)(2,1)S(1)}, bf16[4,3,32,2048]{3,2,1,0:T(8,128)(2,1)S(1)}, u32[]{:S(2)}, u32[]{:S(2)}) collective-permute-start(bf16[4,3,32,2048]{3,2,1,0:T(8,128)(2,1)S(1)} %collective-permute-done.6.refs_0_), channel_id=1, source_target_pairs={{0,2},{2,0},{4,6},{6,4},{8,10},{10,8},{12,14},{14,12},{1,3},{3,1},... | collective-permute-start | bytes 4718600 | tf_op jit(solution)/shard_map/ppermute | solution.py:337
  86.2 20.5 %collective-permute-start.24 = (bf16[4,3,32,2048]{3,2,1,0:T(8,128)(2,1)S(1)}, bf16[4,3,32,2048]{3,2,1,0:T(8,128)(2,1)S(1)}, u32[]{:S(2)}, u32[]{:S(2)}) collective-permute-start(bf16[4,3,32,2048]{3,2,1,0:T(8,128)(2,1)S(1)} %collective-permute-done.7.refs_1_), channel_id=1, source_target_pairs={{0,2},{2,0},{4,6},{6,4},{8,10},{10,8},{12,14},{14,12},{1,3},{3,1},... | collective-permute-start | bytes 4718600 | tf_op jit(solution)/shard_map/ppermute | solution.py:337
  86.6 11.4 %collective-permute-start.28 = (bf16[2,3,32,2048]{3,2,1,0:T(8,128)(2,1)S(1)}, bf16[2,3,32,2048]{3,2,1,0:T(8,128)(2,1)S(1)}, u32[]{:S(2)}, u32[]{:S(2)}) collective-permute-start(bf16[2,3,32,2048]{3,2,1,0:T(8,128)(2,1)S(1)} %pad_maximum_fusion), channel_id=1, source_target_pairs={{0,96},{2,14},{4,100},{6,2},{8,104},{10,6},{12,108},{14,10},{1,97}... | collective-permute-start | bytes 2359304 | tf_op jit(solution)/shard_map/ppermute | solution.py:337
  87.0 16.6 %collective-permute-start.27 = (bf16[2,3,32,2048]{3,2,1,0:T(8,128)(2,1)S(1)}, bf16[2,3,32,2048]{3,2,1,0:T(8,128)(2,1)S(1)}, u32[]{:S(2)}, u32[]{:S(2)}) collective-permute-start(bf16[2,3,32,2048]{3,2,1,0:T(8,128)(2,1)S(1)} %slice.14), channel_id=1, source_target_pairs={{0,32},{2,6},{4,36},{6,10},{8,40},{10,14},{12,44},{14,2},{1,33},{3... | collective-permute-start | bytes 2359304 | tf_op jit(solution)/shard_map/ppermute | solution.py:337
  88.7 22.3 %collective-permute-start.21 = (bf16[2,3,32,2048]{3,2,1,0:T(8,128)(2,1)S(1)}, bf16[2,3,32,2048]{3,2,1,0:T(8,128)(2,1)S(1)}, u32[]{:S(2)}, u32[]{:S(2)}) collective-permute-start(bf16[2,3,32,2048]{3,2,1,0:T(8,128)(2,1)S(1)} %slice.12), channel_id=1, source_target_pairs={{0,32},{2,6},{4,36},{6,10},{8,40},{10,14},{12,44},{14,2},{1,33},{3... | collective-permute-start | bytes 2359304 | tf_op jit(solution)/shard_map/ppermute | solution.py:337
  98.1 12.9 %collective-permute-start.22 = (bf16[2,3,32,2048]{3,2,1,0:T(8,128)(2,1)S(1)}, bf16[2,3,32,2048]{3,2,1,0:T(8,128)(2,1)S(1)}, u32[]{:S(2)}, u32[]{:S(2)}) collective-permute-start(bf16[2,3,32,2048]{3,2,1,0:T(8,128)(2,1)S(1)} %slice.13), channel_id=1, source_target_pairs={{0,96},{2,14},{4,100},{6,2},{8,104},{10,6},{12,108},{14,10},{1,97}... | collective-permute-start | bytes 2359304 | tf_op jit(solution)/shard_map/ppermute | solution.py:337
  103.7 8.2 %collective-permute-start.29 = (bf16[2,3,32,2048]{3,2,1,0:T(8,128)(2,1)S(1)}, bf16[2,3,32,2048]{3,2,1,0:T(8,128)(2,1)S(1)}, u32[]{:S(2)}, u32[]{:S(2)}) collective-permute-start(bf16[2,3,32,2048]{3,2,1,0:T(8,128)(2,1)S(1)} %collective-permute-done.27.refs_0_), channel_id=1, source_target_pairs={{0,2},{2,0},{4,6},{6,4},{8,10},{10,8},{12,14},{14,12},{1,3},{3,1},... | collective-permute-start | bytes 2359304 | tf_op jit(solution)/shard_map/ppermute | solution.py:337
  106.5 5.3 %collective-permute-start.30 = (bf16[2,3,32,2048]{3,2,1,0:T(8,128)(2,1)S(1)}, bf16[2,3,32,2048]{3,2,1,0:T(8,128)(2,1)S(1)}, u32[]{:S(2)}, u32[]{:S(2)}) collective-permute-start(bf16[2,3,32,2048]{3,2,1,0:T(8,128)(2,1)S(1)} %collective-permute-done.28.refs_1_), channel_id=1, source_target_pairs={{0,2},{2,0},{4,6},{6,4},{8,10},{10,8},{12,14},{14,12},{1,3},{3,1},... | collective-permute-start | bytes 2359304 | tf_op jit(solution)/shard_map/ppermute | solution.py:337
  111.0 5.2 %collective-permute-start.25 = (bf16[2,3,32,2048]{3,2,1,0:T(8,128)(2,1)S(1)}, bf16[2,3,32,2048]{3,2,1,0:T(8,128)(2,1)S(1)}, u32[]{:S(2)}, u32[]{:S(2)}) collective-permute-start(bf16[2,3,32,2048]{3,2,1,0:T(8,128)(2,1)S(1)} %collective-permute-done.21.refs_0_), channel_id=1, source_target_pairs={{0,2},{2,0},{4,6},{6,4},{8,10},{10,8},{12,14},{14,12},{1,3},{3,1},... | collective-permute-start | bytes 2359304 | tf_op jit(solution)/shard_map/ppermute | solution.py:337
  111.6 4.5 %collective-permute-start.26 = (bf16[2,3,32,2048]{3,2,1,0:T(8,128)(2,1)S(1)}, bf16[2,3,32,2048]{3,2,1,0:T(8,128)(2,1)S(1)}, u32[]{:S(2)}, u32[]{:S(2)}) collective-permute-start(bf16[2,3,32,2048]{3,2,1,0:T(8,128)(2,1)S(1)} %collective-permute-done.22.refs_1_), channel_id=1, source_target_pairs={{0,2},{2,0},{4,6},{6,4},{8,10},{10,8},{12,14},{14,12},{1,3},{3,1},... | collective-permute-start | bytes 2359304 | tf_op jit(solution)/shard_map/ppermute | solution.py:337
